TPU v7x, 512 devices: a whole 4x8x8 slice. The times are simulated.
512 devices in a mesh: rows: 64 (over z, y), cols: 8 (over x, core).
Axes of the slice: x: 4, y: 8, z: 8, core: 2. Of those that a mesh axis runs over, the one named last changes fastest.
Arguments:
- basis_values: bfloat16 [8192, 512, 128], P(('rows', 'cols')), may hold values from -0.125 to 0.125
- potential: float32 [262144], P(('rows', 'cols')), may hold values from -6 to 6
- contrib_index: int32 [65536, 4], P(('rows', 'cols')), may hold values from 0 to 63, as said below
- pattern: int32 [64, 128, 2], P('rows'), may hold values from 0 to 135, as said below
- ghost_list: int32 [64, 64, 2], P('rows'), may hold values from -1 to 511, as said below
- state: float32 [512, 65536], P('cols', 'rows'), may hold values from -6 to 6
- damp_lower: float32 [1], replicated, may hold values from -2.5 to -1
- damp_upper: float32 [1], replicated, may hold values from 1 to 2.5
Outputs:
- first_term: float32 [512, 65536], P('cols', 'rows')
- second_term: float32 [512, 65536], P('cols', 'rows')
Inputs may be any that keep to these rules, and one draw needn't show every extreme that they name: `contrib_index`: column 0 is the rows index that receives the contribution, column 1 its slot among the 16 slots held by the device of that rows index with the sender's cols index, columns 2 and 3 blocks of the sender's batch (below 16). Among the 128 rows of one device at most 4 name the same rows index, and those that do all name the same slot; one rows index receives 4 from every device. pattern[q, g, 0] is below 8. pattern[q, g, 1] is below 8 exactly for the first 4 of each 16 slots; above that it points at an entry of ghost_list[q] that is not -1, and every such entry is pointed at by some slot. ghost_list[q, p, :] holds distinct row blocks owned by rows index p (from p * 8 to p * 8 + 7) or -1; always -1 where p equals q; exactly 48 entries of ghost_list[q] are not -1, and for each q some p has 2 of them.
All inputs are finite; a program needn't handle non-finite values.
Results may differ from a plain program's by a relative error of at most 0.0079.
Values may be sent and summed in bfloat16 or wider, within the bound.
No kernel may reach another device: no remote copies, remote signals or barrier semaphores. Data moves between devices by JAX's collectives and lax.ppermute only.
A program may use at most 64 MiB of HBM per device.

v0:
```python
import jax
import jax.numpy as jnp
from jax import lax
from jax.sharding import PartitionSpec as P

CAP = 4


def on_device(
    basis_values, potential, contrib_index, pattern, ghost_list, state, damp_lower, damp_upper
):
    n_rows = lax.axis_size("rows")
    n_cols = lax.axis_size("cols")
    basis_blocks, points, block_size = basis_values.shape
    contrib_count = contrib_index.shape[0]
    vec_count = state.shape[0]
    row_blocks = state.shape[1] // block_size
    group_slots = pattern.shape[1]
    slot_count = group_slots // n_cols
    ghost_width = ghost_list.shape[2]
    weighted = (basis_values.astype(jnp.float32) * potential[None, :, None]).astype(jnp.bfloat16)

    def pair_block(index_pair):
        left_vals = basis_values[index_pair[:, 0]]
        right_vals = weighted[index_pair[:, 1]]
        return jnp.einsum(
            "snx,sny->sxy", left_vals, right_vals, preferred_element_type=jnp.float32
        ).astype(jnp.bfloat16)

    tile_set = lax.map(pair_block, contrib_index[:, 2:4].reshape(contrib_count // 4, 4, 2)).reshape(
        contrib_count, block_size, block_size
    )
    target_row = contrib_index[:, 0]
    slot_wanted = jnp.arange(slot_count, dtype=jnp.int32)
    matches = (target_row[:, None] == jnp.arange(n_rows, dtype=jnp.int32)[None, :]).astype(
        jnp.int32
    )
    before = jnp.cumsum(matches, axis=0) - matches
    arrival = jnp.sum(before * matches, axis=1)
    position = target_row * CAP + arrival
    wanted = jnp.arange(n_rows * CAP, dtype=jnp.int32)
    matched = position[None, :] == wanted[:, None]
    source = jnp.sum(
        jnp.where(matched, jnp.arange(contrib_count, dtype=jnp.int32)[None, :], 0), axis=1
    )
    filled = jnp.any(matched, axis=1)
    send_tiles = jnp.where(
        filled[:, None, None], tile_set[source], jnp.zeros((), jnp.bfloat16)
    ).reshape(n_rows, CAP, block_size, block_size)
    send_slots = jnp.where(filled, contrib_index[source, 1], -1).reshape(n_rows, CAP)
    arrived_tiles, arrived_slots = (
        lax.all_to_all(send_tiles, "rows", split_axis=0, concat_axis=0, tiled=True),
        lax.all_to_all(send_slots, "rows", split_axis=0, concat_axis=0, tiled=True),
    )
    selector = (arrived_slots.reshape(-1)[None, :] == slot_wanted[:, None]).astype(jnp.bfloat16)
    assembled = jnp.dot(
        selector,
        arrived_tiles.reshape(n_rows * CAP, block_size * block_size),
        preferred_element_type=jnp.float32,
    )
    assembled = assembled.astype(jnp.bfloat16).reshape(slot_count, block_size, block_size)
    ghost_ids = ghost_list[0]
    owners = jnp.arange(n_rows, dtype=jnp.int32)[:, None] * row_blocks
    requested = jnp.where(ghost_ids >= 0, ghost_ids - owners, -1)
    wanted_by = lax.all_to_all(requested, "rows", split_axis=0, concat_axis=0, tiled=True)
    rows_local = pattern[0, :, 0]
    sources = pattern[0, :, 1]
    center = (damp_upper[0] + damp_lower[0]) / 2.0
    half_width = (damp_upper[0] - damp_lower[0]) / 2.0

    def own_blocks(vectors):
        return (
            vectors.astype(jnp.bfloat16)
            .reshape(vec_count, row_blocks, block_size)
            .transpose(1, 0, 2)
        )

    def with_ghosts(blocks):
        outgoing = jnp.where(
            (wanted_by >= 0)[:, :, None, None],
            blocks[jnp.clip(wanted_by, 0, row_blocks - 1)],
            jnp.zeros((), jnp.bfloat16),
        )
        arrived = lax.all_to_all(outgoing, "rows", split_axis=0, concat_axis=0, tiled=True)
        return jnp.concatenate(
            [blocks, arrived.reshape(n_rows * ghost_width, vec_count, block_size)], axis=0
        )

    def accumulate(tile_part, source_part, row_part, operand_pool):
        operands = operand_pool[source_part]
        products = jnp.einsum(
            "kvb,kab->kva", operands, tile_part, preferred_element_type=jnp.float32
        )
        row_select = (row_part[:, None] == jnp.arange(row_blocks, dtype=jnp.int32)[None, :]).astype(
            jnp.float32
        )
        return jnp.einsum("ki,kva->iva", row_select, products, precision=lax.Precision.HIGHEST)

    def as_field(running):
        return running.transpose(1, 0, 2).reshape(vec_count, row_blocks * block_size)

    def product(blocks, group_tiles):
        operand_pool = with_ghosts(blocks)
        running = accumulate(group_tiles, sources, rows_local, operand_pool)
        return as_field(running)

    group_tiles = lax.all_gather(assembled, "cols", axis=0, tiled=True)
    first_image = product(own_blocks(state), group_tiles)
    first_term = (first_image - center * state) / half_width
    second_image = product(own_blocks(first_term), group_tiles)
    second_term = 2.0 * (second_image - center * first_term) / half_width - state
    return (first_term, second_term)


def solution(mesh):
    in_specs = (
        P(("rows", "cols"), None, None),
        P(("rows", "cols")),
        P(("rows", "cols"), None),
        P("rows", None, None),
        P("rows", None, None),
        P("cols", "rows"),
        P(),
        P(),
    )
    out_specs = (P("cols", "rows"), P("cols", "rows"))
    return jax.shard_map(
        on_device, mesh=mesh, in_specs=in_specs, out_specs=out_specs, check_vma=False
    )
```

profile of v0, /device:TPU:56, one launch (start us, length us, event | category | flops | bytes accessed | tf_op | source)
XLA Modules:
  0.0 650.6 jit_solution(13887404985358008637)
XLA Ops:
  9.2 2.3 gather_fusion.4
  12.3 15.9 %all-to-all-start.2 = ((s32[64,1,4]{2,1,0:T(1,128)}), s32[64,1,4]{2,1,0:T(1,128)S(1)}, u32[]{:S(2)}, u32[]{:S(2)}) async-start(s32[64,1,4]{2,1,0:T(1,128)} %bitcast.17), calls=%async_computation.2 | async-start | bytes 65536 | tf_op jit(solution)/shard_map/all_to_all | solution.py:53
  31.4 126.3 %while.10 = (s32[]{:T(128)}, bf16[32,4,128,128]{3,2,1,0:T(8,128)(2,1)}, s32[32,4,2]{1,0,2:T(8,128)S(1)}, bf16[16,512,128]{2,1,0:T(8,128)(2,1)}, bf16[16,512,128]{2,1,0:T(8,128)(2,1)S(1)}, /*index=5*/s32[]{:T(128)}) while((s32[]{:T(128)}, bf16[32,4,128,128]{3,2,1,0:T(8,128)(2,1)}, s32[32,4,2]{1,0,2:T(8,128)S(1)}, ...), condition=%wide.region_5.6_spmd, body=%wide.region_4.5_spmd.sunk | while | flops 67176472 | bytes 3285769 | solution.py:30
  31.4 2.2 gather_fusion
  35.4 2.2 gather_fusion
  39.3 2.2 gather_fusion
  43.2 2.2 gather_fusion
  47.2 2.2 gather_fusion
  51.1 2.2 gather_fusion
  55.1 2.2 gather_fusion
  157.7 10.7 %gather_fusion.5 = bf16[256,128,128]{2,1,0:T(8,128)(2,1)} fusion(bf16[128,128,128]{2,1,0:T(8,128)(2,1)} %bitcast.112, s32[1024]{0:T(1024)S(1)} %pad_clamp_fusion.2), kind=kCustom, calls=%fused_computation.5 | custom fusion | bytes 16778240 | tf_op jit(solution)/shard_map/gather | solution.py:48
  168.4 7.3 %broadcast_select_fusion = bf16[64,4,128,128]{3,2,1,0:T(8,128)(2,1)} fusion(bf16[64,4,128,128]{3,2,1,0:T(8,128)(2,1)} %bitcast.110, pred[64,4]{1,0:T(8,128)(4,1)S(1)} %broadcast_in_dim.84), kind=kLoop, calls=%fused_computation.21 | loop fusion | flops 4194304 | bytes 16777472 | tf_op jit(solution)/shard_map/jit(_where)/select_n | solution.py:47
  175.6 12.9 %all-to-all-start.3 = ((bf16[64,4,128,128]{3,2,1,0:T(8,128)(2,1)}), bf16[64,4,128,128]{3,2,1,0:T(8,128)(2,1)}, u32[]{:S(2)}, u32[]{:S(2)}) async-start(bf16[64,4,128,128]{3,2,1,0:T(8,128)(2,1)} %broadcast_select_fusion), calls=%async_computation.3 | async-start | bytes 16777216 | tf_op jit(solution)/shard_map/all_to_all | solution.py:52
  190.1 222.6 %all-to-all-done.3 = bf16[64,4,128,128]{3,2,1,0:T(8,128)(2,1)} async-done(((bf16[64,4,128,128]{3,2,1,0:T(8,128)(2,1)}), bf16[64,4,128,128]{3,2,1,0:T(8,128)(2,1)}, u32[]{:S(2)}, u32[]{:S(2)}) %all-to-all-start.3) | async-done | bytes 8388640 | tf_op jit(solution)/shard_map/all_to_all | solution.py:52
  412.7 7.9 %fusion.10 = bf16[2,8,128,128]{3,1,2,0:T(8,128)(2,1)S(1)} fusion(bf16[32,8,128,128]{3,2,1,0:T(8,128)(2,1)} %bitcast.37, s32[256]{0:T(256)S(1)} %eq.73), kind=kOutput, calls=%fused_computation.31 | convolution fusion | flops 134483968 | bytes 8913920 | tf_op jit(solution)/shard_map/dot_general | solution.py:56
  422.3 70.2 %all-to-all-start = ((s32[64,1,2]{2,1,0:T(1,128)}), s32[64,1,2]{2,1,0:T(1,128)S(1)}, u32[]{:S(2)}, u32[]{:S(2)}) async-start(s32[64,1,2]{2,1,0:T(1,128)} %copy.39), calls=%async_computation | async-start | bytes 65536 | tf_op jit(solution)/shard_map/all_to_all | solution.py:65
  492.5 9.5 %all-to-all-done = s32[64,1,2]{2,1,0:T(1,128)S(1)} async-done(((s32[64,1,2]{2,1,0:T(1,128)}), s32[64,1,2]{2,1,0:T(1,128)S(1)}, u32[]{:S(2)}, u32[]{:S(2)}) %all-to-all-start) | async-done | bytes 544 | tf_op jit(solution)/shard_map/all_to_all | solution.py:65
  505.0 7.1 %all-to-all-start.1 = ((bf16[64,2,64,128]{3,2,1,0:T(8,128)(2,1)}), bf16[64,2,64,128]{3,2,1,0:T(8,128)(2,1)S(1)}, u32[]{:S(2)}, u32[]{:S(2)}) async-start(bf16[64,2,64,128]{3,2,1,0:T(8,128)(2,1)} %broadcast_select_fusion.2), calls=%async_computation.1 | async-start | bytes 4194304 | tf_op jit(solution)/shard_map/all_to_all | solution.py:84
  513.5 46.2 %all-to-all-done.1 = bf16[64,2,64,128]{3,2,1,0:T(8,128)(2,1)S(1)} async-done(((bf16[64,2,64,128]{3,2,1,0:T(8,128)(2,1)}), bf16[64,2,64,128]{3,2,1,0:T(8,128)(2,1)S(1)}, u32[]{:S(2)}, u32[]{:S(2)}) %all-to-all-start.1) | async-done | bytes 2097184 | tf_op jit(solution)/shard_map/all_to_all | solution.py:84
  564.9 5.8 fusion.27
  570.7 3.8 fusion.8
  575.8 55.2 %all_to_all.27 = bf16[64,2,64,128]{3,2,1,0:T(8,128)(2,1)S(1)} all-to-all(bf16[64,2,64,128]{3,2,1,0:T(8,128)(2,1)S(1)} %broadcast_select_fusion.1), channel_id=1, replica_groups=mesh['rows'=64,'cols'=8] {'rows'}, dimensions={0} | all-to-all | bytes 4194304 | tf_op jit(solution)/shard_map/all_to_all | solution.py:84
  633.4 5.8 fusion.28
  639.2 3.8 fusion.6
  (244 shorter events, 131.6 us)
Async XLA Ops:
  12.3 163.3 %all-to-all-start.2 = ((s32[64,1,4]{2,1,0:T(1,128)}), s32[64,1,4]{2,1,0:T(1,128)S(1)}, u32[]{:S(2)}, u32[]{:S(2)}) async-start(s32[64,1,4]{2,1,0:T(1,128)} %bitcast.17), calls=%async_computation.2 | async-start | bytes 65536 | tf_op jit(solution)/shard_map/all_to_all | solution.py:53
  175.6 237.1 %all-to-all-start.3 = ((bf16[64,4,128,128]{3,2,1,0:T(8,128)(2,1)}), bf16[64,4,128,128]{3,2,1,0:T(8,128)(2,1)}, u32[]{:S(2)}, u32[]{:S(2)}) async-start(bf16[64,4,128,128]{3,2,1,0:T(8,128)(2,1)} %broadcast_select_fusion), calls=%async_computation.3 | async-start | bytes 16777216 | tf_op jit(solution)/shard_map/all_to_all | solution.py:52
  188.5 376.4 %all-gather.2.cloned.1.call-start = ((), (), s32[]{:S(2)}) async-start(), calls=%async_computation.5 | async-start | bytes 4718592 | tf_op jit(solution)/shard_map/all_gather | solution.py:107
  412.7 8.9 %copy-start.3 = (s32[1,64,2]{1,2,0:T(2,128)S(1)}, s32[1,64,2]{1,2,0:T(2,128)}, u32[]{:S(2)}) copy-start(s32[1,64,2]{1,2,0:T(2,128)} %param.14) | copy-start | bytes 1540
  412.7 79.8 %copy-start.1 = (f32[64,1024]{1,0:T(8,128)S(1)}, f32[64,1024]{1,0:T(8,128)}, u32[]{:S(2)}) copy-start(f32[64,1024]{1,0:T(8,128)} %param.15) | copy-start | bytes 786436
  422.3 79.7 %all-to-all-start = ((s32[64,1,2]{2,1,0:T(1,128)}), s32[64,1,2]{2,1,0:T(1,128)S(1)}, u32[]{:S(2)}, u32[]{:S(2)}) async-start(s32[64,1,2]{2,1,0:T(1,128)} %copy.39), calls=%async_computation | async-start | bytes 65536 | tf_op jit(solution)/shard_map/all_to_all | solution.py:65
  505.0 8.5 %copy-start.4 = (s32[1,128,2]{1,2,0:T(2,128)S(1)}, s32[1,128,2]{1,2,0:T(2,128)}, u32[]{:S(2)}) copy-start(s32[1,128,2]{1,2,0:T(2,128)} %param.13) | copy-start | bytes 3076
  505.0 54.7 %all-to-all-start.1 = ((bf16[64,2,64,128]{3,2,1,0:T(8,128)(2,1)}), bf16[64,2,64,128]{3,2,1,0:T(8,128)(2,1)S(1)}, u32[]{:S(2)}, u32[]{:S(2)}) async-start(bf16[64,2,64,128]{3,2,1,0:T(8,128)(2,1)} %broadcast_select_fusion.2), calls=%async_computation.1 | async-start | bytes 4194304 | tf_op jit(solution)/shard_map/all_to_all | solution.py:84
  559.7 1.3 copy-start
  574.6 68.4 %copy-start.2 = (f32[64,1024]{1,0:T(8,128)}, f32[64,1024]{1,0:T(8,128)S(1)}, u32[]{:S(2)}) copy-start(f32[64,1024]{1,0:T(8,128)S(1)} %get-tuple-element.61) | copy-start | bytes 786436
Sparse Core Ops, SparseCore 0:
  421.7 93.4 all-gather.1
where the time goes:
time: 657 us; the launch traced here: 651 us
  waiting for transfers between devices  278 us (42%)
  local copies, waits for them, and re-layouts  118 us (18%)
  starting transfers between devices  106 us (16%)
  matrix products  59.5 us (9%)
  blocking collectives  55.2 us (8%)
  other arithmetic  16.8 us (3%)
  between operations  15.6 us (2%)
    all_to_all x1, waiting for transfers between devices, on_device(): lax.all_to_all(send_tiles, 'rows', split_axis=0, concat_axis=0, tiled=True)  223 us
    gather x32, local copies, waits for them, and re-layouts, pair_block(): left_vals = basis_values[index_pair[:, 0]]  71.7 us
    all_to_all x1, starting transfers between devices, on_device(): lax.all_to_all(requested, 'rows', split_axis=0, concat_axis=0, tiled=True)  70.2 us
    all_to_all x1, blocking collectives, with_ghosts(): lax.all_to_all(outgoing, 'rows', split_axis=0, concat_axis=0, tiled=True)  55.2 us
    all_to_all x1, waiting for transfers between devices, with_ghosts(): lax.all_to_all(outgoing, 'rows', split_axis=0, concat_axis=0, tiled=True)  46.2 us
    dot_general x32, matrix products, pair_block(): jnp.einsum('snx,sny->sxy', left_vals, right_vals, preferred_element_type=...  32.4 us
    gather x32, local copies, waits for them, and re-layouts, pair_block(): right_vals = weighted[index_pair[:, 1]]  20.7 us
    all_to_all x1, starting transfers between devices, on_device(): lax.all_to_all(send_slots, 'rows', split_axis=0, concat_axis=0, tiled=True)  15.9 us
  transfers between devices with their start and end apart: 5, of which 3 were waited for; matrix products, arithmetic and copies ran while one was open for 24% of the time, Pallas kernels for 0%

commit v1 on v0

v1 whole, which is shorter than its diff:
```python
import jax
import jax.numpy as jnp
from jax import lax
from jax.sharding import PartitionSpec as P


def on_device(
    basis_values, potential, contrib_index, pattern, ghost_list, state, damp_lower, damp_upper
):
    n_rows = lax.axis_size("rows")
    n_cols = lax.axis_size("cols")
    basis_blocks, points, block_size = basis_values.shape
    vec_count = state.shape[0]
    row_blocks = state.shape[1] // block_size
    group_slots = pattern.shape[1]
    slot_count = group_slots // n_cols
    ghost_width = ghost_list.shape[2]
    pair_count = basis_blocks * basis_blocks

    ghost_ids = ghost_list[0]
    owners = jnp.arange(n_rows, dtype=jnp.int32)[:, None] * row_blocks
    requested = jnp.where(ghost_ids >= 0, ghost_ids - owners, -1)
    target_row = contrib_index[:, 0]
    to_target = target_row[:, None] == jnp.arange(n_rows, dtype=jnp.int32)[None, :]
    slot_for_target = jnp.max(jnp.where(to_target, contrib_index[:, 1:2], -1), axis=0)
    index_send = jnp.concatenate([requested, slot_for_target[:, None]], axis=1)
    index_recv = lax.all_to_all(index_send, "rows", split_axis=0, concat_axis=0, tiled=True)
    wanted_by = index_recv[:, :ghost_width]
    arrived_slots = index_recv[:, ghost_width]

    center = (damp_upper[0] + damp_lower[0]) / 2.0
    half_width = (damp_upper[0] - damp_lower[0]) / 2.0

    def own_blocks(vectors):
        return (
            vectors.astype(jnp.bfloat16)
            .reshape(vec_count, row_blocks, block_size)
            .transpose(1, 0, 2)
        )

    def with_ghosts(blocks):
        outgoing = jnp.where(
            (wanted_by >= 0)[:, :, None, None],
            blocks[jnp.clip(wanted_by, 0, row_blocks - 1)],
            jnp.zeros((), jnp.bfloat16),
        )
        arrived = lax.all_to_all(outgoing, "rows", split_axis=0, concat_axis=0, tiled=True)
        return jnp.concatenate(
            [blocks, arrived.reshape(n_rows * ghost_width, vec_count, block_size)], axis=0
        )

    state_blocks = own_blocks(state)
    state_pool = with_ghosts(state_blocks)

    weighted = (basis_values.astype(jnp.float32) * potential[None, :, None]).astype(jnp.bfloat16)
    pair_tiles = jnp.einsum(
        "anx,bny->abxy", basis_values, weighted, preferred_element_type=jnp.float32
    ).astype(jnp.bfloat16)
    pair_id = contrib_index[:, 2] * basis_blocks + contrib_index[:, 3]
    pair_hot = (pair_id[:, None] == jnp.arange(pair_count, dtype=jnp.int32)[None, :]).astype(
        jnp.bfloat16
    )
    counts = jnp.dot(
        to_target.astype(jnp.bfloat16).T, pair_hot, preferred_element_type=jnp.float32
    ).astype(jnp.bfloat16)
    send_tiles = jnp.dot(
        counts,
        pair_tiles.reshape(pair_count, block_size * block_size),
        preferred_element_type=jnp.float32,
    ).astype(jnp.bfloat16).reshape(n_rows, block_size, block_size)
    arrived_tiles = lax.all_to_all(send_tiles, "rows", split_axis=0, concat_axis=0, tiled=True)
    slot_wanted = jnp.arange(slot_count, dtype=jnp.int32)
    selector = (arrived_slots[None, :] == slot_wanted[:, None]).astype(jnp.bfloat16)
    assembled = jnp.dot(
        selector,
        arrived_tiles.reshape(n_rows, block_size * block_size),
        preferred_element_type=jnp.float32,
    )
    assembled = assembled.astype(jnp.bfloat16).reshape(slot_count, block_size, block_size)
    group_tiles = lax.all_gather(assembled, "cols", axis=0, tiled=True)

    rows_local = pattern[0, :, 0]
    sources = pattern[0, :, 1]

    def accumulate(tile_part, source_part, row_part, operand_pool):
        operands = operand_pool[source_part]
        products = jnp.einsum(
            "kvb,kab->kva", operands, tile_part, preferred_element_type=jnp.float32
        )
        row_select = (row_part[:, None] == jnp.arange(row_blocks, dtype=jnp.int32)[None, :]).astype(
            jnp.float32
        )
        return jnp.einsum("ki,kva->iva", row_select, products, precision=lax.Precision.HIGHEST)

    def as_field(running):
        return running.transpose(1, 0, 2).reshape(vec_count, row_blocks * block_size)

    first_image = as_field(accumulate(group_tiles, sources, rows_local, state_pool))
    first_term = (first_image - center * state) / half_width
    first_pool = with_ghosts(own_blocks(first_term))
    second_image = as_field(accumulate(group_tiles, sources, rows_local, first_pool))
    second_term = 2.0 * (second_image - center * first_term) / half_width - state
    return (first_term, second_term)


def solution(mesh):
    in_specs = (
        P(("rows", "cols"), None, None),
        P(("rows", "cols")),
        P(("rows", "cols"), None),
        P("rows", None, None),
        P("rows", None, None),
        P("cols", "rows"),
        P(),
        P(),
    )
    out_specs = (P("cols", "rows"), P("cols", "rows"))
    return jax.shard_map(
        on_device, mesh=mesh, in_specs=in_specs, out_specs=out_specs, check_vma=False
    )
```

time: 657 us -> 281 us (0.43)
  waiting for transfers between devices: 278 us -> 96.7 us
  local copies, waits for them, and re-layouts: 118 us -> 23.8 us
  starting transfers between devices: 106 us -> 40.3 us
  matrix products: 59.5 us -> 39 us
  other arithmetic: 16.8 us -> 6.3 us
    all_to_all x1, waiting for transfers between devices: 223 us -> 49.3 us  [on_device(): lax.all_to_all(send_tiles, 'rows', split_axis=0, concat_axis=0, tiled=True)]
    gather x66 -> x0, local copies, waits for them, and re-layouts: 105 us -> none  [the longest x32 71.7 us: pair_block(): left_vals = basis_values[index_pair[:, 0]]]
    all_to_all x2 -> x1, starting transfers between devices: 86.1 us -> 15.9 us  [on_device(): lax.all_to_all(index_send, 'rows', split_axis=0, concat_axis=0, tiled=True)]
    dot_general x33 -> x3, matrix products: 40.3 us -> 19.8 us  [the longest x1 10.1 us: on_device(): jnp.einsum('anx,bny->abxy', basis_values, weighted, preferred_element_typ...]
    convert_element_type x0 -> x1, local copies, waits for them, and re-layouts: none -> 12.3 us  [on_device(): pair_tiles = jnp.einsum('anx,bny->abxy', basis_values, weighted, preferre...]
    all_to_all x2 -> x1, waiting for transfers between devices: 9.49 us -> 0.01 us  [on_device(): lax.all_to_all(index_send, 'rows', split_axis=0, concat_axis=0, tiled=True)]
    select_n x34 -> x0, other arithmetic: 7.54 us -> none  [the longest x1 7.26 us: on_device(): jnp.where(filled[:, None, None], tile_set[source], jnp.zeros((), jnp.bflo...]
  transfers between devices with their start and end apart: 5 -> 4, of which waited for: 3 -> 2; matrix products, arithmetic and copies ran while one was open for 24% -> 14% of each run, Pallas kernels for 0% -> 0%
where the time goes in v1:
time: 281 us; the launch traced here: 278 us
  waiting for transfers between devices  96.7 us (34%)
  blocking collectives  55.9 us (20%)
  starting transfers between devices  40.3 us (14%)
  matrix products  39 us (14%)
  local copies, waits for them, and re-layouts  23.8 us (8%)
  between operations  15.5 us (6%)
  other arithmetic  6.3 us (2%)
    all_to_all x1, blocking collectives, with_ghosts(): lax.all_to_all(outgoing, 'rows', split_axis=0, concat_axis=0, tiled=True)  55.9 us
    all_to_all x1, waiting for transfers between devices, on_device(): lax.all_to_all(send_tiles, 'rows', split_axis=0, concat_axis=0, tiled=True)  49.3 us
    all_to_all x1, waiting for transfers between devices, with_ghosts(): lax.all_to_all(outgoing, 'rows', split_axis=0, concat_axis=0, tiled=True)  47.4 us
    all_to_all x1, starting transfers between devices, on_device(): lax.all_to_all(index_send, 'rows', split_axis=0, concat_axis=0, tiled=True)  15.9 us
    all_to_all x1, starting transfers between devices, on_device(): lax.all_to_all(send_tiles, 'rows', split_axis=0, concat_axis=0, tiled=True)  12.7 us
    convert_element_type x1, local copies, waits for them, and re-layouts, on_device(): pair_tiles = jnp.einsum('anx,bny->abxy', basis_values, weighted, preferre...  12.3 us
    all_to_all x1, starting transfers between devices, with_ghosts(): lax.all_to_all(outgoing, 'rows', split_axis=0, concat_axis=0, tiled=True)  11.7 us
    dot_general x2, matrix products, accumulate(): jnp.einsum('kvb,kab->kva', operands, tile_part, preferred_element_type=jn...  11.6 us
  transfers between devices with their start and end apart: 4, of which 2 were waited for; matrix products, arithmetic and copies ran while one was open for 14% of the time, Pallas kernels for 0%

profile of v1, /device:TPU:56, one launch (start us, length us, event | category | flops | bytes accessed | tf_op | source)
XLA Modules:
  0.0 277.5 jit_solution(16939795496643485081)
XLA Ops:
  7.2 0.8 add_bitcast_fusion.1
  9.5 15.9 %all-to-all-start = ((s32[64,1,3]{2,1,0:T(1,128)}), s32[64,1,3]{2,1,0:T(1,128)S(1)}, u32[]{:S(2)}, u32[]{:S(2)}) async-start(s32[64,1,3]{2,1,0:T(1,128)} %copy.36), calls=%async_computation | async-start | bytes 65536 | tf_op jit(solution)/shard_map/all_to_all | solution.py:27
  25.4 10.1 %convert_bitcast_fusion = bf16[16,16,128,128]{2,3,0,1:T(8,128)(2,1)} fusion(bf16[16,512,128]{2,1,0:T(8,128)(2,1)} %param.8, f32[512]{0:T(512)} %param.9), kind=kOutput, calls=%fused_computation.8 | convolution fusion | flops 4302307328 | bytes 10487808 | tf_op jit(solution)/shard_map/anx,bny->abxy/dot_general | solution.py:56
  35.6 12.3 %copy.41 = bf16[16,16,128,128]{3,2,1,0:T(8,128)(2,1)} copy(bf16[16,16,128,128]{2,3,0,1:T(8,128)(2,1)} %convert_bitcast_fusion) | data formatting | bytes 16777216 | tf_op jit(solution)/shard_map/convert_element_type | solution.py:58
  47.9 8.4 %fusion.12 = bf16[8,8,128,128]{3,1,2,0:T(8,128)(2,1)S(1)} fusion(bf16[32,8,128,128]{3,2,1,0:T(8,128)(2,1)} %bitcast.100, s32[128]{0:T(128)S(1)} %get-tuple-element.4, s32[128]{0:T(128)S(1)} %get-tuple-element.5), kind=kOutput, calls=%fused_computation.23 | convolution fusion | flops 542171136 | bytes 10486784 | tf_op jit(solution)/shard_map/dot_general | solution.py:66
  56.3 1.9 copy.51
  58.2 12.7 %all-to-all-start.2 = ((bf16[64,128,128]{2,1,0:T(8,128)(2,1)}), bf16[64,128,128]{2,1,0:T(8,128)(2,1)S(1)}, u32[]{:S(2)}, u32[]{:S(2)}) async-start(bf16[64,128,128]{2,1,0:T(8,128)(2,1)} %bitcast.35), calls=%async_computation.2 | async-start | bytes 4194304 | tf_op jit(solution)/shard_map/all_to_all | solution.py:71
  71.0 49.3 %all-to-all-done.2 = bf16[64,128,128]{2,1,0:T(8,128)(2,1)S(1)} async-done(((bf16[64,128,128]{2,1,0:T(8,128)(2,1)}), bf16[64,128,128]{2,1,0:T(8,128)(2,1)S(1)}, u32[]{:S(2)}, u32[]{:S(2)}) %all-to-all-start.2) | async-done | bytes 2097184 | tf_op jit(solution)/shard_map/all_to_all | solution.py:71
  120.3 1.2 fusion.15
  121.5 0.9 copy.53
  122.9 1.0 gather_fusion
  123.8 1.5 broadcast_select_fusion.1
  125.4 11.7 %all-to-all-start.1 = ((bf16[64,2,64,128]{3,2,1,0:T(8,128)(2,1)}), bf16[64,2,64,128]{3,2,1,0:T(8,128)(2,1)S(1)}, u32[]{:S(2)}, u32[]{:S(2)}) async-start(bf16[64,2,64,128]{3,2,1,0:T(8,128)(2,1)} %broadcast_select_fusion.1), calls=%async_computation.1 | async-start | bytes 4194304 | tf_op jit(solution)/shard_map/all_to_all | solution.py:47
  138.5 47.4 %all-to-all-done.1 = bf16[64,2,64,128]{3,2,1,0:T(8,128)(2,1)S(1)} async-done(((bf16[64,2,64,128]{3,2,1,0:T(8,128)(2,1)}), bf16[64,2,64,128]{3,2,1,0:T(8,128)(2,1)S(1)}, u32[]{:S(2)}, u32[]{:S(2)}) %all-to-all-start.1) | async-done | bytes 2097184 | tf_op jit(solution)/shard_map/all_to_all | solution.py:47
  185.9 1.3 copy-done
  187.2 1.8 pad_maximum_fusion
  189.0 2.1 gather_fusion.1
  191.1 5.8 %fusion.34 = f32[128,64,128]{2,1,0:T(8,128)S(1)} fusion(bf16[128,64,128]{2,1,0:T(8,128)(2,1)} %gather_fusion.1, bf16[128,128,128]{2,1,0:T(8,128)(2,1)} %all-gather.2.cloned.1.call-done), kind=kOutput, calls=%fused_computation.62 | convolution fusion | flops 268435456 | bytes 10485760 | tf_op jit(solution)/shard_map/kvb,kab->kva/dot_general | solution.py:87
  196.9 3.8 %fusion.4 = f32[8,64,128]{2,0,1:T(8,128)S(1)} fusion(f32[128,64,128]{2,1,0:T(8,128)S(1)} %fusion.34, s32[128]{0:T(128)S(1)} %slice_bitcast_fusion.3), kind=kOutput, calls=%fused_computation.11 | convolution fusion | flops 100664320 | bytes 4456960 | tf_op jit(solution)/shard_map/ki,kva->iva/dot_general | solution.py:93
  200.8 1.0 gather_fusion.2
  202.0 55.9 %all_to_all.27 = bf16[64,2,64,128]{3,2,1,0:T(8,128)(2,1)S(1)} all-to-all(bf16[64,2,64,128]{3,2,1,0:T(8,128)(2,1)S(1)} %broadcast_select_fusion), channel_id=1, replica_groups=mesh['rows'=64,'cols'=8] {'rows'}, dimensions={0} | all-to-all | bytes 4194304 | tf_op jit(solution)/shard_map/all_to_all | solution.py:47
  258.1 2.1 gather_fusion.3
  260.3 5.8 %fusion.35 = f32[128,64,128]{2,1,0:T(8,128)S(1)} fusion(bf16[128,64,128]{2,1,0:T(8,128)(2,1)} %gather_fusion.3, bf16[128,128,128]{2,1,0:T(8,128)(2,1)} %all-gather.2.cloned.1.call-done), kind=kOutput, calls=%fused_computation.63 | convolution fusion | flops 268435456 | bytes 10485760 | tf_op jit(solution)/shard_map/kvb,kab->kva/dot_general | solution.py:87
  266.1 3.8 %fusion.2 = f32[8,64,128]{2,0,1:T(8,128)S(1)} fusion(f32[128,64,128]{2,1,0:T(8,128)S(1)} %fusion.35, s32[128]{0:T(128)S(1)} %slice_bitcast_fusion.3), kind=kOutput, calls=%fused_computation.9 | convolution fusion | flops 100664320 | bytes 4456960 | tf_op jit(solution)/shard_map/ki,kva->iva/dot_general | solution.py:93
  (33 shorter events, 3.4 us)
Async XLA Ops:
  9.5 48.7 %all-to-all-start = ((s32[64,1,3]{2,1,0:T(1,128)}), s32[64,1,3]{2,1,0:T(1,128)S(1)}, u32[]{:S(2)}, u32[]{:S(2)}) async-start(s32[64,1,3]{2,1,0:T(1,128)} %copy.36), calls=%async_computation | async-start | bytes 65536 | tf_op jit(solution)/shard_map/all_to_all | solution.py:27
  58.2 62.1 %all-to-all-start.2 = ((bf16[64,128,128]{2,1,0:T(8,128)(2,1)}), bf16[64,128,128]{2,1,0:T(8,128)(2,1)S(1)}, u32[]{:S(2)}, u32[]{:S(2)}) async-start(bf16[64,128,128]{2,1,0:T(8,128)(2,1)} %bitcast.35), calls=%async_computation.2 | async-start | bytes 4194304 | tf_op jit(solution)/shard_map/all_to_all | solution.py:71
  70.9 120.2 %all-gather.2.cloned.1.call-start = ((), (), s32[]{:S(2)}) async-start(), calls=%async_computation.4 | async-start | bytes 4718592 | tf_op jit(solution)/shard_map/all_gather | solution.py:80
  120.3 2.2 copy-start.1
  125.4 13.0 %copy-start.3 = (s32[1,128,2]{1,2,0:T(2,128)S(1)}, s32[1,128,2]{1,2,0:T(2,128)}, u32[]{:S(2)}) copy-start(s32[1,128,2]{1,2,0:T(2,128)} %param.11) | copy-start | bytes 3076
  125.4 60.5 %all-to-all-start.1 = ((bf16[64,2,64,128]{3,2,1,0:T(8,128)(2,1)}), bf16[64,2,64,128]{3,2,1,0:T(8,128)(2,1)S(1)}, u32[]{:S(2)}, u32[]{:S(2)}) async-start(bf16[64,2,64,128]{3,2,1,0:T(8,128)(2,1)} %broadcast_select_fusion.1), calls=%async_computation.1 | async-start | bytes 4194304 | tf_op jit(solution)/shard_map/all_to_all | solution.py:47
  185.9 1.3 copy-start
  200.8 69.1 %copy-start.2 = (f32[64,1024]{1,0:T(8,128)}, f32[64,1024]{1,0:T(8,128)S(1)}, u32[]{:S(2)}) copy-start(f32[64,1024]{1,0:T(8,128)S(1)} %get-tuple-element.3) | copy-start | bytes 786436
Sparse Core Ops, SparseCore 0:
  122.6 37.0 all-gather.1

commit v2 on v1

--- a/solution.py
+++ b/solution.py
@@ -68,6 +68,7 @@
         pair_tiles.reshape(pair_count, block_size * block_size),
         preferred_element_type=jnp.float32,
     ).astype(jnp.bfloat16).reshape(n_rows, block_size, block_size)
+    send_tiles, state_pool = lax.optimization_barrier((send_tiles, state_pool))
     arrived_tiles = lax.all_to_all(send_tiles, "rows", split_axis=0, concat_axis=0, tiled=True)
     slot_wanted = jnp.arange(slot_count, dtype=jnp.int32)
     selector = (arrived_slots[None, :] == slot_wanted[:, None]).astype(jnp.bfloat16)

time: 281 us -> 291 us (1.036)
  blocking collectives: 55.9 us -> 63.4 us
  starting transfers between devices: 40.3 us -> 32.9 us
  waiting for transfers between devices: 96.7 us -> 100 us
  matrix products: 39 us -> 42 us
    all_to_all x1, waiting for transfers between devices: 47.4 us -> 13.5 us  [with_ghosts(): lax.all_to_all(outgoing, 'rows', split_axis=0, concat_axis=0, tiled=True)]
    all_gather x1, waiting for transfers between devices: 0.01 us -> 30.1 us  [on_device(): group_tiles = lax.all_gather(assembled, 'cols', axis=0, tiled=True)]
    all_to_all x1, waiting for transfers between devices: 0.01 us -> 8.55 us  [on_device(): lax.all_to_all(index_send, 'rows', split_axis=0, concat_axis=0, tiled=True)]
    all_to_all x1, blocking collectives: 55.9 us -> 63.4 us  [with_ghosts(): lax.all_to_all(outgoing, 'rows', split_axis=0, concat_axis=0, tiled=True)]
    all_to_all x1, starting transfers between devices: 11.7 us -> 7.15 us  [with_ghosts(): lax.all_to_all(outgoing, 'rows', split_axis=0, concat_axis=0, tiled=True)]
    all_to_all x1, starting transfers between devices: 12.7 us -> 9.55 us  [on_device(): lax.all_to_all(send_tiles, 'rows', split_axis=0, concat_axis=0, tiled=True)]
  transfers between devices with their start and end apart: 4 -> 4, of which waited for: 2 -> 4; matrix products, arithmetic and copies ran while one was open for 14% -> 14% of each run, Pallas kernels for 0% -> 0%
where the time goes in v2:
time: 291 us; the launch traced here: 287 us
  waiting for transfers between devices  100 us (34%)
  blocking collectives  63.4 us (22%)
  matrix products  42 us (14%)
  starting transfers between devices  32.9 us (11%)
  local copies, waits for them, and re-layouts  25.4 us (9%)
  between operations  15.5 us (5%)
  other arithmetic  7.26 us (2%)
    all_to_all x1, blocking collectives, with_ghosts(): lax.all_to_all(outgoing, 'rows', split_axis=0, concat_axis=0, tiled=True)  63.4 us
    all_to_all x1, waiting for transfers between devices, on_device(): lax.all_to_all(send_tiles, 'rows', split_axis=0, concat_axis=0, tiled=True)  48.3 us
    all_gather x1, waiting for transfers between devices, on_device(): group_tiles = lax.all_gather(assembled, 'cols', axis=0, tiled=True)  30.1 us
    all_to_all x1, starting transfers between devices, on_device(): lax.all_to_all(index_send, 'rows', split_axis=0, concat_axis=0, tiled=True)  15.9 us
    all_to_all x1, waiting for transfers between devices, with_ghosts(): lax.all_to_all(outgoing, 'rows', split_axis=0, concat_axis=0, tiled=True)  13.5 us
    convert_element_type x1, local copies, waits for them, and re-layouts, on_device(): pair_tiles = jnp.einsum('anx,bny->abxy', basis_values, weighted, preferre...  12.3 us
    dot_general x2, matrix products, accumulate(): jnp.einsum('kvb,kab->kva', operands, tile_part, preferred_element_type=jn...  11.6 us
    dot_general x1, matrix products, on_device(): jnp.einsum('anx,bny->abxy', basis_values, weighted, preferred_element_typ...  10.1 us
  transfers between devices with their start and end apart: 4, of which 4 were waited for; matrix products, arithmetic and copies ran while one was open for 14% of the time, Pallas kernels for 0%

profile of v2, /device:TPU:56, one launch (start us, length us, event | category | flops | bytes accessed | tf_op | source)
XLA Modules:
  0.0 286.8 jit_solution(3091037968818858958)
XLA Ops:
  9.5 15.9 %all-to-all-start = ((s32[64,1,3]{2,1,0:T(1,128)}), s32[64,1,3]{2,1,0:T(1,128)S(1)}, u32[]{:S(2)}, u32[]{:S(2)}) async-start(s32[64,1,3]{2,1,0:T(1,128)} %copy.38), calls=%async_computation | async-start | bytes 65536 | tf_op jit(solution)/shard_map/all_to_all | solution.py:27
  25.4 1.0 bitcast_bitcast_fusion.1
  26.4 8.6 %all-to-all-done = s32[64,1,3]{2,1,0:T(1,128)S(1)} async-done(((s32[64,1,3]{2,1,0:T(1,128)}), s32[64,1,3]{2,1,0:T(1,128)S(1)}, u32[]{:S(2)}, u32[]{:S(2)}) %all-to-all-start) | async-done | bytes 800 | tf_op jit(solution)/shard_map/all_to_all | solution.py:27
  36.4 1.5 broadcast_select_fusion.1
  37.9 7.1 %all-to-all-start.1 = ((bf16[64,2,64,128]{3,2,1,0:T(8,128)(2,1)}), bf16[64,2,64,128]{3,2,1,0:T(8,128)(2,1)S(1)}, u32[]{:S(2)}, u32[]{:S(2)}) async-start(bf16[64,2,64,128]{3,2,1,0:T(8,128)(2,1)} %broadcast_select_fusion.1), calls=%async_computation.1 | async-start | bytes 4194304 | tf_op jit(solution)/shard_map/all_to_all | solution.py:47
  45.1 10.1 %convert_bitcast_fusion = bf16[16,16,128,128]{2,3,0,1:T(8,128)(2,1)} fusion(bf16[16,512,128]{2,1,0:T(8,128)(2,1)} %param.8, f32[512]{0:T(512)S(1)} %copy-done.3), kind=kOutput, calls=%fused_computation.8 | convolution fusion | flops 4302307328 | bytes 10487808 | tf_op jit(solution)/shard_map/anx,bny->abxy/dot_general | solution.py:56
  55.2 12.3 %copy.36 = bf16[16,16,128,128]{3,2,1,0:T(8,128)(2,1)} copy(bf16[16,16,128,128]{2,3,0,1:T(8,128)(2,1)} %convert_bitcast_fusion) | data formatting | bytes 16777216 | tf_op jit(solution)/shard_map/convert_element_type | solution.py:58
  67.5 9.8 %fusion.12 = bf16[8,8,128,128]{3,1,2,0:T(8,128)(2,1)} fusion(bf16[32,8,128,128]{3,2,1,0:T(8,128)(2,1)} %bitcast.100, s32[128]{0:T(128)S(1)} %get-tuple-element.10, s32[128]{0:T(128)S(1)} %get-tuple-element.9), kind=kOutput, calls=%fused_computation.23 | convolution fusion | flops 542171136 | bytes 10486784 | tf_op jit(solution)/shard_map/dot_general | solution.py:66
  77.3 3.5 %copy.51 = bf16[8,8,128,128]{3,2,1,0:T(8,128)(2,1)} copy(bf16[8,8,128,128]{3,1,2,0:T(8,128)(2,1)} %fusion.12) | data formatting | bytes 4194304
  80.8 13.5 %all-to-all-done.1 = bf16[64,2,64,128]{3,2,1,0:T(8,128)(2,1)S(1)} async-done(((bf16[64,2,64,128]{3,2,1,0:T(8,128)(2,1)}), bf16[64,2,64,128]{3,2,1,0:T(8,128)(2,1)S(1)}, u32[]{:S(2)}, u32[]{:S(2)}) %all-to-all-start.1) | async-done | bytes 2097184 | tf_op jit(solution)/shard_map/all_to_all | solution.py:47
  94.3 1.3 copy-done
  95.6 1.8 pad_maximum_fusion
  97.4 9.5 %all-to-all-start.2 = ((bf16[64,128,128]{2,1,0:T(8,128)(2,1)}), bf16[64,128,128]{2,1,0:T(8,128)(2,1)}, u32[]{:S(2)}, u32[]{:S(2)}) async-start(bf16[64,128,128]{2,1,0:T(8,128)(2,1)} %bitcast.102), calls=%async_computation.2 | async-start | bytes 4194304 | tf_op jit(solution)/shard_map/all_to_all | solution.py:72
  107.2 48.3 %all-to-all-done.2 = bf16[64,128,128]{2,1,0:T(8,128)(2,1)} async-done(((bf16[64,128,128]{2,1,0:T(8,128)(2,1)}), bf16[64,128,128]{2,1,0:T(8,128)(2,1)}, u32[]{:S(2)}, u32[]{:S(2)}) %all-to-all-start.2) | async-done | bytes 2097184 | tf_op jit(solution)/shard_map/all_to_all | solution.py:72
  155.5 2.8 fusion.15
  160.6 2.1 gather_fusion.1
  162.8 30.1 %all-gather.2.cloned.1.call-done = bf16[128,128,128]{2,1,0:T(8,128)(2,1)} async-done(((bf16[16,128,128]{2,1,0:T(8,128)(2,1)}), bf16[128,128,128]{2,1,0:T(8,128)(2,1)}) %all-gather.2.cloned.1.call-update) | async-done | bytes 4194320 | tf_op jit(solution)/shard_map/all_gather | solution.py:81
  192.9 5.8 %fusion.34 = f32[128,64,128]{2,1,0:T(8,128)S(1)} fusion(bf16[128,64,128]{2,1,0:T(8,128)(2,1)} %gather_fusion.1, bf16[128,128,128]{2,1,0:T(8,128)(2,1)} %all-gather.2.cloned.1.call-done), kind=kOutput, calls=%fused_computation.62 | convolution fusion | flops 268435456 | bytes 10485760 | tf_op jit(solution)/shard_map/kvb,kab->kva/dot_general | solution.py:88
  198.7 3.8 %fusion.4 = f32[8,64,128]{2,0,1:T(8,128)S(1)} fusion(f32[128,64,128]{2,1,0:T(8,128)S(1)} %fusion.34, s32[128]{0:T(128)S(1)} %slice_bitcast_fusion.3), kind=kOutput, calls=%fused_computation.11 | convolution fusion | flops 100664320 | bytes 4456960 | tf_op jit(solution)/shard_map/ki,kva->iva/dot_general | solution.py:94
  202.6 1.0 gather_fusion.2
  203.8 63.4 %all_to_all.27 = bf16[64,2,64,128]{3,2,1,0:T(8,128)(2,1)S(1)} all-to-all(bf16[64,2,64,128]{3,2,1,0:T(8,128)(2,1)S(1)} %broadcast_select_fusion), channel_id=1, replica_groups=mesh['rows'=64,'cols'=8] {'rows'}, dimensions={0} | all-to-all | bytes 4194304 | tf_op jit(solution)/shard_map/all_to_all | solution.py:47
  267.4 2.1 gather_fusion.3
  269.5 5.8 %fusion.35 = f32[128,64,128]{2,1,0:T(8,128)S(1)} fusion(bf16[128,64,128]{2,1,0:T(8,128)(2,1)} %gather_fusion.3, bf16[128,128,128]{2,1,0:T(8,128)(2,1)} %all-gather.2.cloned.1.call-done), kind=kOutput, calls=%fused_computation.63 | convolution fusion | flops 268435456 | bytes 10485760 | tf_op jit(solution)/shard_map/kvb,kab->kva/dot_general | solution.py:88
  275.3 3.8 %fusion.2 = f32[8,64,128]{2,0,1:T(8,128)S(1)} fusion(f32[128,64,128]{2,1,0:T(8,128)S(1)} %fusion.35, s32[128]{0:T(128)S(1)} %slice_bitcast_fusion.3), kind=kOutput, calls=%fused_computation.9 | convolution fusion | flops 100664320 | bytes 4456960 | tf_op jit(solution)/shard_map/ki,kva->iva/dot_general | solution.py:94
  (35 shorter events, 6.3 us)
Async XLA Ops:
  9.5 25.4 %all-to-all-start = ((s32[64,1,3]{2,1,0:T(1,128)}), s32[64,1,3]{2,1,0:T(1,128)S(1)}, u32[]{:S(2)}, u32[]{:S(2)}) async-start(s32[64,1,3]{2,1,0:T(1,128)} %copy.38), calls=%async_computation | async-start | bytes 65536 | tf_op jit(solution)/shard_map/all_to_all | solution.py:27
  37.9 7.2 %copy-start.3 = (f32[512]{0:T(512)S(1)}, f32[512]{0:T(512)}, u32[]{:S(2)}) copy-start(f32[512]{0:T(512)} %param.9) | copy-start | bytes 6148
  37.9 56.3 %all-to-all-start.1 = ((bf16[64,2,64,128]{3,2,1,0:T(8,128)(2,1)}), bf16[64,2,64,128]{3,2,1,0:T(8,128)(2,1)S(1)}, u32[]{:S(2)}, u32[]{:S(2)}) async-start(bf16[64,2,64,128]{3,2,1,0:T(8,128)(2,1)} %broadcast_select_fusion.1), calls=%async_computation.1 | async-start | bytes 4194304 | tf_op jit(solution)/shard_map/all_to_all | solution.py:47
  94.3 1.3 copy-start
  97.4 58.1 %all-to-all-start.2 = ((bf16[64,128,128]{2,1,0:T(8,128)(2,1)}), bf16[64,128,128]{2,1,0:T(8,128)(2,1)}, u32[]{:S(2)}, u32[]{:S(2)}) async-start(bf16[64,128,128]{2,1,0:T(8,128)(2,1)} %bitcast.102), calls=%async_computation.2 | async-start | bytes 4194304 | tf_op jit(solution)/shard_map/all_to_all | solution.py:72
  106.9 86.0 %all-gather.2.cloned.1.call-start = ((), (), s32[]{:S(2)}) async-start(), calls=%async_computation.4 | async-start | bytes 4718592 | tf_op jit(solution)/shard_map/all_gather | solution.py:81
  155.5 5.1 %copy-start.4 = (s32[1,128,2]{1,2,0:T(2,128)S(1)}, s32[1,128,2]{1,2,0:T(2,128)}, u32[]{:S(2)}) copy-start(s32[1,128,2]{1,2,0:T(2,128)} %param.11) | copy-start | bytes 3076
  198.7 3.8 %copy-start.1 = (f32[64,1024]{1,0:T(8,128)S(1)}, f32[64,1024]{1,0:T(8,128)}, u32[]{:S(2)}) copy-start(f32[64,1024]{1,0:T(8,128)} %param.13) | copy-start | bytes 786436
  202.6 76.6 %copy-start.2 = (f32[64,1024]{1,0:T(8,128)}, f32[64,1024]{1,0:T(8,128)S(1)}, u32[]{:S(2)}) copy-start(f32[64,1024]{1,0:T(8,128)S(1)} %get-tuple-element.7) | copy-start | bytes 786436
Sparse Core Ops, SparseCore 0:
  159.4 33.4 all-gather.1

commit v3 on v1

--- a/solution.py
+++ b/solution.py
@@ -1,7 +1,50 @@
 import jax
 import jax.numpy as jnp
 from jax import lax
+from jax.experimental import pallas as pl
+from jax.experimental.pallas import tpu as pltpu
 from jax.sharding import PartitionSpec as P
+
+
+def presum_kernel(index_ref, basis_ref, weighted_ref, out_ref, acc_ref):
+    acc_ref[...] = jnp.zeros_like(acc_ref)
+
+    def body(s, carry):
+        target = index_ref[4 * s]
+        left = index_ref[4 * s + 2]
+        right = index_ref[4 * s + 3]
+        tile = lax.dot_general(
+            basis_ref[left],
+            weighted_ref[right],
+            (((0,), (0,)), ((), ())),
+            preferred_element_type=jnp.float32,
+        )
+        acc_ref[target] += tile.astype(jnp.bfloat16).astype(jnp.float32)
+        return carry
+
+    lax.fori_loop(0, index_ref.shape[0] // 4, body, 0)
+    out_ref[...] = acc_ref[...].astype(out_ref.dtype)
+
+
+def presum_tiles(index_flat, basis, weighted, n_rows):
+    blocks, points, block_size = basis.shape
+    contribs = index_flat.shape[0] // 4
+    return pl.pallas_call(
+        presum_kernel,
+        out_shape=jax.ShapeDtypeStruct((n_rows, block_size, block_size), jnp.bfloat16),
+        in_specs=[
+            pl.BlockSpec(memory_space=pltpu.SMEM),
+            pl.BlockSpec(memory_space=pltpu.VMEM),
+            pl.BlockSpec(memory_space=pltpu.VMEM),
+        ],
+        out_specs=pl.BlockSpec(memory_space=pltpu.VMEM),
+        scratch_shapes=[pltpu.VMEM((n_rows, block_size, block_size), jnp.float32)],
+        cost_estimate=pl.CostEstimate(
+            flops=2 * contribs * points * block_size * block_size,
+            transcendentals=0,
+            bytes_accessed=2 * basis.size * 2 + n_rows * block_size * block_size * 2,
+        ),
+    )(index_flat, basis, weighted)
 
 
 def on_device(
@@ -15,7 +58,6 @@
     group_slots = pattern.shape[1]
     slot_count = group_slots // n_cols
     ghost_width = ghost_list.shape[2]
-    pair_count = basis_blocks * basis_blocks
 
     ghost_ids = ghost_list[0]
     owners = jnp.arange(n_rows, dtype=jnp.int32)[:, None] * row_blocks
@@ -49,26 +91,11 @@
             [blocks, arrived.reshape(n_rows * ghost_width, vec_count, block_size)], axis=0
         )
 
-    state_blocks = own_blocks(state)
-    state_pool = with_ghosts(state_blocks)
-
     weighted = (basis_values.astype(jnp.float32) * potential[None, :, None]).astype(jnp.bfloat16)
-    pair_tiles = jnp.einsum(
-        "anx,bny->abxy", basis_values, weighted, preferred_element_type=jnp.float32
-    ).astype(jnp.bfloat16)
-    pair_id = contrib_index[:, 2] * basis_blocks + contrib_index[:, 3]
-    pair_hot = (pair_id[:, None] == jnp.arange(pair_count, dtype=jnp.int32)[None, :]).astype(
-        jnp.bfloat16
-    )
-    counts = jnp.dot(
-        to_target.astype(jnp.bfloat16).T, pair_hot, preferred_element_type=jnp.float32
-    ).astype(jnp.bfloat16)
-    send_tiles = jnp.dot(
-        counts,
-        pair_tiles.reshape(pair_count, block_size * block_size),
-        preferred_element_type=jnp.float32,
-    ).astype(jnp.bfloat16).reshape(n_rows, block_size, block_size)
+    send_tiles = presum_tiles(contrib_index.reshape(-1), basis_values, weighted, n_rows)
     arrived_tiles = lax.all_to_all(send_tiles, "rows", split_axis=0, concat_axis=0, tiled=True)
+    arrived_tiles, state_in = lax.optimization_barrier((arrived_tiles, state))
+    state_pool = with_ghosts(own_blocks(state_in))
     slot_wanted = jnp.arange(slot_count, dtype=jnp.int32)
     selector = (arrived_slots[None, :] == slot_wanted[:, None]).astype(jnp.bfloat16)
     assembled = jnp.dot(

time: 281 us -> 286 us (1.018)
  Pallas kernels: 0 us -> 33.8 us
  matrix products: 39 us -> 20.4 us
  local copies, waits for them, and re-layouts: 23.8 us -> 11.8 us
    pallas_call x0 -> x1, Pallas kernels: none -> 33.8 us  [presum_tiles(): pl.pallas_call(presum_kernel, out_shape=jax.ShapeDtypeStruct((n_rows, blo...]
    dot_general x2 -> x0, matrix products: 18.6 us -> none  [the longest x1 10.1 us: on_device(): jnp.einsum('anx,bny->abxy', basis_values, weighted, preferred_element_typ...]
    convert_element_type x1 -> x0, local copies, waits for them, and re-layouts: 12.3 us -> none  [on_device(): pair_tiles = jnp.einsum('anx,bny->abxy', basis_values, weighted, preferre...]
    convert_element_type x0 -> x1, other arithmetic: none -> 3.55 us  [on_device(): (basis_values.astype(jnp.float32) * potential[None, :, None]).astype(jnp....]
  transfers between devices with their start and end apart: 4 -> 4, of which waited for: 2 -> 2; matrix products, arithmetic and copies ran while one was open for 14% -> 4% of each run, Pallas kernels for 0% -> 12%
where the time goes in v3:
time: 286 us; the launch traced here: 284 us
  waiting for transfers between devices  96.7 us (34%)
  blocking collectives  55.9 us (20%)
  starting transfers between devices  40.3 us (14%)
  Pallas kernels  33.8 us (12%)
  matrix products  20.4 us (7%)
  between operations  15.5 us (5%)
  local copies, waits for them, and re-layouts  11.8 us (4%)
  other arithmetic  9.01 us (3%)
    all_to_all x1, blocking collectives, with_ghosts(): lax.all_to_all(outgoing, 'rows', split_axis=0, concat_axis=0, tiled=True)  55.9 us
    all_to_all x1, waiting for transfers between devices, on_device(): lax.all_to_all(send_tiles, 'rows', split_axis=0, concat_axis=0, tiled=True)  49.3 us
    all_to_all x1, waiting for transfers between devices, with_ghosts(): lax.all_to_all(outgoing, 'rows', split_axis=0, concat_axis=0, tiled=True)  47.4 us
    pallas_call x1, Pallas kernels, presum_tiles(): pl.pallas_call(presum_kernel, out_shape=jax.ShapeDtypeStruct((n_rows, blo...  33.8 us
    all_to_all x1, starting transfers between devices, on_device(): lax.all_to_all(index_send, 'rows', split_axis=0, concat_axis=0, tiled=True)  15.9 us
    all_to_all x1, starting transfers between devices, on_device(): lax.all_to_all(send_tiles, 'rows', split_axis=0, concat_axis=0, tiled=True)  12.7 us
    all_to_all x1, starting transfers between devices, with_ghosts(): lax.all_to_all(outgoing, 'rows', split_axis=0, concat_axis=0, tiled=True)  11.7 us
    dot_general x2, matrix products, accumulate(): jnp.einsum('kvb,kab->kva', operands, tile_part, preferred_element_type=jn...  11.6 us
  transfers between devices with their start and end apart: 4, of which 2 were waited for; matrix products, arithmetic and copies ran while one was open for 4% of the time, Pallas kernels for 12%

profile of v3, /device:TPU:56, one launch (start us, length us, event | category | flops | bytes accessed | tf_op | source)
XLA Modules:
  0.0 283.6 jit_solution(16162665475247899759)
XLA Ops:
  7.2 0.8 slice_bitcast_fusion.2
  9.5 15.9 %all-to-all-start.1 = ((s32[64,1,3]{2,1,0:T(1,128)}), s32[64,1,3]{2,1,0:T(1,128)S(1)}, u32[]{:S(2)}, u32[]{:S(2)}) async-start(s32[64,1,3]{2,1,0:T(1,128)} %copy.33), calls=%async_computation.1 | async-start | bytes 65536 | tf_op jit(solution)/shard_map/all_to_all | solution.py:69
  25.4 0.8 copy.31
  26.8 3.6 %multiply_convert_fusion.weighted_ref = bf16[16,512,128]{2,1,0:T(8,128)(2,1)} fusion(bf16[16,512,128]{2,1,0:T(8,128)(2,1)} %basis_ref.1, f32[512]{0:T(512)} %param.9), kind=kLoop, calls=%fused_computation.9 | loop fusion | flops 3145728 | bytes 4196352 | tf_op jit(solution)/shard_map/convert_element_type | solution.py:94
  30.4 33.8 %shard_map.95 = bf16[64,128,128]{2,1,0:T(8,128)(2,1)} custom-call(s32[512]{0:T(512)} %reshape.76.index_ref, bf16[16,512,128]{2,1,0:T(8,128)(2,1)} %basis_ref.1, bf16[16,512,128]{2,1,0:T(8,128)(2,1)} %multiply_convert_fusion.weighted_ref), custom_call_target="tpu_custom_call" | custom-call | flops 2147483648 | bytes 6291456 | tf_op jit(solution)/shard_map/pallas_call | solution.py:32
  64.3 12.7 %all-to-all-start = ((bf16[64,128,128]{2,1,0:T(8,128)(2,1)}), bf16[64,128,128]{2,1,0:T(8,128)(2,1)S(1)}, u32[]{:S(2)}, u32[]{:S(2)}) async-start(bf16[64,128,128]{2,1,0:T(8,128)(2,1)} %shard_map.95), calls=%async_computation | async-start | bytes 4194304 | tf_op jit(solution)/shard_map/all_to_all | solution.py:96
  77.1 49.3 %all-to-all-done = bf16[64,128,128]{2,1,0:T(8,128)(2,1)S(1)} async-done(((bf16[64,128,128]{2,1,0:T(8,128)(2,1)}), bf16[64,128,128]{2,1,0:T(8,128)(2,1)S(1)}, u32[]{:S(2)}, u32[]{:S(2)}) %all-to-all-start) | async-done | bytes 2097184 | tf_op jit(solution)/shard_map/all_to_all | solution.py:96
  126.3 1.2 fusion.6
  127.6 0.9 copy.43
  128.9 1.0 gather_fusion
  129.9 1.5 broadcast_select_fusion.1
  131.4 11.7 %all-to-all-start.2 = ((bf16[64,2,64,128]{3,2,1,0:T(8,128)(2,1)}), bf16[64,2,64,128]{3,2,1,0:T(8,128)(2,1)S(1)}, u32[]{:S(2)}, u32[]{:S(2)}) async-start(bf16[64,2,64,128]{3,2,1,0:T(8,128)(2,1)} %broadcast_select_fusion.1), calls=%async_computation.2 | async-start | bytes 4194304 | tf_op jit(solution)/shard_map/all_to_all | solution.py:89
  144.5 47.4 %all-to-all-done.2 = bf16[64,2,64,128]{3,2,1,0:T(8,128)(2,1)S(1)} async-done(((bf16[64,2,64,128]{3,2,1,0:T(8,128)(2,1)}), bf16[64,2,64,128]{3,2,1,0:T(8,128)(2,1)S(1)}, u32[]{:S(2)}, u32[]{:S(2)}) %all-to-all-start.2) | async-done | bytes 2097184 | tf_op jit(solution)/shard_map/all_to_all | solution.py:89
  191.9 1.3 copy-done
  193.3 1.8 pad_maximum_fusion
  195.1 2.1 gather_fusion.1
  197.2 5.8 %fusion.21 = f32[128,64,128]{2,1,0:T(8,128)S(1)} fusion(bf16[128,64,128]{2,1,0:T(8,128)(2,1)} %gather_fusion.1, bf16[128,128,128]{2,1,0:T(8,128)(2,1)} %all-gather.2.cloned.1.call-done), kind=kOutput, calls=%fused_computation.49 | convolution fusion | flops 268435456 | bytes 10485760 | tf_op jit(solution)/shard_map/kvb,kab->kva/dot_general | solution.py:114
  203.0 3.8 %fusion.2 = f32[8,64,128]{2,0,1:T(8,128)S(1)} fusion(f32[128,64,128]{2,1,0:T(8,128)S(1)} %fusion.21, s32[128]{0:T(128)S(1)} %slice_bitcast_fusion.3), kind=kOutput, calls=%fused_computation.7 | convolution fusion | flops 100664320 | bytes 4456960 | tf_op jit(solution)/shard_map/ki,kva->iva/dot_general | solution.py:120
  206.9 1.0 gather_fusion.2
  208.1 55.9 %all_to_all.27 = bf16[64,2,64,128]{3,2,1,0:T(8,128)(2,1)S(1)} all-to-all(bf16[64,2,64,128]{3,2,1,0:T(8,128)(2,1)S(1)} %broadcast_select_fusion), channel_id=1, replica_groups=mesh['rows'=64,'cols'=8] {'rows'}, dimensions={0} | all-to-all | bytes 4194304 | tf_op jit(solution)/shard_map/all_to_all | solution.py:89
  264.2 2.1 gather_fusion.3
  266.3 5.8 %fusion.22 = f32[128,64,128]{2,1,0:T(8,128)S(1)} fusion(bf16[128,64,128]{2,1,0:T(8,128)(2,1)} %gather_fusion.3, bf16[128,128,128]{2,1,0:T(8,128)(2,1)} %all-gather.2.cloned.1.call-done), kind=kOutput, calls=%fused_computation.50 | convolution fusion | flops 268435456 | bytes 10485760 | tf_op jit(solution)/shard_map/kvb,kab->kva/dot_general | solution.py:114
  272.1 3.8 %fusion = f32[8,64,128]{2,0,1:T(8,128)S(1)} fusion(f32[128,64,128]{2,1,0:T(8,128)S(1)} %fusion.22, s32[128]{0:T(128)S(1)} %slice_bitcast_fusion.3), kind=kOutput, calls=%fused_computation.5 | convolution fusion | flops 100664320 | bytes 4456960 | tf_op jit(solution)/shard_map/ki,kva->iva/dot_general | solution.py:120
  275.9 0.8 fusion.11
  (33 shorter events, 3.3 us)
Async XLA Ops:
  9.5 54.8 %all-to-all-start.1 = ((s32[64,1,3]{2,1,0:T(1,128)}), s32[64,1,3]{2,1,0:T(1,128)S(1)}, u32[]{:S(2)}, u32[]{:S(2)}) async-start(s32[64,1,3]{2,1,0:T(1,128)} %copy.33), calls=%async_computation.1 | async-start | bytes 65536 | tf_op jit(solution)/shard_map/all_to_all | solution.py:69
  64.3 62.1 %all-to-all-start = ((bf16[64,128,128]{2,1,0:T(8,128)(2,1)}), bf16[64,128,128]{2,1,0:T(8,128)(2,1)S(1)}, u32[]{:S(2)}, u32[]{:S(2)}) async-start(bf16[64,128,128]{2,1,0:T(8,128)(2,1)} %shard_map.95), calls=%async_computation | async-start | bytes 4194304 | tf_op jit(solution)/shard_map/all_to_all | solution.py:96
  77.0 120.2 %all-gather.2.cloned.1.call-start = ((), (), s32[]{:S(2)}) async-start(), calls=%async_computation.4 | async-start | bytes 4718592 | tf_op jit(solution)/shard_map/all_gather | solution.py:107
  126.3 2.6 copy-start.1
  131.4 13.0 %copy-start.3 = (s32[1,128,2]{1,2,0:T(2,128)S(1)}, s32[1,128,2]{1,2,0:T(2,128)}, u32[]{:S(2)}) copy-start(s32[1,128,2]{1,2,0:T(2,128)} %param.11) | copy-start | bytes 3076
  131.4 60.5 %all-to-all-start.2 = ((bf16[64,2,64,128]{3,2,1,0:T(8,128)(2,1)}), bf16[64,2,64,128]{3,2,1,0:T(8,128)(2,1)S(1)}, u32[]{:S(2)}, u32[]{:S(2)}) async-start(bf16[64,2,64,128]{3,2,1,0:T(8,128)(2,1)} %broadcast_select_fusion.1), calls=%async_computation.2 | async-start | bytes 4194304 | tf_op jit(solution)/shard_map/all_to_all | solution.py:89
  191.9 1.3 copy-start
  206.9 69.1 %copy-start.2 = (f32[64,1024]{1,0:T(8,128)}, f32[64,1024]{1,0:T(8,128)S(1)}, u32[]{:S(2)}) copy-start(f32[64,1024]{1,0:T(8,128)S(1)} %get-tuple-element.7) | copy-start | bytes 786436
Sparse Core Ops, SparseCore 0:
  128.6 37.0 all-gather.1

commit v4 on v3

--- a/solution.py
+++ b/solution.py
@@ -6,20 +6,19 @@
 from jax.sharding import PartitionSpec as P
 
 
-def presum_kernel(index_ref, basis_ref, weighted_ref, out_ref, acc_ref):
+def presum_kernel(index_ref, stacked_ref, basis_ref, out_ref, tiles_ref, acc_ref):
+    blocks, block_size = basis_ref.shape[0], basis_ref.shape[2]
+    for left in range(blocks):
+        product = jnp.dot(stacked_ref[...], basis_ref[left], preferred_element_type=jnp.float32)
+        for right in range(blocks):
+            tiles_ref[left, right] = product[right * block_size : (right + 1) * block_size].astype(
+                jnp.bfloat16
+            )
     acc_ref[...] = jnp.zeros_like(acc_ref)
 
     def body(s, carry):
         target = index_ref[4 * s]
-        left = index_ref[4 * s + 2]
-        right = index_ref[4 * s + 3]
-        tile = lax.dot_general(
-            basis_ref[left],
-            weighted_ref[right],
-            (((0,), (0,)), ((), ())),
-            preferred_element_type=jnp.float32,
-        )
-        acc_ref[target] += tile.astype(jnp.bfloat16).astype(jnp.float32)
+        acc_ref[target] += tiles_ref[index_ref[4 * s + 2], index_ref[4 * s + 3]].astype(jnp.float32)
         return carry
 
     lax.fori_loop(0, index_ref.shape[0] // 4, body, 0)
@@ -28,7 +27,7 @@
 
 def presum_tiles(index_flat, basis, weighted, n_rows):
     blocks, points, block_size = basis.shape
-    contribs = index_flat.shape[0] // 4
+    stacked = weighted.transpose(0, 2, 1).reshape(blocks * block_size, points)
     return pl.pallas_call(
         presum_kernel,
         out_shape=jax.ShapeDtypeStruct((n_rows, block_size, block_size), jnp.bfloat16),
@@ -38,13 +37,16 @@
             pl.BlockSpec(memory_space=pltpu.VMEM),
         ],
         out_specs=pl.BlockSpec(memory_space=pltpu.VMEM),
-        scratch_shapes=[pltpu.VMEM((n_rows, block_size, block_size), jnp.float32)],
+        scratch_shapes=[
+            pltpu.VMEM((blocks, blocks, block_size, block_size), jnp.bfloat16),
+            pltpu.VMEM((n_rows, block_size, block_size), jnp.float32),
+        ],
         cost_estimate=pl.CostEstimate(
-            flops=2 * contribs * points * block_size * block_size,
+            flops=2 * blocks * blocks * points * block_size * block_size,
             transcendentals=0,
             bytes_accessed=2 * basis.size * 2 + n_rows * block_size * block_size * 2,
         ),
-    )(index_flat, basis, weighted)
+    )(index_flat, stacked, basis)
 
 
 def on_device(
@@ -112,7 +114,7 @@
     def accumulate(tile_part, source_part, row_part, operand_pool):
         operands = operand_pool[source_part]
         products = jnp.einsum(
-            "kvb,kab->kva", operands, tile_part, preferred_element_type=jnp.float32
+            "kvb,kba->kva", operands, tile_part, preferred_element_type=jnp.float32
         )
         row_select = (row_part[:, None] == jnp.arange(row_blocks, dtype=jnp.int32)[None, :]).astype(
             jnp.float32

time: 286 us -> 265 us (0.927)
  Pallas kernels: 33.8 us -> 14.6 us
  matrix products: 20.4 us -> 17 us
    pallas_call x1, Pallas kernels: 33.8 us -> 14.6 us  [presum_tiles(): pl.pallas_call(presum_kernel, out_shape=jax.ShapeDtypeStruct((n_rows, blo...]
    convert_element_type x1 -> x0, other arithmetic: 3.55 us -> none  [on_device(): (basis_values.astype(jnp.float32) * potential[None, :, None]).astype(jnp....]
    dot_general x2, matrix products: 11.6 us -> 8.09 us  [accumulate(): jnp.einsum('kvb,kba->kva', operands, tile_part, preferred_element_type=jn...]
  transfers between devices with their start and end apart: 4 -> 4, of which waited for: 2 -> 2; matrix products, arithmetic and copies ran while one was open for 4% -> 5% of each run, Pallas kernels for 12% -> 6%
where the time goes in v4:
time: 265 us; the launch traced here: 262 us
  waiting for transfers between devices  96.5 us (36%)
  blocking collectives  55.9 us (21%)
  starting transfers between devices  40.5 us (15%)
  matrix products  17 us (6%)
  between operations  15.5 us (6%)
  Pallas kernels  14.6 us (6%)
  local copies, waits for them, and re-layouts  14.4 us (5%)
  other arithmetic  7.67 us (3%)
    all_to_all x1, blocking collectives, with_ghosts(): lax.all_to_all(outgoing, 'rows', split_axis=0, concat_axis=0, tiled=True)  55.9 us
    all_to_all x1, waiting for transfers between devices, on_device(): lax.all_to_all(send_tiles, 'rows', split_axis=0, concat_axis=0, tiled=True)  49.1 us
    all_to_all x1, waiting for transfers between devices, with_ghosts(): lax.all_to_all(outgoing, 'rows', split_axis=0, concat_axis=0, tiled=True)  47.4 us
    all_to_all x1, starting transfers between devices, on_device(): lax.all_to_all(index_send, 'rows', split_axis=0, concat_axis=0, tiled=True)  15.9 us
    pallas_call x1, Pallas kernels, presum_tiles(): pl.pallas_call(presum_kernel, out_shape=jax.ShapeDtypeStruct((n_rows, blo...  14.6 us
    all_to_all x1, starting transfers between devices, on_device(): lax.all_to_all(send_tiles, 'rows', split_axis=0, concat_axis=0, tiled=True)  12.7 us
    all_to_all x1, starting transfers between devices, with_ghosts(): lax.all_to_all(outgoing, 'rows', split_axis=0, concat_axis=0, tiled=True)  11.7 us
    dot_general x2, matrix products, accumulate(): jnp.einsum('kvb,kba->kva', operands, tile_part, preferred_element_type=jn...  8.09 us
  transfers between devices with their start and end apart: 4, of which 2 were waited for; matrix products, arithmetic and copies ran while one was open for 5% of the time, Pallas kernels for 6%

profile of v4, /device:TPU:56, one launch (start us, length us, event | category | flops | bytes accessed | tf_op | source)
XLA Modules:
  0.0 262.0 jit_solution(10914689570889633236)
XLA Ops:
  9.5 15.9 %all-to-all-start.1 = ((s32[64,1,3]{2,1,0:T(1,128)}), s32[64,1,3]{2,1,0:T(1,128)S(1)}, u32[]{:S(2)}, u32[]{:S(2)}) async-start(s32[64,1,3]{2,1,0:T(1,128)} %copy.38), calls=%async_computation.1 | async-start | bytes 65536 | tf_op jit(solution)/shard_map/all_to_all | solution.py:71
  25.4 0.8 copy.35
  26.8 2.2 fusion.4
  29.1 2.6 copy.36
  31.7 14.6 %shard_map.95 = bf16[64,128,128]{2,1,0:T(8,128)(2,1)} custom-call(s32[512]{0:T(512)} %reshape.79.index_ref, bf16[2048,512]{1,0:T(8,128)(2,1)} %bitcast.86, bf16[16,512,128]{2,1,0:T(8,128)(2,1)} %basis_ref.1), custom_call_target="tpu_custom_call" | custom-call | flops 4294967296 | bytes 6291456 | tf_op jit(solution)/shard_map/pallas_call | solution.py:31
  46.3 12.7 %all-to-all-start = ((bf16[64,128,128]{2,1,0:T(8,128)(2,1)}), bf16[64,128,128]{2,1,0:T(8,128)(2,1)S(1)}, u32[]{:S(2)}, u32[]{:S(2)}) async-start(bf16[64,128,128]{2,1,0:T(8,128)(2,1)} %shard_map.95), calls=%async_computation | async-start | bytes 4194304 | tf_op jit(solution)/shard_map/all_to_all | solution.py:98
  59.3 49.1 %all-to-all-done = bf16[64,128,128]{2,1,0:T(8,128)(2,1)S(1)} async-done(((bf16[64,128,128]{2,1,0:T(8,128)(2,1)}), bf16[64,128,128]{2,1,0:T(8,128)(2,1)S(1)}, u32[]{:S(2)}, u32[]{:S(2)}) %all-to-all-start) | async-done | bytes 2097184 | tf_op jit(solution)/shard_map/all_to_all | solution.py:98
  108.4 1.2 fusion.7
  109.6 0.9 copy.48
  111.0 1.0 gather_fusion
  111.9 1.5 broadcast_select_fusion.1
  113.5 11.7 %all-to-all-start.2 = ((bf16[64,2,64,128]{3,2,1,0:T(8,128)(2,1)}), bf16[64,2,64,128]{3,2,1,0:T(8,128)(2,1)S(1)}, u32[]{:S(2)}, u32[]{:S(2)}) async-start(bf16[64,2,64,128]{3,2,1,0:T(8,128)(2,1)} %broadcast_select_fusion.1), calls=%async_computation.2 | async-start | bytes 4194304 | tf_op jit(solution)/shard_map/all_to_all | solution.py:91
  126.5 47.4 %all-to-all-done.2 = bf16[64,2,64,128]{3,2,1,0:T(8,128)(2,1)S(1)} async-done(((bf16[64,2,64,128]{3,2,1,0:T(8,128)(2,1)}), bf16[64,2,64,128]{3,2,1,0:T(8,128)(2,1)S(1)}, u32[]{:S(2)}, u32[]{:S(2)}) %all-to-all-start.2) | async-done | bytes 2097184 | tf_op jit(solution)/shard_map/all_to_all | solution.py:91
  173.9 1.3 copy-done
  175.3 1.8 pad_maximum_fusion
  177.0 2.1 gather_fusion.1
  179.2 4.0 %fusion.22 = f32[128,64,128]{2,1,0:T(8,128)S(1)} fusion(bf16[128,64,128]{2,1,0:T(8,128)(2,1)} %gather_fusion.1, bf16[128,128,128]{2,1,0:T(8,128)(2,1)} %all-gather.2.cloned.1.call-done), kind=kOutput, calls=%fused_computation.50 | convolution fusion | flops 268435456 | bytes 10485760 | tf_op jit(solution)/shard_map/kvb,kba->kva/dot_general | solution.py:116
  183.2 3.8 %fusion.2 = f32[8,64,128]{2,0,1:T(8,128)S(1)} fusion(f32[128,64,128]{2,1,0:T(8,128)S(1)} %fusion.22, s32[128]{0:T(128)S(1)} %slice_bitcast_fusion.3), kind=kOutput, calls=%fused_computation.7 | convolution fusion | flops 100664320 | bytes 4456960 | tf_op jit(solution)/shard_map/ki,kva->iva/dot_general | solution.py:122
  187.2 1.0 gather_fusion.2
  188.3 55.9 %all_to_all.27 = bf16[64,2,64,128]{3,2,1,0:T(8,128)(2,1)S(1)} all-to-all(bf16[64,2,64,128]{3,2,1,0:T(8,128)(2,1)S(1)} %broadcast_select_fusion), channel_id=1, replica_groups=mesh['rows'=64,'cols'=8] {'rows'}, dimensions={0} | all-to-all | bytes 4194304 | tf_op jit(solution)/shard_map/all_to_all | solution.py:91
  244.4 2.1 gather_fusion.3
  246.5 4.0 %fusion.23 = f32[128,64,128]{2,1,0:T(8,128)S(1)} fusion(bf16[128,64,128]{2,1,0:T(8,128)(2,1)} %gather_fusion.3, bf16[128,128,128]{2,1,0:T(8,128)(2,1)} %all-gather.2.cloned.1.call-done), kind=kOutput, calls=%fused_computation.51 | convolution fusion | flops 268435456 | bytes 10485760 | tf_op jit(solution)/shard_map/kvb,kba->kva/dot_general | solution.py:116
  250.6 3.8 %fusion = f32[8,64,128]{2,0,1:T(8,128)S(1)} fusion(f32[128,64,128]{2,1,0:T(8,128)S(1)} %fusion.23, s32[128]{0:T(128)S(1)} %slice_bitcast_fusion.3), kind=kOutput, calls=%fused_computation.5 | convolution fusion | flops 100664320 | bytes 4456960 | tf_op jit(solution)/shard_map/ki,kva->iva/dot_general | solution.py:122
  254.4 0.8 fusion.12
  (34 shorter events, 4.2 us)
Async XLA Ops:
  9.5 36.8 %all-to-all-start.1 = ((s32[64,1,3]{2,1,0:T(1,128)}), s32[64,1,3]{2,1,0:T(1,128)S(1)}, u32[]{:S(2)}, u32[]{:S(2)}) async-start(s32[64,1,3]{2,1,0:T(1,128)} %copy.38), calls=%async_computation.1 | async-start | bytes 65536 | tf_op jit(solution)/shard_map/all_to_all | solution.py:71
  46.3 62.1 %all-to-all-start = ((bf16[64,128,128]{2,1,0:T(8,128)(2,1)}), bf16[64,128,128]{2,1,0:T(8,128)(2,1)S(1)}, u32[]{:S(2)}, u32[]{:S(2)}) async-start(bf16[64,128,128]{2,1,0:T(8,128)(2,1)} %shard_map.95), calls=%async_computation | async-start | bytes 4194304 | tf_op jit(solution)/shard_map/all_to_all | solution.py:98
  59.0 120.2 %all-gather.2.cloned.1.call-start = ((), (), s32[]{:S(2)}) async-start(), calls=%async_computation.4 | async-start | bytes 4718592 | tf_op jit(solution)/shard_map/all_gather | solution.py:109
  108.4 2.6 copy-start.1
  113.5 13.0 %copy-start.3 = (s32[1,128,2]{1,2,0:T(2,128)S(1)}, s32[1,128,2]{1,2,0:T(2,128)}, u32[]{:S(2)}) copy-start(s32[1,128,2]{1,2,0:T(2,128)} %param.11) | copy-start | bytes 3076
  113.5 60.5 %all-to-all-start.2 = ((bf16[64,2,64,128]{3,2,1,0:T(8,128)(2,1)}), bf16[64,2,64,128]{3,2,1,0:T(8,128)(2,1)S(1)}, u32[]{:S(2)}, u32[]{:S(2)}) async-start(bf16[64,2,64,128]{3,2,1,0:T(8,128)(2,1)} %broadcast_select_fusion.1), calls=%async_computation.2 | async-start | bytes 4194304 | tf_op jit(solution)/shard_map/all_to_all | solution.py:91
  173.9 1.3 copy-start
  187.1 67.3 %copy-start.2 = (f32[64,1024]{1,0:T(8,128)}, f32[64,1024]{1,0:T(8,128)S(1)}, u32[]{:S(2)}) copy-start(f32[64,1024]{1,0:T(8,128)S(1)} %get-tuple-element.7) | copy-start | bytes 786436
Sparse Core Ops, SparseCore 0:
  110.6 37.0 all-gather.1

commit v5 on v4

--- a/solution.py
+++ b/solution.py
@@ -49,6 +49,46 @@
     )(index_flat, stacked, basis)
 
 
+def product_kernel(pattern_ref, tiles_ref, local_ref, ghost_ref, out_ref, acc_ref):
+    row_blocks, vec_count, block_size = local_ref.shape
+    acc_ref[...] = jnp.zeros_like(acc_ref)
+
+    def body(g, carry):
+        row = pattern_ref[2 * g]
+        source = pattern_ref[2 * g + 1]
+        local = local_ref[jnp.minimum(source, row_blocks - 1)]
+        ghost = ghost_ref[jnp.maximum(source - row_blocks, 0)]
+        operand = jnp.where(source < row_blocks, local, ghost)
+        acc_ref[row] += jnp.dot(operand, tiles_ref[g], preferred_element_type=jnp.float32)
+        return carry
+
+    lax.fori_loop(0, tiles_ref.shape[0], body, 0, unroll=8)
+    for row in range(row_blocks):
+        out_ref[:, row * block_size : (row + 1) * block_size] = acc_ref[row]
+
+
+def apply_tiles(pattern_flat, tiles, local_blocks, ghost_blocks):
+    row_blocks, vec_count, block_size = local_blocks.shape
+    slots = tiles.shape[0]
+    return pl.pallas_call(
+        product_kernel,
+        out_shape=jax.ShapeDtypeStruct((vec_count, row_blocks * block_size), jnp.float32),
+        in_specs=[
+            pl.BlockSpec(memory_space=pltpu.SMEM),
+            pl.BlockSpec(memory_space=pltpu.VMEM),
+            pl.BlockSpec(memory_space=pltpu.VMEM),
+            pl.BlockSpec(memory_space=pltpu.VMEM),
+        ],
+        out_specs=pl.BlockSpec(memory_space=pltpu.VMEM),
+        scratch_shapes=[pltpu.VMEM((row_blocks, vec_count, block_size), jnp.float32)],
+        cost_estimate=pl.CostEstimate(
+            flops=2 * slots * vec_count * block_size * block_size,
+            transcendentals=0,
+            bytes_accessed=tiles.size * 2 + ghost_blocks.size * 2 + vec_count * row_blocks * block_size * 4,
+        ),
+    )(pattern_flat, tiles, local_blocks, ghost_blocks)
+
+
 def on_device(
     basis_values, potential, contrib_index, pattern, ghost_list, state, damp_lower, damp_upper
 ):
@@ -82,22 +122,21 @@
             .transpose(1, 0, 2)
         )
 
-    def with_ghosts(blocks):
+    def ghosts_of(blocks):
         outgoing = jnp.where(
             (wanted_by >= 0)[:, :, None, None],
             blocks[jnp.clip(wanted_by, 0, row_blocks - 1)],
             jnp.zeros((), jnp.bfloat16),
         )
         arrived = lax.all_to_all(outgoing, "rows", split_axis=0, concat_axis=0, tiled=True)
-        return jnp.concatenate(
-            [blocks, arrived.reshape(n_rows * ghost_width, vec_count, block_size)], axis=0
-        )
+        return arrived.reshape(n_rows * ghost_width, vec_count, block_size)
 
     weighted = (basis_values.astype(jnp.float32) * potential[None, :, None]).astype(jnp.bfloat16)
     send_tiles = presum_tiles(contrib_index.reshape(-1), basis_values, weighted, n_rows)
     arrived_tiles = lax.all_to_all(send_tiles, "rows", split_axis=0, concat_axis=0, tiled=True)
     arrived_tiles, state_in = lax.optimization_barrier((arrived_tiles, state))
-    state_pool = with_ghosts(own_blocks(state_in))
+    state_blocks = own_blocks(state_in)
+    state_ghosts = ghosts_of(state_blocks)
     slot_wanted = jnp.arange(slot_count, dtype=jnp.int32)
     selector = (arrived_slots[None, :] == slot_wanted[:, None]).astype(jnp.bfloat16)
     assembled = jnp.dot(
@@ -108,26 +147,11 @@
     assembled = assembled.astype(jnp.bfloat16).reshape(slot_count, block_size, block_size)
     group_tiles = lax.all_gather(assembled, "cols", axis=0, tiled=True)
 
-    rows_local = pattern[0, :, 0]
-    sources = pattern[0, :, 1]
-
-    def accumulate(tile_part, source_part, row_part, operand_pool):
-        operands = operand_pool[source_part]
-        products = jnp.einsum(
-            "kvb,kba->kva", operands, tile_part, preferred_element_type=jnp.float32
-        )
-        row_select = (row_part[:, None] == jnp.arange(row_blocks, dtype=jnp.int32)[None, :]).astype(
-            jnp.float32
-        )
-        return jnp.einsum("ki,kva->iva", row_select, products, precision=lax.Precision.HIGHEST)
-
-    def as_field(running):
-        return running.transpose(1, 0, 2).reshape(vec_count, row_blocks * block_size)
-
-    first_image = as_field(accumulate(group_tiles, sources, rows_local, state_pool))
+    pattern_flat = pattern.reshape(-1)
+    first_image = apply_tiles(pattern_flat, group_tiles, state_blocks, state_ghosts)
     first_term = (first_image - center * state) / half_width
-    first_pool = with_ghosts(own_blocks(first_term))
-    second_image = as_field(accumulate(group_tiles, sources, rows_local, first_pool))
+    first_blocks = own_blocks(first_term)
+    second_image = apply_tiles(pattern_flat, group_tiles, first_blocks, ghosts_of(first_blocks))
     second_term = 2.0 * (second_image - center * first_term) / half_width - state
     return (first_term, second_term)
 

time: 265 us -> 259 us (0.977)
  matrix products: 17 us -> 1.23 us
  Pallas kernels: 14.6 us -> 28.6 us
  local copies, waits for them, and re-layouts: 14.4 us -> 11 us
    dot_general x4 -> x0, matrix products: 15.7 us -> none  [the longest x2 8.09 us: accumulate(): jnp.einsum('kvb,kba->kva', operands, tile_part, preferred_element_type=jn...]
    pallas_call x0 -> x2, Pallas kernels: none -> 14 us  [apply_tiles(): pl.pallas_call(product_kernel, out_shape=jax.ShapeDtypeStruct((vec_count,...]
    gather x4 -> x2, local copies, waits for them, and re-layouts: 6.17 us -> 1.9 us  [ghosts_of(): blocks[jnp.clip(wanted_by, 0, row_blocks - 1)]]
  transfers between devices with their start and end apart: 4 -> 4, of which waited for: 2 -> 2; matrix products, arithmetic and copies ran while one was open for 5% -> 4% of each run, Pallas kernels for 6% -> 6%
where the time goes in v5:
time: 259 us; the launch traced here: 256 us
  waiting for transfers between devices  95.7 us (37%)
  blocking collectives  56 us (22%)
  starting transfers between devices  40.5 us (16%)
  Pallas kernels  28.6 us (11%)
  between operations  15.5 us (6%)
  local copies, waits for them, and re-layouts  11 us (4%)
  other arithmetic  7.54 us (3%)
    all_to_all x1, blocking collectives, ghosts_of(): lax.all_to_all(outgoing, 'rows', split_axis=0, concat_axis=0, tiled=True)  56 us
    all_to_all x1, waiting for transfers between devices, on_device(): lax.all_to_all(send_tiles, 'rows', split_axis=0, concat_axis=0, tiled=True)  49.1 us
    all_to_all x1, waiting for transfers between devices, ghosts_of(): lax.all_to_all(outgoing, 'rows', split_axis=0, concat_axis=0, tiled=True)  46.6 us
    all_to_all x1, starting transfers between devices, on_device(): lax.all_to_all(index_send, 'rows', split_axis=0, concat_axis=0, tiled=True)  15.9 us
    pallas_call x1, Pallas kernels, presum_tiles(): pl.pallas_call(presum_kernel, out_shape=jax.ShapeDtypeStruct((n_rows, blo...  14.6 us
    pallas_call x2, Pallas kernels, apply_tiles(): pl.pallas_call(product_kernel, out_shape=jax.ShapeDtypeStruct((vec_count,...  14 us
    all_to_all x1, starting transfers between devices, on_device(): lax.all_to_all(send_tiles, 'rows', split_axis=0, concat_axis=0, tiled=True)  12.7 us
    all_to_all x1, starting transfers between devices, ghosts_of(): lax.all_to_all(outgoing, 'rows', split_axis=0, concat_axis=0, tiled=True)  11.7 us
  transfers between devices with their start and end apart: 4, of which 2 were waited for; matrix products, arithmetic and copies ran while one was open for 4% of the time, Pallas kernels for 6%

profile of v5, /device:TPU:56, one launch (start us, length us, event | category | flops | bytes accessed | tf_op | source)
XLA Modules:
  0.0 256.2 jit_solution(734955925170596144)
XLA Ops:
  7.2 0.8 slice_bitcast_fusion.2
  8.7 0.7 copy.30
  9.5 15.9 %all-to-all-start = ((s32[64,1,3]{2,1,0:T(1,128)}), s32[64,1,3]{2,1,0:T(1,128)S(1)}, u32[]{:S(2)}, u32[]{:S(2)}) async-start(s32[64,1,3]{2,1,0:T(1,128)} %copy.30), calls=%async_computation | async-start | bytes 65536 | tf_op jit(solution)/shard_map/all_to_all | solution.py:111
  25.4 0.8 copy.32
  26.2 0.7 reshape.48.index_ref
  26.8 2.2 fusion
  29.1 2.6 %copy.33 = bf16[16,128,512]{2,1,0:T(8,128)(2,1)} copy(bf16[16,128,512]{1,2,0:T(8,128)(2,1)S(1)} %fusion) | data formatting | bytes 4194304 | tf_op jit(solution)/shard_map/transpose | solution.py:30
  31.7 14.6 %shard_map.95 = bf16[64,128,128]{2,1,0:T(8,128)(2,1)} custom-call(s32[512]{0:T(512)} %reshape.48.index_ref, bf16[2048,512]{1,0:T(8,128)(2,1)} %bitcast.55, bf16[16,512,128]{2,1,0:T(8,128)(2,1)} %basis_ref.1), custom_call_target="tpu_custom_call" | custom-call | flops 4294967296 | bytes 6291456 | tf_op jit(solution)/shard_map/pallas_call | solution.py:31
  46.3 12.7 %all-to-all-start.1 = ((bf16[64,128,128]{2,1,0:T(8,128)(2,1)}), bf16[64,128,128]{2,1,0:T(8,128)(2,1)S(1)}, u32[]{:S(2)}, u32[]{:S(2)}) async-start(bf16[64,128,128]{2,1,0:T(8,128)(2,1)} %shard_map.95), calls=%async_computation.1 | async-start | bytes 4194304 | tf_op jit(solution)/shard_map/all_to_all | solution.py:136
  59.3 49.1 %all-to-all-done.1 = bf16[64,128,128]{2,1,0:T(8,128)(2,1)S(1)} async-done(((bf16[64,128,128]{2,1,0:T(8,128)(2,1)}), bf16[64,128,128]{2,1,0:T(8,128)(2,1)S(1)}, u32[]{:S(2)}, u32[]{:S(2)}) %all-to-all-start.1) | async-done | bytes 2097184 | tf_op jit(solution)/shard_map/all_to_all | solution.py:136
  108.4 1.2 fusion.3
  109.6 0.9 copy.41
  111.0 1.0 gather_fusion
  112.0 1.6 broadcast_select_fusion.1
  113.5 11.7 %all-to-all-start.2 = ((bf16[64,2,64,128]{3,2,1,0:T(8,128)(2,1)}), bf16[64,2,64,128]{3,2,1,0:T(8,128)(2,1)S(1)}, u32[]{:S(2)}, u32[]{:S(2)}) async-start(bf16[64,2,64,128]{3,2,1,0:T(8,128)(2,1)} %broadcast_select_fusion.1), calls=%async_computation.2 | async-start | bytes 4194304 | tf_op jit(solution)/shard_map/all_to_all | solution.py:131
  126.7 0.7 reshape.47.pattern_ref
  127.4 46.6 %all-to-all-done.2 = bf16[64,2,64,128]{3,2,1,0:T(8,128)(2,1)S(1)} async-done(((bf16[64,2,64,128]{3,2,1,0:T(8,128)(2,1)}), bf16[64,2,64,128]{3,2,1,0:T(8,128)(2,1)S(1)}, u32[]{:S(2)}, u32[]{:S(2)}) %all-to-all-start.2) | async-done | bytes 2097184 | tf_op jit(solution)/shard_map/all_to_all | solution.py:131
  174.0 1.3 copy-done.2
  175.3 7.0 %shard_map.96 = f32[64,1024]{1,0:T(8,128)} custom-call(s32[256]{0:T(256)} %reshape.47.pattern_ref, bf16[128,128,128]{2,1,0:T(8,128)(2,1)} %all-gather.2.cloned.1.call-done.tiles_ref, bf16[8,64,128]{2,1,0:T(8,128)(2,1)} %copy-done, bf16[128,64,128]{2,1,0:T(8,128)(2,1)} %bitcast.50), custom_call_target="tpu_custom_call" | custom-call | flops 268435456 | bytes 6553600 | tf_op jit(solution)/shard_map/pallas_call | solution.py:73
  182.3 1.0 convert_bitcast_fusion
  183.4 1.0 gather_fusion.1
  184.6 56.0 %all_to_all.27 = bf16[64,2,64,128]{3,2,1,0:T(8,128)(2,1)} all-to-all(bf16[64,2,64,128]{3,2,1,0:T(8,128)(2,1)S(1)} %broadcast_select_fusion), channel_id=1, replica_groups=mesh['rows'=64,'cols'=8] {'rows'}, dimensions={0} | all-to-all | bytes 4194304 | tf_op jit(solution)/shard_map/all_to_all | solution.py:131
  240.6 7.0 %shard_map.97 = f32[64,1024]{1,0:T(8,128)} custom-call(s32[256]{0:T(256)} %reshape.47.pattern_ref, bf16[128,128,128]{2,1,0:T(8,128)(2,1)} %all-gather.2.cloned.1.call-done.tiles_ref, bf16[8,64,128]{2,1,0:T(8,128)(2,1)} %bitcast.49, bf16[128,64,128]{2,1,0:T(8,128)(2,1)} %bitcast.52), custom_call_target="tpu_custom_call" | custom-call | flops 268435456 | bytes 6553600 | tf_op jit(solution)/shard_map/pallas_call | solution.py:73
  247.6 1.7 divide_subtract_fusion
  (31 shorter events, 1.9 us)
Async XLA Ops:
  9.5 36.8 %all-to-all-start = ((s32[64,1,3]{2,1,0:T(1,128)}), s32[64,1,3]{2,1,0:T(1,128)S(1)}, u32[]{:S(2)}, u32[]{:S(2)}) async-start(s32[64,1,3]{2,1,0:T(1,128)} %copy.30), calls=%async_computation | async-start | bytes 65536 | tf_op jit(solution)/shard_map/all_to_all | solution.py:111
  46.3 62.1 %all-to-all-start.1 = ((bf16[64,128,128]{2,1,0:T(8,128)(2,1)}), bf16[64,128,128]{2,1,0:T(8,128)(2,1)S(1)}, u32[]{:S(2)}, u32[]{:S(2)}) async-start(bf16[64,128,128]{2,1,0:T(8,128)(2,1)} %shard_map.95), calls=%async_computation.1 | async-start | bytes 4194304 | tf_op jit(solution)/shard_map/all_to_all | solution.py:136
  59.0 115.0 %all-gather.2.cloned.1.call-start = ((), (), s32[]{:S(2)}) async-start(), calls=%async_computation.4 | async-start | bytes 4718592 | tf_op jit(solution)/shard_map/all_gather | solution.py:148
  108.4 2.5 copy-start.3
  111.0 1.0 copy-start
  113.5 13.1 %copy-start.5 = (s32[1,128,2]{1,2,0:T(2,128)S(1)}, s32[1,128,2]{1,2,0:T(2,128)}, u32[]{:S(2)}) copy-start(s32[1,128,2]{1,2,0:T(2,128)} %param.11) | copy-start | bytes 3076
  113.5 60.5 %all-to-all-start.2 = ((bf16[64,2,64,128]{3,2,1,0:T(8,128)(2,1)}), bf16[64,2,64,128]{3,2,1,0:T(8,128)(2,1)S(1)}, u32[]{:S(2)}, u32[]{:S(2)}) async-start(bf16[64,2,64,128]{3,2,1,0:T(8,128)(2,1)} %broadcast_select_fusion.1), calls=%async_computation.2 | async-start | bytes 4194304 | tf_op jit(solution)/shard_map/all_to_all | solution.py:131
  174.0 1.3 copy-start.2
  183.3 64.3 %copy-start.4 = (f32[64,1024]{1,0:T(8,128)}, f32[64,1024]{1,0:T(8,128)S(1)}, u32[]{:S(2)}) copy-start(f32[64,1024]{1,0:T(8,128)S(1)} %get-tuple-element.7) | copy-start | bytes 786436
  183.4 1.0 copy-start.1
Sparse Core Ops, SparseCore 0:
  110.7 37.1 all-gather.1

commit v6 on v5

--- a/solution.py
+++ b/solution.py
@@ -108,7 +108,8 @@
     to_target = target_row[:, None] == jnp.arange(n_rows, dtype=jnp.int32)[None, :]
     slot_for_target = jnp.max(jnp.where(to_target, contrib_index[:, 1:2], -1), axis=0)
     index_send = jnp.concatenate([requested, slot_for_target[:, None]], axis=1)
-    index_recv = lax.all_to_all(index_send, "rows", split_axis=0, concat_axis=0, tiled=True)
+    index_all = lax.all_gather(index_send, "rows", axis=0)
+    index_recv = lax.dynamic_index_in_dim(index_all, lax.axis_index("rows"), axis=1, keepdims=False)
     wanted_by = index_recv[:, :ghost_width]
     arrived_slots = index_recv[:, ghost_width]
 

time: 259 us -> 277 us (1.069)
  blocking collectives: 56 us -> 151 us
  waiting for transfers between devices: 95.7 us -> 37.6 us
  starting transfers between devices: 40.5 us -> 25.9 us
    all_gather x0 -> x1, blocking collectives: none -> 90.9 us  [on_device(): index_all = lax.all_gather(index_send, 'rows', axis=0)]
    all_to_all x1, waiting for transfers between devices: 49.1 us -> 0.01 us  [on_device(): lax.all_to_all(send_tiles, 'rows', split_axis=0, concat_axis=0, tiled=True)]
    all_to_all x1 -> x0, starting transfers between devices: 15.9 us -> none  [on_device(): lax.all_to_all(index_send, 'rows', split_axis=0, concat_axis=0, tiled=True)]
    all_to_all x1, waiting for transfers between devices: 46.6 us -> 37.6 us  [ghosts_of(): lax.all_to_all(outgoing, 'rows', split_axis=0, concat_axis=0, tiled=True)]
    all_to_all x1, blocking collectives: 56 us -> 60.3 us  [ghosts_of(): lax.all_to_all(outgoing, 'rows', split_axis=0, concat_axis=0, tiled=True)]
    all_to_all x1, starting transfers between devices: 12.7 us -> 16 us  [on_device(): lax.all_to_all(send_tiles, 'rows', split_axis=0, concat_axis=0, tiled=True)]
  transfers between devices with their start and end apart: 4 -> 3, of which waited for: 2 -> 1; matrix products, arithmetic and copies ran while one was open for 4% -> 1% of each run, Pallas kernels for 6% -> 0%
where the time goes in v6:
time: 277 us
  blocking collectives  151 us (55%)
  waiting for transfers between devices  37.6 us (14%)
  Pallas kernels  28.6 us (10%)
  starting transfers between devices  25.9 us (9%)
  between operations  15.6 us (6%)
  local copies, waits for them, and re-layouts  9.74 us (4%)
  other arithmetic  6.87 us (2%)
    all_gather x1, blocking collectives, on_device(): index_all = lax.all_gather(index_send, 'rows', axis=0)  90.9 us
    all_to_all x1, blocking collectives, ghosts_of(): lax.all_to_all(outgoing, 'rows', split_axis=0, concat_axis=0, tiled=True)  60.3 us
    all_to_all x1, waiting for transfers between devices, ghosts_of(): lax.all_to_all(outgoing, 'rows', split_axis=0, concat_axis=0, tiled=True)  37.6 us
    all_to_all x1, starting transfers between devices, on_device(): lax.all_to_all(send_tiles, 'rows', split_axis=0, concat_axis=0, tiled=True)  16 us
    pallas_call x1, Pallas kernels, presum_tiles(): pl.pallas_call(presum_kernel, out_shape=jax.ShapeDtypeStruct((n_rows, blo...  14.6 us
    pallas_call x2, Pallas kernels, apply_tiles(): pl.pallas_call(product_kernel, out_shape=jax.ShapeDtypeStruct((vec_count,...  14.1 us
    all_to_all x1, starting transfers between devices, ghosts_of(): lax.all_to_all(outgoing, 'rows', split_axis=0, concat_axis=0, tiled=True)  9.87 us
  transfers between devices with their start and end apart: 3, of which 1 were waited for; matrix products, arithmetic and copies ran while one was open for 1% of the time, Pallas kernels for 0%

profile of v6, /device:TPU:56, one launch (start us, length us, event | category | flops | bytes accessed | tf_op | source)
XLA Modules:
  0.0 276.7 jit_solution(10304552611072445953)
XLA Ops:
  7.2 0.8 copy.31
  8.0 0.7 reshape.46.index_ref
  8.6 2.2 fusion
  10.9 2.6 copy.32
  13.5 14.6 %shard_map.95 = bf16[64,128,128]{2,1,0:T(8,128)(2,1)} custom-call(s32[512]{0:T(512)} %reshape.46.index_ref, bf16[2048,512]{1,0:T(8,128)(2,1)} %bitcast.55, bf16[16,512,128]{2,1,0:T(8,128)(2,1)} %basis_ref.1), custom_call_target="tpu_custom_call" | custom-call | flops 4294967296 | bytes 6291456 | tf_op jit(solution)/shard_map/pallas_call | solution.py:31
  28.1 16.0 %all-to-all-start = ((bf16[64,128,128]{2,1,0:T(8,128)(2,1)}), bf16[64,128,128]{2,1,0:T(8,128)(2,1)S(1)}, u32[]{:S(2)}, u32[]{:S(2)}) async-start(bf16[64,128,128]{2,1,0:T(8,128)(2,1)} %shard_map.95), calls=%async_computation | async-start | bytes 4194304 | tf_op jit(solution)/shard_map/all_to_all | solution.py:137
  44.4 90.9 %all-gather.1 = s32[64,64,3]{1,2,0:T(4,128)S(1)} all-gather(s32[1,64,3]{1,2,0:T(4,128)S(1)} %add_bitcast_fusion), channel_id=2, replica_groups=mesh['rows'=64,'cols'=8] {'rows'}, dimensions={0}, use_global_device_ids=true | all-gather | bytes 49920 | tf_op jit(solution)/shard_map/all_gather | solution.py:111
  135.2 0.1 constant_dynamic-slice_fusion
  135.5 1.2 fusion.3
  136.7 0.9 copy.40
  137.9 0.1 reshape.56
  138.1 1.0 gather_fusion
  139.1 1.6 broadcast_select_fusion.1
  140.6 9.9 %all-to-all-start.1 = ((bf16[64,2,64,128]{3,2,1,0:T(8,128)(2,1)}), bf16[64,2,64,128]{3,2,1,0:T(8,128)(2,1)S(1)}, u32[]{:S(2)}, u32[]{:S(2)}) async-start(bf16[64,2,64,128]{3,2,1,0:T(8,128)(2,1)} %broadcast_select_fusion.1), calls=%async_computation.1 | async-start | bytes 4194304 | tf_op jit(solution)/shard_map/all_to_all | solution.py:132
  151.9 0.7 reshape.45.pattern_ref
  152.7 37.6 %all-to-all-done.1 = bf16[64,2,64,128]{3,2,1,0:T(8,128)(2,1)S(1)} async-done(((bf16[64,2,64,128]{3,2,1,0:T(8,128)(2,1)}), bf16[64,2,64,128]{3,2,1,0:T(8,128)(2,1)S(1)}, u32[]{:S(2)}, u32[]{:S(2)}) %all-to-all-start.1) | async-done | bytes 2097184 | tf_op jit(solution)/shard_map/all_to_all | solution.py:132
  190.2 1.3 copy-done.2
  191.6 7.0 %shard_map.96 = f32[64,1024]{1,0:T(8,128)} custom-call(s32[256]{0:T(256)} %reshape.45.pattern_ref, bf16[128,128,128]{2,1,0:T(8,128)(2,1)} %all-gather.4.cloned.1.call-done.tiles_ref, bf16[8,64,128]{2,1,0:T(8,128)(2,1)} %copy-done, bf16[128,64,128]{2,1,0:T(8,128)(2,1)} %bitcast.51), custom_call_target="tpu_custom_call" | custom-call | flops 268435456 | bytes 6553600 | tf_op jit(solution)/shard_map/pallas_call | solution.py:73
  198.6 1.0 convert_bitcast_fusion
  199.7 1.0 gather_fusion.1
  200.6 0.2 broadcast_select_fusion
  200.9 60.3 %all_to_all.15 = bf16[64,2,64,128]{3,2,1,0:T(8,128)(2,1)} all-to-all(bf16[64,2,64,128]{3,2,1,0:T(8,128)(2,1)S(1)} %broadcast_select_fusion), channel_id=1, replica_groups=mesh['rows'=64,'cols'=8] {'rows'}, dimensions={0} | all-to-all | bytes 4194304 | tf_op jit(solution)/shard_map/all_to_all | solution.py:132
  261.1 7.0 %shard_map.97 = f32[64,1024]{1,0:T(8,128)} custom-call(s32[256]{0:T(256)} %reshape.45.pattern_ref, bf16[128,128,128]{2,1,0:T(8,128)(2,1)} %all-gather.4.cloned.1.call-done.tiles_ref, bf16[8,64,128]{2,1,0:T(8,128)(2,1)} %bitcast.49, bf16[128,64,128]{2,1,0:T(8,128)(2,1)} %bitcast.52), custom_call_target="tpu_custom_call" | custom-call | flops 268435456 | bytes 6553600 | tf_op jit(solution)/shard_map/pallas_call | solution.py:73
  268.1 1.7 divide_subtract_fusion
  (34 shorter events, 0.7 us)
Async XLA Ops:
  28.1 16.1 %copy-start.5 = (s32[128,4]{0,1:T(4,128)S(1)}, s32[128,4]{0,1:T(4,128)}, u32[]{:S(2)}) copy-start(s32[128,4]{0,1:T(4,128)} %param.10) | copy-start | bytes 6148
  28.1 16.2 %copy-start.7 = (s32[1,64,2]{1,2,0:T(2,128)S(1)}, s32[1,64,2]{1,2,0:T(2,128)}, u32[]{:S(2)}) copy-start(s32[1,64,2]{1,2,0:T(2,128)} %param.12) | copy-start | bytes 1540
  28.1 107.4 %all-to-all-start = ((bf16[64,128,128]{2,1,0:T(8,128)(2,1)}), bf16[64,128,128]{2,1,0:T(8,128)(2,1)S(1)}, u32[]{:S(2)}, u32[]{:S(2)}) async-start(bf16[64,128,128]{2,1,0:T(8,128)(2,1)} %shard_map.95), calls=%async_computation | async-start | bytes 4194304 | tf_op jit(solution)/shard_map/all_to_all | solution.py:137
  44.1 146.1 %all-gather.4.cloned.1.call-start = ((), (), s32[]{:S(2)}) async-start(), calls=%async_computation.3 | async-start | bytes 4718592 | tf_op jit(solution)/shard_map/all_gather | solution.py:149
  135.5 2.6 copy-start.3
  138.1 1.0 copy-start
  140.6 11.2 %copy-start.6 = (s32[1,128,2]{1,2,0:T(2,128)S(1)}, s32[1,128,2]{1,2,0:T(2,128)}, u32[]{:S(2)}) copy-start(s32[1,128,2]{1,2,0:T(2,128)} %param.11) | copy-start | bytes 3076
  140.6 49.6 %all-to-all-start.1 = ((bf16[64,2,64,128]{3,2,1,0:T(8,128)(2,1)}), bf16[64,2,64,128]{3,2,1,0:T(8,128)(2,1)S(1)}, u32[]{:S(2)}, u32[]{:S(2)}) async-start(bf16[64,2,64,128]{3,2,1,0:T(8,128)(2,1)} %broadcast_select_fusion.1), calls=%async_computation.1 | async-start | bytes 4194304 | tf_op jit(solution)/shard_map/all_to_all | solution.py:132
  190.2 1.3 copy-start.2
  199.6 68.5 %copy-start.4 = (f32[64,1024]{1,0:T(8,128)}, f32[64,1024]{1,0:T(8,128)S(1)}, u32[]{:S(2)}) copy-start(f32[64,1024]{1,0:T(8,128)S(1)} %get-tuple-element.7) | copy-start | bytes 786436
  199.7 1.0 copy-start.1
Sparse Core Ops, SparseCore 0:
  137.8 35.3 all-gather.3

commit v7 on v5

--- a/solution.py
+++ b/solution.py
@@ -1,3 +1,5 @@
+import functools
+
 import jax
 import jax.numpy as jnp
 from jax import lax
@@ -21,7 +23,7 @@
         acc_ref[target] += tiles_ref[index_ref[4 * s + 2], index_ref[4 * s + 3]].astype(jnp.float32)
         return carry
 
-    lax.fori_loop(0, index_ref.shape[0] // 4, body, 0)
+    lax.fori_loop(0, index_ref.shape[0] // 4, body, 0, unroll=8)
     out_ref[...] = acc_ref[...].astype(out_ref.dtype)
 
 
@@ -49,8 +51,9 @@
     )(index_flat, stacked, basis)
 
 
-def product_kernel(pattern_ref, tiles_ref, local_ref, ghost_ref, out_ref, acc_ref):
+def product_kernel(first, pattern_ref, scalar_ref, tiles_ref, local_ref, ghost_ref, *refs):
     row_blocks, vec_count, block_size = local_ref.shape
+    acc_ref = refs[-1]
     acc_ref[...] = jnp.zeros_like(acc_ref)
 
     def body(g, carry):
@@ -63,30 +66,47 @@
         return carry
 
     lax.fori_loop(0, tiles_ref.shape[0], body, 0, unroll=8)
-    for row in range(row_blocks):
-        out_ref[:, row * block_size : (row + 1) * block_size] = acc_ref[row]
+    center = scalar_ref[0]
+    half_width = scalar_ref[1]
+    if first:
+        state_ref, out_ref, blocks_ref = refs[0], refs[1], refs[2]
+        for row in range(row_blocks):
+            lanes = slice(row * block_size, (row + 1) * block_size)
+            term = (acc_ref[row] - center * state_ref[:, lanes]) / half_width
+            out_ref[:, lanes] = term
+            blocks_ref[row] = term.astype(blocks_ref.dtype)
+    else:
+        first_ref, state_ref, out_ref = refs[0], refs[1], refs[2]
+        for row in range(row_blocks):
+            lanes = slice(row * block_size, (row + 1) * block_size)
+            out_ref[:, lanes] = (
+                2.0 * (acc_ref[row] - center * first_ref[:, lanes]) / half_width
+                - state_ref[:, lanes]
+            )
 
 
-def apply_tiles(pattern_flat, tiles, local_blocks, ghost_blocks):
+def apply_tiles(pattern_flat, scalars, tiles, local_blocks, ghost_blocks, fields):
     row_blocks, vec_count, block_size = local_blocks.shape
     slots = tiles.shape[0]
+    field = jax.ShapeDtypeStruct((vec_count, row_blocks * block_size), jnp.float32)
+    if len(fields) == 1:
+        out_shape = (field, jax.ShapeDtypeStruct(local_blocks.shape, jnp.bfloat16))
+    else:
+        out_shape = field
+    vmem = pl.BlockSpec(memory_space=pltpu.VMEM)
+    smem = pl.BlockSpec(memory_space=pltpu.SMEM)
     return pl.pallas_call(
-        product_kernel,
-        out_shape=jax.ShapeDtypeStruct((vec_count, row_blocks * block_size), jnp.float32),
-        in_specs=[
-            pl.BlockSpec(memory_space=pltpu.SMEM),
-            pl.BlockSpec(memory_space=pltpu.VMEM),
-            pl.BlockSpec(memory_space=pltpu.VMEM),
-            pl.BlockSpec(memory_space=pltpu.VMEM),
-        ],
-        out_specs=pl.BlockSpec(memory_space=pltpu.VMEM),
+        functools.partial(product_kernel, len(fields) == 1),
+        out_shape=out_shape,
+        in_specs=[smem, smem] + [vmem] * (3 + len(fields)),
+        out_specs=(vmem, vmem) if len(fields) == 1 else vmem,
         scratch_shapes=[pltpu.VMEM((row_blocks, vec_count, block_size), jnp.float32)],
         cost_estimate=pl.CostEstimate(
             flops=2 * slots * vec_count * block_size * block_size,
             transcendentals=0,
-            bytes_accessed=tiles.size * 2 + ghost_blocks.size * 2 + vec_count * row_blocks * block_size * 4,
+            bytes_accessed=tiles.size * 2 + ghost_blocks.size * 2 + 3 * field.size * 4,
         ),
-    )(pattern_flat, tiles, local_blocks, ghost_blocks)
+    )(pattern_flat, scalars, tiles, local_blocks, ghost_blocks, *fields)
 
 
 def on_device(
@@ -148,11 +168,13 @@
     group_tiles = lax.all_gather(assembled, "cols", axis=0, tiled=True)
 
     pattern_flat = pattern.reshape(-1)
-    first_image = apply_tiles(pattern_flat, group_tiles, state_blocks, state_ghosts)
-    first_term = (first_image - center * state) / half_width
-    first_blocks = own_blocks(first_term)
-    second_image = apply_tiles(pattern_flat, group_tiles, first_blocks, ghosts_of(first_blocks))
-    second_term = 2.0 * (second_image - center * first_term) / half_width - state
+    scalars = jnp.stack([center, half_width])
+    first_term, first_blocks = apply_tiles(
+        pattern_flat, scalars, group_tiles, state_blocks, state_ghosts, (state,)
+    )
+    second_term = apply_tiles(
+        pattern_flat, scalars, group_tiles, first_blocks, ghosts_of(first_blocks), (first_term, state)
+    )
     return (first_term, second_term)
 
 

time: 259 us -> 256 us (0.988)
  transfers between devices with their start and end apart: 4 -> 4, of which waited for: 2 -> 2; matrix products, arithmetic and copies ran while one was open for 4% -> 4% of each run, Pallas kernels for 6% -> 5%
where the time goes in v7:
time: 256 us; the launch traced here: 254 us
  waiting for transfers between devices  95.1 us (37%)
  blocking collectives  56 us (22%)
  starting transfers between devices  40.5 us (16%)
  Pallas kernels  28.1 us (11%)
  between operations  15.5 us (6%)
  local copies, waits for them, and re-layouts  11.8 us (5%)
  other arithmetic  5.46 us (2%)
    all_to_all x1, blocking collectives, ghosts_of(): lax.all_to_all(outgoing, 'rows', split_axis=0, concat_axis=0, tiled=True)  56 us
    all_to_all x1, waiting for transfers between devices, on_device(): lax.all_to_all(send_tiles, 'rows', split_axis=0, concat_axis=0, tiled=True)  49.1 us
    all_to_all x1, waiting for transfers between devices, ghosts_of(): lax.all_to_all(outgoing, 'rows', split_axis=0, concat_axis=0, tiled=True)  46 us
    all_to_all x1, starting transfers between devices, on_device(): lax.all_to_all(index_send, 'rows', split_axis=0, concat_axis=0, tiled=True)  15.9 us
    pallas_call x2, Pallas kernels, apply_tiles(): pl.pallas_call(functools.partial(product_kernel, len(fields) == 1), out_s...  14.2 us
    pallas_call x1, Pallas kernels, presum_tiles(): pl.pallas_call(presum_kernel, out_shape=jax.ShapeDtypeStruct((n_rows, blo...  13.9 us
    all_to_all x1, starting transfers between devices, on_device(): lax.all_to_all(send_tiles, 'rows', split_axis=0, concat_axis=0, tiled=True)  12.7 us
    all_to_all x1, starting transfers between devices, ghosts_of(): lax.all_to_all(outgoing, 'rows', split_axis=0, concat_axis=0, tiled=True)  11.7 us
  transfers between devices with their start and end apart: 4, of which 2 were waited for; matrix products, arithmetic and copies ran while one was open for 4% of the time, Pallas kernels for 5%

profile of v7, /device:TPU:56, one launch (start us, length us, event | category | flops | bytes accessed | tf_op | source)
XLA Modules:
  0.0 253.7 jit_solution(15693151373810918236)
XLA Ops:
  7.2 0.8 slice_bitcast_fusion.2
  7.9 0.7 compare_select_fusion.1
  8.7 0.7 copy.28
  9.5 15.9 %all-to-all-start = ((s32[64,1,3]{2,1,0:T(1,128)}), s32[64,1,3]{2,1,0:T(1,128)S(1)}, u32[]{:S(2)}, u32[]{:S(2)}) async-start(s32[64,1,3]{2,1,0:T(1,128)} %copy.28), calls=%async_computation | async-start | bytes 65536 | tf_op jit(solution)/shard_map/all_to_all | solution.py:131
  25.4 0.8 copy.30
  26.2 0.7 reshape.47.index_ref
  26.8 2.2 fusion
  29.1 2.6 %copy.31 = bf16[16,128,512]{2,1,0:T(8,128)(2,1)} copy(bf16[16,128,512]{1,2,0:T(8,128)(2,1)S(1)} %fusion) | data formatting | bytes 4194304 | tf_op jit(solution)/shard_map/transpose | solution.py:32
  31.7 13.9 %shard_map.95 = bf16[64,128,128]{2,1,0:T(8,128)(2,1)} custom-call(s32[512]{0:T(512)} %reshape.47.index_ref, bf16[2048,512]{1,0:T(8,128)(2,1)} %bitcast.43, bf16[16,512,128]{2,1,0:T(8,128)(2,1)} %basis_ref.1), custom_call_target="tpu_custom_call" | custom-call | flops 4294967296 | bytes 6291456 | tf_op jit(solution)/shard_map/pallas_call | solution.py:33
  45.6 12.7 %all-to-all-start.1 = ((bf16[64,128,128]{2,1,0:T(8,128)(2,1)}), bf16[64,128,128]{2,1,0:T(8,128)(2,1)S(1)}, u32[]{:S(2)}, u32[]{:S(2)}) async-start(bf16[64,128,128]{2,1,0:T(8,128)(2,1)} %shard_map.95), calls=%async_computation.1 | async-start | bytes 4194304 | tf_op jit(solution)/shard_map/all_to_all | solution.py:156
  58.6 49.1 %all-to-all-done.1 = bf16[64,128,128]{2,1,0:T(8,128)(2,1)S(1)} async-done(((bf16[64,128,128]{2,1,0:T(8,128)(2,1)}), bf16[64,128,128]{2,1,0:T(8,128)(2,1)S(1)}, u32[]{:S(2)}, u32[]{:S(2)}) %all-to-all-start.1) | async-done | bytes 2097184 | tf_op jit(solution)/shard_map/all_to_all | solution.py:156
  107.7 1.2 fusion.3
  108.9 0.9 copy.37
  110.3 1.0 gather_fusion
  111.2 1.5 broadcast_select_fusion.1
  112.8 11.7 %all-to-all-start.2 = ((bf16[64,2,64,128]{3,2,1,0:T(8,128)(2,1)}), bf16[64,2,64,128]{3,2,1,0:T(8,128)(2,1)S(1)}, u32[]{:S(2)}, u32[]{:S(2)}) async-start(bf16[64,2,64,128]{3,2,1,0:T(8,128)(2,1)} %broadcast_select_fusion.1), calls=%async_computation.2 | async-start | bytes 4194304 | tf_op jit(solution)/shard_map/all_to_all | solution.py:151
  125.9 0.7 reshape.46.pattern_ref
  126.6 0.6 pad_maximum_fusion.scalar_ref
  127.3 46.0 %all-to-all-done.2 = bf16[64,2,64,128]{3,2,1,0:T(8,128)(2,1)S(1)} async-done(((bf16[64,2,64,128]{3,2,1,0:T(8,128)(2,1)}), bf16[64,2,64,128]{3,2,1,0:T(8,128)(2,1)S(1)}, u32[]{:S(2)}, u32[]{:S(2)}) %all-to-all-start.2) | async-done | bytes 2097184 | tf_op jit(solution)/shard_map/all_to_all | solution.py:151
  173.3 1.3 copy-done.1
  174.6 7.1 %shard_map.96 = (f32[64,1024]{1,0:T(8,128)}, bf16[8,64,128]{2,1,0:T(8,128)(2,1)}) custom-call(s32[256]{0:T(256)} %reshape.46.pattern_ref, f32[2]{0:T(128)} %pad_maximum_fusion.scalar_ref, bf16[128,128,128]{2,1,0:T(8,128)(2,1)} %all-gather.2.cloned.1.call-done.tiles_ref, bf16[8,64,128]{2,1,0:T(8,128)(2,1)} %copy-done, bf16[128,64,128]{2,1,0:T(8,128)(2,1)} %bitcast.38, ...), custom_call_target="tpu_custom_call" | custom-call | flops 268435456 | bytes 7077888 | tf_op jit(solution)/shard_map/pallas_call | solution.py:98
  181.7 1.9 gather_fusion.1
  183.7 56.0 %all_to_all.27 = bf16[64,2,64,128]{3,2,1,0:T(8,128)(2,1)} all-to-all(bf16[64,2,64,128]{3,2,1,0:T(8,128)(2,1)S(1)} %broadcast_select_fusion), channel_id=1, replica_groups=mesh['rows'=64,'cols'=8] {'rows'}, dimensions={0} | all-to-all | bytes 4194304 | tf_op jit(solution)/shard_map/all_to_all | solution.py:151
  239.7 7.1 %shard_map.97 = f32[64,1024]{1,0:T(8,128)} custom-call(s32[256]{0:T(256)} %reshape.46.pattern_ref, f32[2]{0:T(128)} %pad_maximum_fusion.scalar_ref, bf16[128,128,128]{2,1,0:T(8,128)(2,1)} %all-gather.2.cloned.1.call-done.tiles_ref, bf16[8,64,128]{2,1,0:T(8,128)(2,1)} %get-tuple-element.9.local_ref, bf16[128,64,128]{2,1,0:T(8,128)(2,1)} %bitcast.42, ...), custom_call_target="tpu_custom_call" | custom-call | flops 268435456 | bytes 7077888 | tf_op jit(solution)/shard_map/pallas_call | solution.py:98
  (25 shorter events, 1.2 us)
Async XLA Ops:
  9.5 36.1 %all-to-all-start = ((s32[64,1,3]{2,1,0:T(1,128)}), s32[64,1,3]{2,1,0:T(1,128)S(1)}, u32[]{:S(2)}, u32[]{:S(2)}) async-start(s32[64,1,3]{2,1,0:T(1,128)} %copy.28), calls=%async_computation | async-start | bytes 65536 | tf_op jit(solution)/shard_map/all_to_all | solution.py:131
  45.6 62.1 %all-to-all-start.1 = ((bf16[64,128,128]{2,1,0:T(8,128)(2,1)}), bf16[64,128,128]{2,1,0:T(8,128)(2,1)S(1)}, u32[]{:S(2)}, u32[]{:S(2)}) async-start(bf16[64,128,128]{2,1,0:T(8,128)(2,1)} %shard_map.95), calls=%async_computation.1 | async-start | bytes 4194304 | tf_op jit(solution)/shard_map/all_to_all | solution.py:156
  58.3 115.0 %all-gather.2.cloned.1.call-start = ((), (), s32[]{:S(2)}) async-start(), calls=%async_computation.4 | async-start | bytes 4718592 | tf_op jit(solution)/shard_map/all_gather | solution.py:168
  107.7 2.6 %copy-start.2 = (f32[64,1024]{1,0:T(8,128)S(1)}, f32[64,1024]{1,0:T(8,128)}, u32[]{:S(2)}) copy-start(f32[64,1024]{1,0:T(8,128)} %refs_1_.1) | copy-start | bytes 786436
  110.3 1.0 copy-start
  112.8 13.0 %copy-start.3 = (s32[1,128,2]{1,2,0:T(2,128)S(1)}, s32[1,128,2]{1,2,0:T(2,128)}, u32[]{:S(2)}) copy-start(s32[1,128,2]{1,2,0:T(2,128)} %param.11) | copy-start | bytes 3076
  112.8 60.5 %all-to-all-start.2 = ((bf16[64,2,64,128]{3,2,1,0:T(8,128)(2,1)}), bf16[64,2,64,128]{3,2,1,0:T(8,128)(2,1)S(1)}, u32[]{:S(2)}, u32[]{:S(2)}) async-start(bf16[64,2,64,128]{3,2,1,0:T(8,128)(2,1)} %broadcast_select_fusion.1), calls=%async_computation.2 | async-start | bytes 4194304 | tf_op jit(solution)/shard_map/all_to_all | solution.py:151
  173.3 1.3 copy-start.1
Sparse Core Ops, SparseCore 0:
  110.0 37.0 all-gather.1

commit v8 on v7

--- a/solution.py
+++ b/solution.py
@@ -57,12 +57,14 @@
     acc_ref[...] = jnp.zeros_like(acc_ref)
 
     def body(g, carry):
-        row = pattern_ref[2 * g]
-        source = pattern_ref[2 * g + 1]
+        row = pattern_ref[3 * g]
+        source = pattern_ref[3 * g + 1]
         local = local_ref[jnp.minimum(source, row_blocks - 1)]
         ghost = ghost_ref[jnp.maximum(source - row_blocks, 0)]
         operand = jnp.where(source < row_blocks, local, ghost)
-        acc_ref[row] += jnp.dot(operand, tiles_ref[g], preferred_element_type=jnp.float32)
+        acc_ref[row] += jnp.dot(
+            operand, tiles_ref[pattern_ref[3 * g + 2]], preferred_element_type=jnp.float32
+        )
         return carry
 
     lax.fori_loop(0, tiles_ref.shape[0], body, 0, unroll=8)
@@ -165,9 +167,16 @@
         preferred_element_type=jnp.float32,
     )
     assembled = assembled.astype(jnp.bfloat16).reshape(slot_count, block_size, block_size)
-    group_tiles = lax.all_gather(assembled, "cols", axis=0, tiled=True)
-
-    pattern_flat = pattern.reshape(-1)
+    shifted = [assembled] + [
+        lax.ppermute(assembled, "cols", [(i, (i + k) % n_cols) for i in range(n_cols)])
+        for k in range(1, n_cols)
+    ]
+    group_tiles = jnp.concatenate(shifted, axis=0)
+    slot_ids = jnp.arange(group_slots, dtype=jnp.int32)
+    shift_of = (lax.axis_index("cols") - slot_ids // slot_count) % n_cols
+    tile_index = shift_of * slot_count + slot_ids % slot_count
+
+    pattern_flat = jnp.concatenate([pattern[0], tile_index[:, None]], axis=1).reshape(-1)
     scalars = jnp.stack([center, half_width])
     first_term, first_blocks = apply_tiles(
         pattern_flat, scalars, group_tiles, state_blocks, state_ghosts, (state,)

time: 256 us -> 262 us (1.023)
  the two profiles are of different devices: /device:TPU:56 before, /device:TPU:24 now
where the time goes in v8:
time: 262 us
  waiting for transfers between devices  71.6 us (27%)
  blocking collectives  71.2 us (27%)
  starting transfers between devices  59 us (23%)
  Pallas kernels  28.2 us (11%)
  local copies, waits for them, and re-layouts  21.2 us (8%)
  other arithmetic  5.55 us (2%)
  matrix products  2.82 us (1%)
    all_to_all x1, blocking collectives, ghosts_of(): lax.all_to_all(outgoing, 'rows', split_axis=0, concat_axis=0, tiled=True)  71.2 us
    all_to_all x1, waiting for transfers between devices, on_device(): lax.all_to_all(send_tiles, 'rows', split_axis=0, concat_axis=0, tiled=True)  51.6 us
    ppermute x7, starting transfers between devices, on_device(): lax.ppermute(assembled, 'cols', [(i, (i + k) % n_cols) for i in range(n_c...  20.8 us
    ppermute x7, waiting for transfers between devices, on_device(): lax.ppermute(assembled, 'cols', [(i, (i + k) % n_cols) for i in range(n_c...  19.9 us
    all_to_all x1, starting transfers between devices, on_device(): lax.all_to_all(index_send, 'rows', split_axis=0, concat_axis=0, tiled=True)  16.4 us
    pallas_call x2, Pallas kernels, apply_tiles(): pl.pallas_call(functools.partial(product_kernel, len(fields) == 1), out_s...  14.3 us
    pallas_call x1, Pallas kernels, presum_tiles(): pl.pallas_call(presum_kernel, out_shape=jax.ShapeDtypeStruct((n_rows, blo...  13.9 us
    all_to_all x1, starting transfers between devices, on_device(): lax.all_to_all(send_tiles, 'rows', split_axis=0, concat_axis=0, tiled=True)  13 us
  transfers between devices with their start and end apart: 10, of which 6 were waited for; matrix products, arithmetic and copies ran while one was open for 8% of the time, Pallas kernels for 5%

profile of v8, /device:TPU:24, one launch (start us, length us, event | category | flops | bytes accessed | tf_op | source)
XLA Modules:
  0.0 261.6 jit_solution(14845039359474085935)
XLA Ops:
  2.9 16.4 %all-to-all-start = ((s32[64,1,3]{2,1,0:T(1,128)}), s32[64,1,3]{2,1,0:T(1,128)S(1)}, u32[]{:S(2)}, u32[]{:S(2)}) async-start(s32[64,1,3]{2,1,0:T(1,128)} %copy.28), calls=%async_computation | async-start | bytes 65536 | tf_op jit(solution)/shard_map/all_to_all | solution.py:133
  20.1 2.2 fusion
  22.3 2.7 %copy.31 = bf16[16,128,512]{2,1,0:T(8,128)(2,1)} copy(bf16[16,128,512]{1,2,0:T(8,128)(2,1)S(1)} %fusion) | data formatting | bytes 4194304 | tf_op jit(solution)/shard_map/transpose | solution.py:32
  25.6 13.9 %shard_map.95 = bf16[64,128,128]{2,1,0:T(8,128)(2,1)} custom-call(s32[512]{0:T(512)} %reshape.138.index_ref, bf16[2048,512]{1,0:T(8,128)(2,1)} %bitcast.43, bf16[16,512,128]{2,1,0:T(8,128)(2,1)} %basis_ref.1), custom_call_target="tpu_custom_call" | custom-call | flops 4294967296 | bytes 6291456 | tf_op jit(solution)/shard_map/pallas_call | solution.py:33
  39.6 13.0 %all-to-all-start.1 = ((bf16[64,128,128]{2,1,0:T(8,128)(2,1)}), bf16[64,128,128]{2,1,0:T(8,128)(2,1)}, u32[]{:S(2)}, u32[]{:S(2)}) async-start(bf16[64,128,128]{2,1,0:T(8,128)(2,1)} %shard_map.95), calls=%async_computation.1 | async-start | bytes 4194304 | tf_op jit(solution)/shard_map/all_to_all | solution.py:158
  53.0 51.6 %all-to-all-done.1 = bf16[64,128,128]{2,1,0:T(8,128)(2,1)} async-done(((bf16[64,128,128]{2,1,0:T(8,128)(2,1)}), bf16[64,128,128]{2,1,0:T(8,128)(2,1)}, u32[]{:S(2)}, u32[]{:S(2)}) %all-to-all-start.1) | async-done | bytes 2097184 | tf_op jit(solution)/shard_map/all_to_all | solution.py:158
  107.3 8.8 %all-to-all-start.2 = ((bf16[64,2,64,128]{3,2,1,0:T(8,128)(2,1)}), bf16[64,2,64,128]{3,2,1,0:T(8,128)(2,1)S(1)}, u32[]{:S(2)}, u32[]{:S(2)}) async-start(bf16[64,2,64,128]{3,2,1,0:T(8,128)(2,1)} %broadcast_select_fusion.1), calls=%async_computation.2 | async-start | bytes 4194304 | tf_op jit(solution)/shard_map/all_to_all | solution.py:153
  116.0 2.8 %fusion.3 = bf16[2,8,128,128]{3,1,2,0:T(8,128)(2,1)S(1)} fusion(bf16[8,8,128,128]{3,2,1,0:T(8,128)(2,1)} %bitcast.17, s32[64]{0:T(128)S(1)} %slice_bitcast_fusion), kind=kOutput, calls=%fused_computation.9 | convolution fusion | flops 33817600 | bytes 2621696 | tf_op jit(solution)/shard_map/dot_general | solution.py:164
  119.0 3.5 %collective-permute-start.1 = (bf16[16,128,128]{2,1,0:T(8,128)(2,1)S(1)}, bf16[16,128,128]{2,1,0:T(8,128)(2,1)}, u32[]{:S(2)}, u32[]{:S(2)}) collective-permute-start(bf16[16,128,128]{2,1,0:T(8,128)(2,1)S(1)} %bitcast.45), channel_id=1, source_target_pairs={{0,2},{1,3},{2,4},{3,5},{4,6},{5,7},{6,0},{7,1},{8,10},{9,11},{10,... | collective-permute-start | bytes 1572872 | tf_op jit(solution)/shard_map/ppermute | solution.py:171
  122.5 3.9 %collective-permute-start.2 = (bf16[16,128,128]{2,1,0:T(8,128)(2,1)S(1)}, bf16[16,128,128]{2,1,0:T(8,128)(2,1)}, u32[]{:S(2)}, u32[]{:S(2)}) collective-permute-start(bf16[16,128,128]{2,1,0:T(8,128)(2,1)S(1)} %bitcast.46), channel_id=1, source_target_pairs={{0,3},{1,4},{2,5},{3,6},{4,7},{5,0},{6,1},{7,2},{8,11},{9,12},{10,... | collective-permute-start | bytes 1572872 | tf_op jit(solution)/shard_map/ppermute | solution.py:171
  127.7 4.0 %collective-permute-start.3 = (bf16[16,128,128]{2,1,0:T(8,128)(2,1)S(1)}, bf16[16,128,128]{2,1,0:T(8,128)(2,1)}, u32[]{:S(2)}, u32[]{:S(2)}) collective-permute-start(bf16[16,128,128]{2,1,0:T(8,128)(2,1)S(1)} %bitcast.47), channel_id=1, source_target_pairs={{0,4},{1,5},{2,6},{3,7},{4,0},{5,1},{6,2},{7,3},{8,12},{9,13},{10,... | collective-permute-start | bytes 1572872 | tf_op jit(solution)/shard_map/ppermute | solution.py:171
  133.3 3.4 %collective-permute-start.4 = (bf16[16,128,128]{2,1,0:T(8,128)(2,1)S(1)}, bf16[16,128,128]{2,1,0:T(8,128)(2,1)S(1)}, u32[]{:S(2)}, u32[]{:S(2)}) collective-permute-start(bf16[16,128,128]{2,1,0:T(8,128)(2,1)S(1)} %bitcast.48), channel_id=1, source_target_pairs={{0,5},{1,6},{2,7},{3,0},{4,1},{5,2},{6,3},{7,4},{8,13},{9,14},{10,... | collective-permute-start | bytes 1572872 | tf_op jit(solution)/shard_map/ppermute | solution.py:171
  137.6 3.3 %collective-permute-start.5 = (bf16[16,128,128]{2,1,0:T(8,128)(2,1)S(1)}, bf16[16,128,128]{2,1,0:T(8,128)(2,1)S(1)}, u32[]{:S(2)}, u32[]{:S(2)}) collective-permute-start(bf16[16,128,128]{2,1,0:T(8,128)(2,1)S(1)} %bitcast.50), channel_id=1, source_target_pairs={{0,6},{1,7},{2,0},{3,1},{4,2},{5,3},{6,4},{7,5},{8,14},{9,15},{10,... | collective-permute-start | bytes 1572872 | tf_op jit(solution)/shard_map/ppermute | solution.py:171
  141.7 2.7 %collective-permute-start.6 = (bf16[16,128,128]{2,1,0:T(8,128)(2,1)S(1)}, bf16[16,128,128]{2,1,0:T(8,128)(2,1)S(1)}, u32[]{:S(2)}, u32[]{:S(2)}) collective-permute-start(bf16[16,128,128]{2,1,0:T(8,128)(2,1)S(1)} %bitcast.51), channel_id=1, source_target_pairs={{0,7},{1,0},{2,1},{3,2},{4,3},{5,4},{6,5},{7,6},{8,15},{9,8},{10,9... | collective-permute-start | bytes 1572872 | tf_op jit(solution)/shard_map/ppermute | solution.py:171
  144.4 1.9 constant_dynamic-update-slice_fusion.5
  146.4 9.0 %collective-permute-done.2 = bf16[16,128,128]{2,1,0:T(8,128)(2,1)} collective-permute-done((bf16[16,128,128]{2,1,0:T(8,128)(2,1)S(1)}, bf16[16,128,128]{2,1,0:T(8,128)(2,1)}, u32[]{:S(2)}, u32[]{:S(2)}) %collective-permute-start.2) | collective-permute-done | bytes 524320 | tf_op jit(solution)/shard_map/ppermute | solution.py:171
  155.4 1.9 constant_dynamic-update-slice_fusion.4
  157.3 3.2 %collective-permute-done.3 = bf16[16,128,128]{2,1,0:T(8,128)(2,1)} collective-permute-done((bf16[16,128,128]{2,1,0:T(8,128)(2,1)S(1)}, bf16[16,128,128]{2,1,0:T(8,128)(2,1)}, u32[]{:S(2)}, u32[]{:S(2)}) %collective-permute-start.3) | collective-permute-done | bytes 524320 | tf_op jit(solution)/shard_map/ppermute | solution.py:171
  160.5 1.9 constant_dynamic-update-slice_fusion.3
  162.4 3.6 %collective-permute-done.4 = bf16[16,128,128]{2,1,0:T(8,128)(2,1)S(1)} collective-permute-done((bf16[16,128,128]{2,1,0:T(8,128)(2,1)S(1)}, bf16[16,128,128]{2,1,0:T(8,128)(2,1)S(1)}, u32[]{:S(2)}, u32[]{:S(2)}) %collective-permute-start.4) | collective-permute-done | bytes 524320 | tf_op jit(solution)/shard_map/ppermute | solution.py:171
  168.1 3.7 %collective-permute-done.6 = bf16[16,128,128]{2,1,0:T(8,128)(2,1)S(1)} collective-permute-done((bf16[16,128,128]{2,1,0:T(8,128)(2,1)S(1)}, bf16[16,128,128]{2,1,0:T(8,128)(2,1)S(1)}, u32[]{:S(2)}, u32[]{:S(2)}) %collective-permute-start.6) | collective-permute-done | bytes 524320 | tf_op jit(solution)/shard_map/ppermute | solution.py:171
  174.0 7.1 %shard_map.96 = (f32[64,1024]{1,0:T(8,128)}, bf16[8,64,128]{2,1,0:T(8,128)(2,1)}) custom-call(s32[384]{0:T(512)} %reshape.137.pattern_ref, f32[2]{0:T(128)} %pad_maximum_fusion.scalar_ref, bf16[128,128,128]{2,1,0:T(8,128)(2,1)} %constant_dynamic-update-slice_fusion.tiles_ref, bf16[8,64,128]{2,1,0:T(8,128)(2,1)} %copy-done, bf16[128,64,128]{2,1,0:T(8,128)(2,1)} %bitcast.39, ...), custom_call_target="tpu_custom_call" | custom-call | flops 268435456 | bytes 7077888 | tf_op jit(solution)/shard_map/pallas_call | solution.py:100
  183.2 71.2 %all_to_all.27 = bf16[64,2,64,128]{3,2,1,0:T(8,128)(2,1)} all-to-all(bf16[64,2,64,128]{3,2,1,0:T(8,128)(2,1)S(1)} %broadcast_select_fusion), channel_id=1, replica_groups=mesh['rows'=64,'cols'=8] {'rows'}, dimensions={0} | all-to-all | bytes 4194304 | tf_op jit(solution)/shard_map/all_to_all | solution.py:153
  254.4 7.2 %shard_map.97 = f32[64,1024]{1,0:T(8,128)} custom-call(s32[384]{0:T(512)} %reshape.137.pattern_ref, f32[2]{0:T(128)} %pad_maximum_fusion.scalar_ref, bf16[128,128,128]{2,1,0:T(8,128)(2,1)} %constant_dynamic-update-slice_fusion.tiles_ref, bf16[8,64,128]{2,1,0:T(8,128)(2,1)} %get-tuple-element.9.local_ref, bf16[128,64,128]{2,1,0:T(8,128)(2,1)} %bitcast.42, ...), custom_call_target="tpu_custom_call" | custom-call | flops 268435456 | bytes 7077888 | tf_op jit(solution)/shard_map/pallas_call | solution.py:100
  (46 shorter events, 16.6 us)
Async XLA Ops:
  2.9 36.6 %all-to-all-start = ((s32[64,1,3]{2,1,0:T(1,128)}), s32[64,1,3]{2,1,0:T(1,128)S(1)}, u32[]{:S(2)}, u32[]{:S(2)}) async-start(s32[64,1,3]{2,1,0:T(1,128)} %copy.28), calls=%async_computation | async-start | bytes 65536 | tf_op jit(solution)/shard_map/all_to_all | solution.py:133
  39.5 65.1 %copy-start.2 = (f32[64,1024]{1,0:T(8,128)S(1)}, f32[64,1024]{1,0:T(8,128)}, u32[]{:S(2)}) copy-start(f32[64,1024]{1,0:T(8,128)} %refs_1_.1) | copy-start | bytes 786436
  39.6 65.1 %all-to-all-start.1 = ((bf16[64,128,128]{2,1,0:T(8,128)(2,1)}), bf16[64,128,128]{2,1,0:T(8,128)(2,1)}, u32[]{:S(2)}, u32[]{:S(2)}) async-start(bf16[64,128,128]{2,1,0:T(8,128)(2,1)} %shard_map.95), calls=%async_computation.1 | async-start | bytes 4194304 | tf_op jit(solution)/shard_map/all_to_all | solution.py:158
  104.7 1.0 copy-start
  107.3 65.4 %all-to-all-start.2 = ((bf16[64,2,64,128]{3,2,1,0:T(8,128)(2,1)}), bf16[64,2,64,128]{3,2,1,0:T(8,128)(2,1)S(1)}, u32[]{:S(2)}, u32[]{:S(2)}) async-start(bf16[64,2,64,128]{3,2,1,0:T(8,128)(2,1)} %broadcast_select_fusion.1), calls=%async_computation.2 | async-start | bytes 4194304 | tf_op jit(solution)/shard_map/all_to_all | solution.py:153
  116.0 10.4 %copy-start.3 = (s32[1,128,2]{1,2,0:T(2,128)S(1)}, s32[1,128,2]{1,2,0:T(2,128)}, u32[]{:S(2)}) copy-start(s32[1,128,2]{1,2,0:T(2,128)} %param.11) | copy-start | bytes 3076
  119.0 18.6 %collective-permute-start = (bf16[16,128,128]{2,1,0:T(8,128)(2,1)S(1)}, bf16[16,128,128]{2,1,0:T(8,128)(2,1)S(1)}, u32[]{:S(2)}, u32[]{:S(2)}) collective-permute-start(bf16[16,128,128]{2,1,0:T(8,128)(2,1)S(1)} %bitcast.44), channel_id=1, source_target_pairs={{0,1},{1,2},{2,3},{3,4},{4,5},{5,6},{6,7},{7,0},{8,9},{9,10},{10,1... | collective-permute-start | bytes 1572872 | tf_op jit(solution)/shard_map/ppermute | solution.py:171
  119.0 22.7 %collective-permute-start.1 = (bf16[16,128,128]{2,1,0:T(8,128)(2,1)S(1)}, bf16[16,128,128]{2,1,0:T(8,128)(2,1)}, u32[]{:S(2)}, u32[]{:S(2)}) collective-permute-start(bf16[16,128,128]{2,1,0:T(8,128)(2,1)S(1)} %bitcast.45), channel_id=1, source_target_pairs={{0,2},{1,3},{2,4},{3,5},{4,6},{5,7},{6,0},{7,1},{8,10},{9,11},{10,... | collective-permute-start | bytes 1572872 | tf_op jit(solution)/shard_map/ppermute | solution.py:171
  122.5 32.9 %collective-permute-start.2 = (bf16[16,128,128]{2,1,0:T(8,128)(2,1)S(1)}, bf16[16,128,128]{2,1,0:T(8,128)(2,1)}, u32[]{:S(2)}, u32[]{:S(2)}) collective-permute-start(bf16[16,128,128]{2,1,0:T(8,128)(2,1)S(1)} %bitcast.46), channel_id=1, source_target_pairs={{0,3},{1,4},{2,5},{3,6},{4,7},{5,0},{6,1},{7,2},{8,11},{9,12},{10,... | collective-permute-start | bytes 1572872 | tf_op jit(solution)/shard_map/ppermute | solution.py:171
  127.7 32.8 %collective-permute-start.3 = (bf16[16,128,128]{2,1,0:T(8,128)(2,1)S(1)}, bf16[16,128,128]{2,1,0:T(8,128)(2,1)}, u32[]{:S(2)}, u32[]{:S(2)}) collective-permute-start(bf16[16,128,128]{2,1,0:T(8,128)(2,1)S(1)} %bitcast.47), channel_id=1, source_target_pairs={{0,4},{1,5},{2,6},{3,7},{4,0},{5,1},{6,2},{7,3},{8,12},{9,13},{10,... | collective-permute-start | bytes 1572872 | tf_op jit(solution)/shard_map/ppermute | solution.py:171
  133.3 32.7 %collective-permute-start.4 = (bf16[16,128,128]{2,1,0:T(8,128)(2,1)S(1)}, bf16[16,128,128]{2,1,0:T(8,128)(2,1)S(1)}, u32[]{:S(2)}, u32[]{:S(2)}) collective-permute-start(bf16[16,128,128]{2,1,0:T(8,128)(2,1)S(1)} %bitcast.48), channel_id=1, source_target_pairs={{0,5},{1,6},{2,7},{3,0},{4,1},{5,2},{6,3},{7,4},{8,13},{9,14},{10,... | collective-permute-start | bytes 1572872 | tf_op jit(solution)/shard_map/ppermute | solution.py:171
  137.6 29.7 %collective-permute-start.5 = (bf16[16,128,128]{2,1,0:T(8,128)(2,1)S(1)}, bf16[16,128,128]{2,1,0:T(8,128)(2,1)S(1)}, u32[]{:S(2)}, u32[]{:S(2)}) collective-permute-start(bf16[16,128,128]{2,1,0:T(8,128)(2,1)S(1)} %bitcast.50), channel_id=1, source_target_pairs={{0,6},{1,7},{2,0},{3,1},{4,2},{5,3},{6,4},{7,5},{8,14},{9,15},{10,... | collective-permute-start | bytes 1572872 | tf_op jit(solution)/shard_map/ppermute | solution.py:171
  141.7 30.1 %collective-permute-start.6 = (bf16[16,128,128]{2,1,0:T(8,128)(2,1)S(1)}, bf16[16,128,128]{2,1,0:T(8,128)(2,1)S(1)}, u32[]{:S(2)}, u32[]{:S(2)}) collective-permute-start(bf16[16,128,128]{2,1,0:T(8,128)(2,1)S(1)} %bitcast.51), channel_id=1, source_target_pairs={{0,7},{1,0},{2,1},{3,2},{4,3},{5,4},{6,5},{7,6},{8,15},{9,8},{10,9... | collective-permute-start | bytes 1572872 | tf_op jit(solution)/shard_map/ppermute | solution.py:171
  172.7 1.4 copy-start.1

commit v9 on v8

--- a/solution.py
+++ b/solution.py
@@ -167,13 +167,16 @@
         preferred_element_type=jnp.float32,
     )
     assembled = assembled.astype(jnp.bfloat16).reshape(slot_count, block_size, block_size)
-    shifted = [assembled] + [
-        lax.ppermute(assembled, "cols", [(i, (i + k) % n_cols) for i in range(n_cols)])
-        for k in range(1, n_cols)
-    ]
-    group_tiles = jnp.concatenate(shifted, axis=0)
+    group_tiles = assembled
+    step = 1
+    while step < n_cols:
+        partner = [(i, i ^ step) for i in range(n_cols)]
+        group_tiles = jnp.concatenate(
+            [group_tiles, lax.ppermute(group_tiles, "cols", partner)], axis=0
+        )
+        step *= 2
     slot_ids = jnp.arange(group_slots, dtype=jnp.int32)
-    shift_of = (lax.axis_index("cols") - slot_ids // slot_count) % n_cols
+    shift_of = lax.bitwise_xor(lax.axis_index("cols"), slot_ids // slot_count)
     tile_index = shift_of * slot_count + slot_ids % slot_count
 
     pattern_flat = jnp.concatenate([pattern[0], tile_index[:, None]], axis=1).reshape(-1)

time: 262 us -> 284 us (1.084)
  the two profiles are of different devices: /device:TPU:24 before, /device:TPU:56 now
where the time goes in v9:
time: 284 us; the launch traced here: 280 us
  waiting for transfers between devices  112 us (39%)
  blocking collectives  61.3 us (22%)
  starting transfers between devices  50.5 us (18%)
  Pallas kernels  28.1 us (10%)
  local copies, waits for them, and re-layouts  17.1 us (6%)
  other arithmetic  7.32 us (3%)
    ppermute x3, waiting for transfers between devices, on_device(): lax.ppermute(group_tiles, 'cols', partner)  63.3 us
    all_to_all x1, blocking collectives, ghosts_of(): lax.all_to_all(outgoing, 'rows', split_axis=0, concat_axis=0, tiled=True)  61.3 us
    all_to_all x1, waiting for transfers between devices, on_device(): lax.all_to_all(send_tiles, 'rows', split_axis=0, concat_axis=0, tiled=True)  48.9 us
    all_to_all x1, starting transfers between devices, on_device(): lax.all_to_all(index_send, 'rows', split_axis=0, concat_axis=0, tiled=True)  15.9 us
    pallas_call x2, Pallas kernels, apply_tiles(): pl.pallas_call(functools.partial(product_kernel, len(fields) == 1), out_s...  14.2 us
    pallas_call x1, Pallas kernels, presum_tiles(): pl.pallas_call(presum_kernel, out_shape=jax.ShapeDtypeStruct((n_rows, blo...  13.9 us
    all_to_all x1, starting transfers between devices, on_device(): lax.all_to_all(send_tiles, 'rows', split_axis=0, concat_axis=0, tiled=True)  12.7 us
    all_to_all x1, starting transfers between devices, ghosts_of(): lax.all_to_all(outgoing, 'rows', split_axis=0, concat_axis=0, tiled=True)  11.6 us
  transfers between devices with their start and end apart: 6, of which 3 were waited for; matrix products, arithmetic and copies ran while one was open for 7% of the time, Pallas kernels for 5%

profile of v9, /device:TPU:56, one launch (start us, length us, event | category | flops | bytes accessed | tf_op | source)
XLA Modules:
  0.0 280.0 jit_solution(15216933504100985160)
XLA Ops:
  2.9 15.9 %all-to-all-start = ((s32[64,1,3]{2,1,0:T(1,128)}), s32[64,1,3]{2,1,0:T(1,128)S(1)}, u32[]{:S(2)}, u32[]{:S(2)}) async-start(s32[64,1,3]{2,1,0:T(1,128)} %copy.28), calls=%async_computation | async-start | bytes 65536 | tf_op jit(solution)/shard_map/all_to_all | solution.py:133
  20.3 2.2 fusion
  22.5 2.6 copy.31
  25.2 13.9 %shard_map.95 = bf16[64,128,128]{2,1,0:T(8,128)(2,1)} custom-call(s32[512]{0:T(512)} %reshape.105.index_ref, bf16[2048,512]{1,0:T(8,128)(2,1)} %bitcast.48, bf16[16,512,128]{2,1,0:T(8,128)(2,1)} %basis_ref.1), custom_call_target="tpu_custom_call" | custom-call | flops 4294967296 | bytes 6291456 | tf_op jit(solution)/shard_map/pallas_call | solution.py:33
  39.1 12.7 %all-to-all-start.1 = ((bf16[64,128,128]{2,1,0:T(8,128)(2,1)}), bf16[64,128,128]{2,1,0:T(8,128)(2,1)S(1)}, u32[]{:S(2)}, u32[]{:S(2)}) async-start(bf16[64,128,128]{2,1,0:T(8,128)(2,1)} %shard_map.95), calls=%async_computation.1 | async-start | bytes 4194304 | tf_op jit(solution)/shard_map/all_to_all | solution.py:158
  52.3 48.9 %all-to-all-done.1 = bf16[64,128,128]{2,1,0:T(8,128)(2,1)S(1)} async-done(((bf16[64,128,128]{2,1,0:T(8,128)(2,1)}), bf16[64,128,128]{2,1,0:T(8,128)(2,1)S(1)}, u32[]{:S(2)}, u32[]{:S(2)}) %all-to-all-start.1) | async-done | bytes 2097184 | tf_op jit(solution)/shard_map/all_to_all | solution.py:158
  101.2 1.2 fusion.3
  102.5 2.1 collective-permute-start
  104.7 1.0 gather_fusion
  105.6 1.6 broadcast_select_fusion.1
  107.2 11.6 %all-to-all-start.2 = ((bf16[64,2,64,128]{3,2,1,0:T(8,128)(2,1)}), bf16[64,2,64,128]{3,2,1,0:T(8,128)(2,1)S(1)}, u32[]{:S(2)}, u32[]{:S(2)}) async-start(bf16[64,2,64,128]{3,2,1,0:T(8,128)(2,1)} %broadcast_select_fusion.1), calls=%async_computation.2 | async-start | bytes 4194304 | tf_op jit(solution)/shard_map/all_to_all | solution.py:153
  118.9 3.3 %collective-permute-start.1 = (bf16[32,128,128]{2,1,0:T(8,128)(2,1)S(1)}, bf16[32,128,128]{2,1,0:T(8,128)(2,1)S(1)}, u32[]{:S(2)}, u32[]{:S(2)}) collective-permute-start(bf16[32,128,128]{2,1,0:T(8,128)(2,1)S(1)} %pad_maximum_fusion.1), channel_id=1, source_target_pairs={{0,2},{1,3},{2,0},{3,1},{4,6},{5,7},{6,4},{7,5},{8,10},{9,11},{10,... | collective-permute-start | bytes 3145736 | tf_op jit(solution)/shard_map/ppermute | solution.py:175
  122.3 23.5 %collective-permute-done.1 = bf16[32,128,128]{2,1,0:T(8,128)(2,1)S(1)} collective-permute-done((bf16[32,128,128]{2,1,0:T(8,128)(2,1)S(1)}, bf16[32,128,128]{2,1,0:T(8,128)(2,1)S(1)}, u32[]{:S(2)}, u32[]{:S(2)}) %collective-permute-start.1) | collective-permute-done | bytes 1048608 | tf_op jit(solution)/shard_map/ppermute | solution.py:175
  145.8 1.7 pad_maximum_fusion
  147.5 4.9 %collective-permute-start.2 = (bf16[64,128,128]{2,1,0:T(8,128)(2,1)}, bf16[64,128,128]{2,1,0:T(8,128)(2,1)}, u32[]{:S(2)}, u32[]{:S(2)}) collective-permute-start(bf16[64,128,128]{2,1,0:T(8,128)(2,1)} %pad_maximum_fusion), channel_id=1, source_target_pairs={{0,4},{1,5},{2,6},{3,7},{4,0},{5,1},{6,2},{7,3},{8,12},{9,13},{10,... | collective-permute-start | bytes 6291464 | tf_op jit(solution)/shard_map/ppermute | solution.py:175
  156.2 0.8 constant_dynamic-update-slice_fusion.2
  157.0 1.1 constant_dynamic-update-slice_fusion.1
  158.1 39.8 %collective-permute-done.2 = bf16[64,128,128]{2,1,0:T(8,128)(2,1)} collective-permute-done((bf16[64,128,128]{2,1,0:T(8,128)(2,1)}, bf16[64,128,128]{2,1,0:T(8,128)(2,1)}, u32[]{:S(2)}, u32[]{:S(2)}) %collective-permute-start.2) | collective-permute-done | bytes 2097184 | tf_op jit(solution)/shard_map/ppermute | solution.py:175
  197.8 3.2 %constant_dynamic-update-slice_fusion.tiles_ref = bf16[128,128,128]{2,1,0:T(8,128)(2,1)} fusion(bf16[128,128,128]{2,1,0:T(8,128)(2,1)} %constant_dynamic-update-slice_fusion.1, bf16[64,128,128]{2,1,0:T(8,128)(2,1)} %collective-permute-done.2), kind=kLoop, calls=%fused_computation.16 | loop fusion | bytes 4194304 | tf_op jit(solution)/shard_map/concatenate | solution.py:174
  201.0 1.3 copy-done.1
  202.3 7.1 %shard_map.96 = (f32[64,1024]{1,0:T(8,128)}, bf16[8,64,128]{2,1,0:T(8,128)(2,1)}) custom-call(s32[384]{0:T(512)} %reshape.104.pattern_ref, f32[2]{0:T(128)} %pad_maximum_fusion.2.scalar_ref, bf16[128,128,128]{2,1,0:T(8,128)(2,1)} %constant_dynamic-update-slice_fusion.tiles_ref, bf16[8,64,128]{2,1,0:T(8,128)(2,1)} %copy-done, bf16[128,64,128]{2,1,0:T(8,128)(2,1)} %bitcast.39, ...), custom_call_target="tpu_custom_call" | custom-call | flops 268435456 | bytes 7077888 | tf_op jit(solution)/shard_map/pallas_call | solution.py:100
  209.4 1.9 gather_fusion.1
  211.5 61.3 %all_to_all.27 = bf16[64,2,64,128]{3,2,1,0:T(8,128)(2,1)} all-to-all(bf16[64,2,64,128]{3,2,1,0:T(8,128)(2,1)S(1)} %broadcast_select_fusion), channel_id=1, replica_groups=mesh['rows'=64,'cols'=8] {'rows'}, dimensions={0} | all-to-all | bytes 4194304 | tf_op jit(solution)/shard_map/all_to_all | solution.py:153
  272.8 7.2 %shard_map.97 = f32[64,1024]{1,0:T(8,128)} custom-call(s32[384]{0:T(512)} %reshape.104.pattern_ref, f32[2]{0:T(128)} %pad_maximum_fusion.2.scalar_ref, bf16[128,128,128]{2,1,0:T(8,128)(2,1)} %constant_dynamic-update-slice_fusion.tiles_ref, bf16[8,64,128]{2,1,0:T(8,128)(2,1)} %get-tuple-element.9.local_ref, bf16[128,64,128]{2,1,0:T(8,128)(2,1)} %bitcast.43, ...), custom_call_target="tpu_custom_call" | custom-call | flops 268435456 | bytes 7077888 | tf_op jit(solution)/shard_map/pallas_call | solution.py:100
  (40 shorter events, 7.1 us)
Async XLA Ops:
  2.9 36.1 %all-to-all-start = ((s32[64,1,3]{2,1,0:T(1,128)}), s32[64,1,3]{2,1,0:T(1,128)S(1)}, u32[]{:S(2)}, u32[]{:S(2)}) async-start(s32[64,1,3]{2,1,0:T(1,128)} %copy.28), calls=%async_computation | async-start | bytes 65536 | tf_op jit(solution)/shard_map/all_to_all | solution.py:133
  39.1 62.1 %all-to-all-start.1 = ((bf16[64,128,128]{2,1,0:T(8,128)(2,1)}), bf16[64,128,128]{2,1,0:T(8,128)(2,1)S(1)}, u32[]{:S(2)}, u32[]{:S(2)}) async-start(bf16[64,128,128]{2,1,0:T(8,128)(2,1)} %shard_map.95), calls=%async_computation.1 | async-start | bytes 4194304 | tf_op jit(solution)/shard_map/all_to_all | solution.py:158
  51.8 52.8 %copy-start.4 = (f32[64,1024]{1,0:T(8,128)S(1)}, f32[64,1024]{1,0:T(8,128)}, u32[]{:S(2)}) copy-start(f32[64,1024]{1,0:T(8,128)} %refs_1_.1) | copy-start | bytes 786436
  102.5 16.3 %collective-permute-start = (bf16[16,128,128]{2,1,0:T(8,128)(2,1)S(1)}, bf16[16,128,128]{2,1,0:T(8,128)(2,1)S(1)}, u32[]{:S(2)}, u32[]{:S(2)}) collective-permute-start(bf16[16,128,128]{2,1,0:T(8,128)(2,1)S(1)} %bitcast.44), channel_id=1, source_target_pairs={{0,1},{1,0},{2,3},{3,2},{4,5},{5,4},{6,7},{7,6},{8,9},{9,8},{10,11... | collective-permute-start | bytes 1572872 | tf_op jit(solution)/shard_map/ppermute | solution.py:175
  104.6 1.0 copy-start
  107.2 93.8 %all-to-all-start.2 = ((bf16[64,2,64,128]{3,2,1,0:T(8,128)(2,1)}), bf16[64,2,64,128]{3,2,1,0:T(8,128)(2,1)S(1)}, u32[]{:S(2)}, u32[]{:S(2)}) async-start(bf16[64,2,64,128]{3,2,1,0:T(8,128)(2,1)} %broadcast_select_fusion.1), calls=%async_computation.2 | async-start | bytes 4194304 | tf_op jit(solution)/shard_map/all_to_all | solution.py:153
  118.9 34.8 %copy-start.5 = (s32[1,128,2]{1,2,0:T(2,128)S(1)}, s32[1,128,2]{1,2,0:T(2,128)}, u32[]{:S(2)}) copy-start(s32[1,128,2]{1,2,0:T(2,128)} %param.11) | copy-start | bytes 3076
  118.9 26.9 %collective-permute-start.1 = (bf16[32,128,128]{2,1,0:T(8,128)(2,1)S(1)}, bf16[32,128,128]{2,1,0:T(8,128)(2,1)S(1)}, u32[]{:S(2)}, u32[]{:S(2)}) collective-permute-start(bf16[32,128,128]{2,1,0:T(8,128)(2,1)S(1)} %pad_maximum_fusion.1), channel_id=1, source_target_pairs={{0,2},{1,3},{2,0},{3,1},{4,6},{5,7},{6,4},{7,5},{8,10},{9,11},{10,... | collective-permute-start | bytes 3145736 | tf_op jit(solution)/shard_map/ppermute | solution.py:175
  145.8 1.7 copy-start.2
  147.5 50.3 %collective-permute-start.2 = (bf16[64,128,128]{2,1,0:T(8,128)(2,1)}, bf16[64,128,128]{2,1,0:T(8,128)(2,1)}, u32[]{:S(2)}, u32[]{:S(2)}) collective-permute-start(bf16[64,128,128]{2,1,0:T(8,128)(2,1)} %pad_maximum_fusion), channel_id=1, source_target_pairs={{0,4},{1,5},{2,6},{3,7},{4,0},{5,1},{6,2},{7,3},{8,12},{9,13},{10,... | collective-permute-start | bytes 6291464 | tf_op jit(solution)/shard_map/ppermute | solution.py:175
  154.7 2.3 copy-start.3
  201.0 1.3 copy-start.1

commit v10 on v7

--- a/solution.py
+++ b/solution.py
@@ -69,12 +69,21 @@
     center = scalar_ref[0]
     half_width = scalar_ref[1]
     if first:
-        state_ref, out_ref, blocks_ref = refs[0], refs[1], refs[2]
+        state_ref, wanted_ref, out_ref, blocks_ref, outgoing_ref = refs[:5]
         for row in range(row_blocks):
             lanes = slice(row * block_size, (row + 1) * block_size)
             term = (acc_ref[row] - center * state_ref[:, lanes]) / half_width
             out_ref[:, lanes] = term
             blocks_ref[row] = term.astype(blocks_ref.dtype)
+        width = outgoing_ref.shape[1]
+
+        def send(e, carry):
+            wanted = wanted_ref[e]
+            block = blocks_ref[jnp.clip(wanted, 0, row_blocks - 1)]
+            outgoing_ref[e // width, e % width] = jnp.where(wanted >= 0, block, jnp.zeros_like(block))
+            return carry
+
+        lax.fori_loop(0, wanted_ref.shape[0], send, 0, unroll=8)
     else:
         first_ref, state_ref, out_ref = refs[0], refs[1], refs[2]
         for row in range(row_blocks):
@@ -85,21 +94,28 @@
             )
 
 
-def apply_tiles(pattern_flat, scalars, tiles, local_blocks, ghost_blocks, fields):
+def apply_tiles(pattern_flat, scalars, tiles, local_blocks, ghost_blocks, fields, width, first=True):
     row_blocks, vec_count, block_size = local_blocks.shape
     slots = tiles.shape[0]
     field = jax.ShapeDtypeStruct((vec_count, row_blocks * block_size), jnp.float32)
-    if len(fields) == 1:
-        out_shape = (field, jax.ShapeDtypeStruct(local_blocks.shape, jnp.bfloat16))
+    vmem = pl.BlockSpec(memory_space=pltpu.VMEM)
+    smem = pl.BlockSpec(memory_space=pltpu.SMEM)
+    if first:
+        peers = fields[1].shape[0] // width
+        out_shape = (
+            field,
+            jax.ShapeDtypeStruct(local_blocks.shape, jnp.bfloat16),
+            jax.ShapeDtypeStruct((peers, width, vec_count, block_size), jnp.bfloat16),
+        )
+        field_specs = [vmem, smem]
     else:
         out_shape = field
-    vmem = pl.BlockSpec(memory_space=pltpu.VMEM)
-    smem = pl.BlockSpec(memory_space=pltpu.SMEM)
+        field_specs = [vmem, vmem]
     return pl.pallas_call(
-        functools.partial(product_kernel, len(fields) == 1),
+        functools.partial(product_kernel, first),
         out_shape=out_shape,
-        in_specs=[smem, smem] + [vmem] * (3 + len(fields)),
-        out_specs=(vmem, vmem) if len(fields) == 1 else vmem,
+        in_specs=[smem, smem, vmem, vmem, vmem] + field_specs,
+        out_specs=(vmem, vmem, vmem) if first else vmem,
         scratch_shapes=[pltpu.VMEM((row_blocks, vec_count, block_size), jnp.float32)],
         cost_estimate=pl.CostEstimate(
             flops=2 * slots * vec_count * block_size * block_size,
@@ -142,21 +158,25 @@
             .transpose(1, 0, 2)
         )
 
-    def ghosts_of(blocks):
-        outgoing = jnp.where(
+    def ghost_payload(blocks):
+        return jnp.where(
             (wanted_by >= 0)[:, :, None, None],
             blocks[jnp.clip(wanted_by, 0, row_blocks - 1)],
             jnp.zeros((), jnp.bfloat16),
         )
+
+    def exchange_ghosts(outgoing):
         arrived = lax.all_to_all(outgoing, "rows", split_axis=0, concat_axis=0, tiled=True)
         return arrived.reshape(n_rows * ghost_width, vec_count, block_size)
+
+    state_blocks = own_blocks(state)
+    state_outgoing = ghost_payload(state_blocks)
 
     weighted = (basis_values.astype(jnp.float32) * potential[None, :, None]).astype(jnp.bfloat16)
     send_tiles = presum_tiles(contrib_index.reshape(-1), basis_values, weighted, n_rows)
     arrived_tiles = lax.all_to_all(send_tiles, "rows", split_axis=0, concat_axis=0, tiled=True)
-    arrived_tiles, state_in = lax.optimization_barrier((arrived_tiles, state))
-    state_blocks = own_blocks(state_in)
-    state_ghosts = ghosts_of(state_blocks)
+    arrived_tiles, state_outgoing = lax.optimization_barrier((arrived_tiles, state_outgoing))
+    state_ghosts = exchange_ghosts(state_outgoing)
     slot_wanted = jnp.arange(slot_count, dtype=jnp.int32)
     selector = (arrived_slots[None, :] == slot_wanted[:, None]).astype(jnp.bfloat16)
     assembled = jnp.dot(
@@ -169,11 +189,18 @@
 
     pattern_flat = pattern.reshape(-1)
     scalars = jnp.stack([center, half_width])
-    first_term, first_blocks = apply_tiles(
-        pattern_flat, scalars, group_tiles, state_blocks, state_ghosts, (state,)
+    first_term, first_blocks, first_outgoing = apply_tiles(
+        pattern_flat, scalars, group_tiles, state_blocks, state_ghosts, (state, wanted_by.reshape(-1)), ghost_width
     )
     second_term = apply_tiles(
-        pattern_flat, scalars, group_tiles, first_blocks, ghosts_of(first_blocks), (first_term, state)
+        pattern_flat,
+        scalars,
+        group_tiles,
+        first_blocks,
+        exchange_ghosts(first_outgoing),
+        (first_term, state),
+        ghost_width,
+        first=False,
     )
     return (first_term, second_term)
 

time: 256 us -> 254 us (level)
  waiting for transfers between devices: 95.1 us -> 88.6 us
    all_to_all x1, waiting for transfers between devices: 49.1 us -> 43.4 us  [on_device(): lax.all_to_all(send_tiles, 'rows', split_axis=0, concat_axis=0, tiled=True)]
  transfers between devices with their start and end apart: 4 -> 4, of which waited for: 2 -> 2; matrix products, arithmetic and copies ran while one was open for 4% -> 6% of each run, Pallas kernels for 5% -> 6%
where the time goes in v10:
time: 254 us; the launch traced here: 251 us
  waiting for transfers between devices  88.6 us (35%)
  blocking collectives  56.2 us (22%)
  starting transfers between devices  40.6 us (16%)
  Pallas kernels  30.3 us (12%)
  between operations  15.4 us (6%)
  local copies, waits for them, and re-layouts  12 us (5%)
  other arithmetic  6.78 us (3%)
    all_to_all x1, blocking collectives, exchange_ghosts(): lax.all_to_all(outgoing, 'rows', split_axis=0, concat_axis=0, tiled=True)  56.2 us
    all_to_all x1, waiting for transfers between devices, exchange_ghosts(): lax.all_to_all(outgoing, 'rows', split_axis=0, concat_axis=0, tiled=True)  45.2 us
    all_to_all x1, waiting for transfers between devices, on_device(): lax.all_to_all(send_tiles, 'rows', split_axis=0, concat_axis=0, tiled=True)  43.4 us
    pallas_call x2, Pallas kernels, apply_tiles(): pl.pallas_call(functools.partial(product_kernel, first), out_shape=out_sh...  16.4 us
    all_to_all x1, starting transfers between devices, on_device(): lax.all_to_all(index_send, 'rows', split_axis=0, concat_axis=0, tiled=True)  15.9 us
    pallas_call x1, Pallas kernels, presum_tiles(): pl.pallas_call(presum_kernel, out_shape=jax.ShapeDtypeStruct((n_rows, blo...  13.9 us
    all_to_all x1, starting transfers between devices, on_device(): lax.all_to_all(send_tiles, 'rows', split_axis=0, concat_axis=0, tiled=True)  12.8 us
    all_to_all x1, starting transfers between devices, exchange_ghosts(): lax.all_to_all(outgoing, 'rows', split_axis=0, concat_axis=0, tiled=True)  11.6 us
  transfers between devices with their start and end apart: 4, of which 2 were waited for; matrix products, arithmetic and copies ran while one was open for 6% of the time, Pallas kernels for 6%

profile of v10, /device:TPU:56, one launch (start us, length us, event | category | flops | bytes accessed | tf_op | source)
XLA Modules:
  0.0 251.1 jit_solution(12605393610995289898)
XLA Ops:
  7.2 0.8 slice_bitcast_fusion.2
  7.9 0.7 compare_select_fusion.1
  8.7 0.7 copy.31
  9.5 15.9 %all-to-all-start = ((s32[64,1,3]{2,1,0:T(1,128)}), s32[64,1,3]{2,1,0:T(1,128)S(1)}, u32[]{:S(2)}, u32[]{:S(2)}) async-start(s32[64,1,3]{2,1,0:T(1,128)} %copy.31), calls=%async_computation | async-start | bytes 65536 | tf_op jit(solution)/shard_map/all_to_all | solution.py:147
  25.4 0.8 copy.33
  26.2 0.7 reshape.50.index_ref
  26.8 2.2 fusion
  29.1 2.6 %copy.34 = bf16[16,128,512]{2,1,0:T(8,128)(2,1)} copy(bf16[16,128,512]{1,2,0:T(8,128)(2,1)S(1)} %fusion) | data formatting | bytes 4194304 | tf_op jit(solution)/shard_map/transpose | solution.py:32
  31.7 13.9 %shard_map.95 = bf16[64,128,128]{2,1,0:T(8,128)(2,1)} custom-call(s32[512]{0:T(512)} %reshape.50.index_ref, bf16[2048,512]{1,0:T(8,128)(2,1)} %bitcast.41, bf16[16,512,128]{2,1,0:T(8,128)(2,1)} %basis_ref.1), custom_call_target="tpu_custom_call" | custom-call | flops 4294967296 | bytes 6291456 | tf_op jit(solution)/shard_map/pallas_call | solution.py:33
  45.6 12.8 %all-to-all-start.1 = ((bf16[64,128,128]{2,1,0:T(8,128)(2,1)}), bf16[64,128,128]{2,1,0:T(8,128)(2,1)S(1)}, u32[]{:S(2)}, u32[]{:S(2)}) async-start(bf16[64,128,128]{2,1,0:T(8,128)(2,1)} %shard_map.95), calls=%async_computation.1 | async-start | bytes 4194304 | tf_op jit(solution)/shard_map/all_to_all | solution.py:177
  59.2 2.1 gather_fusion
  61.3 3.1 %broadcast_select_fusion = bf16[64,2,64,128]{3,2,1,0:T(8,128)(2,1)} fusion(bf16[64,2,64,128]{3,2,1,0:T(8,128)(2,1)} %bitcast.39, pred[64,2]{1,0:T(8,128)(4,1)S(1)} %copy.35), kind=kLoop, calls=%fused_computation.6 | loop fusion | flops 1048576 | bytes 4194432 | tf_op jit(solution)/shard_map/jit(_where)/select_n | solution.py:162
  64.4 43.4 %all-to-all-done.1 = bf16[64,128,128]{2,1,0:T(8,128)(2,1)S(1)} async-done(((bf16[64,128,128]{2,1,0:T(8,128)(2,1)}), bf16[64,128,128]{2,1,0:T(8,128)(2,1)S(1)}, u32[]{:S(2)}, u32[]{:S(2)}) %all-to-all-start.1) | async-done | bytes 2097184 | tf_op jit(solution)/shard_map/all_to_all | solution.py:177
  107.8 1.2 fusion.3
  109.0 0.9 copy.41
  110.0 11.6 %all-to-all-start.2 = ((bf16[64,2,64,128]{3,2,1,0:T(8,128)(2,1)}), bf16[64,2,64,128]{3,2,1,0:T(8,128)(2,1)S(1)}, u32[]{:S(2)}, u32[]{:S(2)}) async-start(bf16[64,2,64,128]{3,2,1,0:T(8,128)(2,1)} %broadcast_select_fusion), calls=%async_computation.2 | async-start | bytes 4194304 | tf_op jit(solution)/shard_map/all_to_all | solution.py:169
  123.0 0.7 reshape.49.pattern_ref
  123.7 0.6 pad_maximum_fusion.scalar_ref
  124.4 0.7 reshape.56.refs_1_
  125.1 45.2 %all-to-all-done.2 = bf16[64,2,64,128]{3,2,1,0:T(8,128)(2,1)S(1)} async-done(((bf16[64,2,64,128]{3,2,1,0:T(8,128)(2,1)}), bf16[64,2,64,128]{3,2,1,0:T(8,128)(2,1)S(1)}, u32[]{:S(2)}, u32[]{:S(2)}) %all-to-all-start.2) | async-done | bytes 2097184 | tf_op jit(solution)/shard_map/all_to_all | solution.py:169
  170.3 1.3 copy-done.1
  171.7 9.3 %shard_map.96 = (f32[64,1024]{1,0:T(8,128)}, bf16[8,64,128]{2,1,0:T(8,128)(2,1)}, bf16[64,2,64,128]{3,2,1,0:T(8,128)(2,1)}) custom-call(s32[256]{0:T(256)} %reshape.49.pattern_ref, f32[2]{0:T(128)} %pad_maximum_fusion.scalar_ref, bf16[128,128,128]{2,1,0:T(8,128)(2,1)} %all-gather.2.cloned.1.call-done.tiles_ref, bf16[8,64,128]{2,1,0:T(8,128)(2,1)} %copy-done, ...), custom_call_target="tpu_custom_call" | custom-call | flops 268435456 | bytes 7077888 | tf_op jit(solution)/shard_map/pallas_call | solution.py:114
  180.9 56.2 %all_to_all.27 = bf16[64,2,64,128]{3,2,1,0:T(8,128)(2,1)} all-to-all(bf16[64,2,64,128]{3,2,1,0:T(8,128)(2,1)} %get-tuple-element.11), channel_id=1, replica_groups=mesh['rows'=64,'cols'=8] {'rows'}, dimensions={0} | all-to-all | bytes 4194304 | tf_op jit(solution)/shard_map/all_to_all | solution.py:169
  237.2 7.1 %shard_map.97 = f32[64,1024]{1,0:T(8,128)} custom-call(s32[256]{0:T(256)} %reshape.49.pattern_ref, f32[2]{0:T(128)} %pad_maximum_fusion.scalar_ref, bf16[128,128,128]{2,1,0:T(8,128)(2,1)} %all-gather.2.cloned.1.call-done.tiles_ref, bf16[8,64,128]{2,1,0:T(8,128)(2,1)} %get-tuple-element.10.local_ref, bf16[128,64,128]{2,1,0:T(8,128)(2,1)} %bitcast.40, ...), custom_call_target="tpu_custom_call" | custom-call | flops 268435456 | bytes 7077888 | tf_op jit(solution)/shard_map/pallas_call | solution.py:114
  (25 shorter events, 1.1 us)
Async XLA Ops:
  9.5 36.1 %all-to-all-start = ((s32[64,1,3]{2,1,0:T(1,128)}), s32[64,1,3]{2,1,0:T(1,128)S(1)}, u32[]{:S(2)}, u32[]{:S(2)}) async-start(s32[64,1,3]{2,1,0:T(1,128)} %copy.31), calls=%async_computation | async-start | bytes 65536 | tf_op jit(solution)/shard_map/all_to_all | solution.py:147
  45.6 13.1 %copy-start.2 = (f32[64,1024]{1,0:T(8,128)S(1)}, f32[64,1024]{1,0:T(8,128)}, u32[]{:S(2)}) copy-start(f32[64,1024]{1,0:T(8,128)} %refs_1_.1) | copy-start | bytes 786436
  45.6 62.2 %all-to-all-start.1 = ((bf16[64,128,128]{2,1,0:T(8,128)(2,1)}), bf16[64,128,128]{2,1,0:T(8,128)(2,1)S(1)}, u32[]{:S(2)}, u32[]{:S(2)}) async-start(bf16[64,128,128]{2,1,0:T(8,128)(2,1)} %shard_map.95), calls=%async_computation.1 | async-start | bytes 4194304 | tf_op jit(solution)/shard_map/all_to_all | solution.py:177
  58.4 111.9 %all-gather.2.cloned.1.call-start = ((), (), s32[]{:S(2)}) async-start(), calls=%async_computation.4 | async-start | bytes 4718592 | tf_op jit(solution)/shard_map/all_gather | solution.py:188
  58.7 2.6 %copy-start = (bf16[8,64,128]{2,1,0:T(8,128)(2,1)}, bf16[8,64,128]{2,1,0:T(8,128)(2,1)S(1)}, u32[]{:S(2)}) copy-start(bf16[8,64,128]{2,1,0:T(8,128)(2,1)S(1)} %bitcast_bitcast_fusion.local_ref) | copy-start | bytes 393220
  110.0 12.9 %copy-start.3 = (s32[1,128,2]{1,2,0:T(2,128)S(1)}, s32[1,128,2]{1,2,0:T(2,128)}, u32[]{:S(2)}) copy-start(s32[1,128,2]{1,2,0:T(2,128)} %param.11) | copy-start | bytes 3076
  110.0 60.4 %all-to-all-start.2 = ((bf16[64,2,64,128]{3,2,1,0:T(8,128)(2,1)}), bf16[64,2,64,128]{3,2,1,0:T(8,128)(2,1)S(1)}, u32[]{:S(2)}, u32[]{:S(2)}) async-start(bf16[64,2,64,128]{3,2,1,0:T(8,128)(2,1)} %broadcast_select_fusion), calls=%async_computation.2 | async-start | bytes 4194304 | tf_op jit(solution)/shard_map/all_to_all | solution.py:169
  170.3 1.3 copy-start.1
Sparse Core Ops, SparseCore 0:
  110.1 37.1 all-gather.1

commit v11 on v10

--- a/solution.py
+++ b/solution.py
@@ -8,8 +8,11 @@
 from jax.sharding import PartitionSpec as P
 
 
-def presum_kernel(index_ref, stacked_ref, basis_ref, out_ref, tiles_ref, acc_ref):
+def presum_kernel(index_ref, potential_ref, basis_ref, out_ref, stacked_ref, tiles_ref, acc_ref):
     blocks, block_size = basis_ref.shape[0], basis_ref.shape[2]
+    for right in range(blocks):
+        weighted = basis_ref[right].astype(jnp.float32) * potential_ref[...]
+        stacked_ref[right * block_size : (right + 1) * block_size] = weighted.T.astype(jnp.bfloat16)
     for left in range(blocks):
         product = jnp.dot(stacked_ref[...], basis_ref[left], preferred_element_type=jnp.float32)
         for right in range(blocks):
@@ -27,9 +30,8 @@
     out_ref[...] = acc_ref[...].astype(out_ref.dtype)
 
 
-def presum_tiles(index_flat, basis, weighted, n_rows):
+def presum_tiles(index_flat, basis, potential, n_rows):
     blocks, points, block_size = basis.shape
-    stacked = weighted.transpose(0, 2, 1).reshape(blocks * block_size, points)
     return pl.pallas_call(
         presum_kernel,
         out_shape=jax.ShapeDtypeStruct((n_rows, block_size, block_size), jnp.bfloat16),
@@ -40,6 +42,7 @@
         ],
         out_specs=pl.BlockSpec(memory_space=pltpu.VMEM),
         scratch_shapes=[
+            pltpu.VMEM((blocks * block_size, points), jnp.bfloat16),
             pltpu.VMEM((blocks, blocks, block_size, block_size), jnp.bfloat16),
             pltpu.VMEM((n_rows, block_size, block_size), jnp.float32),
         ],
@@ -48,7 +51,7 @@
             transcendentals=0,
             bytes_accessed=2 * basis.size * 2 + n_rows * block_size * block_size * 2,
         ),
-    )(index_flat, stacked, basis)
+    )(index_flat, potential[:, None], basis)
 
 
 def product_kernel(first, pattern_ref, scalar_ref, tiles_ref, local_ref, ghost_ref, *refs):
@@ -172,8 +175,7 @@
     state_blocks = own_blocks(state)
     state_outgoing = ghost_payload(state_blocks)
 
-    weighted = (basis_values.astype(jnp.float32) * potential[None, :, None]).astype(jnp.bfloat16)
-    send_tiles = presum_tiles(contrib_index.reshape(-1), basis_values, weighted, n_rows)
+    send_tiles = presum_tiles(contrib_index.reshape(-1), basis_values, potential, n_rows)
     arrived_tiles = lax.all_to_all(send_tiles, "rows", split_axis=0, concat_axis=0, tiled=True)
     arrived_tiles, state_outgoing = lax.optimization_barrier((arrived_tiles, state_outgoing))
     state_ghosts = exchange_ghosts(state_outgoing)

time: 254 us -> 251 us (0.988)
    transpose x1 -> x0, local copies, waits for them, and re-layouts: 2.6 us -> none  [presum_tiles(): stacked = weighted.transpose(0, 2, 1).reshape(blocks * block_size, points)]
  transfers between devices with their start and end apart: 4 -> 4, of which waited for: 2 -> 2; matrix products, arithmetic and copies ran while one was open for 6% -> 4% of each run, Pallas kernels for 6% -> 6%
where the time goes in v11:
time: 251 us; the launch traced here: 248 us
  waiting for transfers between devices  88.6 us (35%)
  blocking collectives  56.3 us (22%)
  starting transfers between devices  40.5 us (16%)
  Pallas kernels  30.8 us (12%)
  between operations  15.4 us (6%)
  local copies, waits for them, and re-layouts  10.9 us (4%)
  other arithmetic  4.57 us (2%)
    all_to_all x1, blocking collectives, exchange_ghosts(): lax.all_to_all(outgoing, 'rows', split_axis=0, concat_axis=0, tiled=True)  56.3 us
    all_to_all x1, waiting for transfers between devices, exchange_ghosts(): lax.all_to_all(outgoing, 'rows', split_axis=0, concat_axis=0, tiled=True)  45.3 us
    all_to_all x1, waiting for transfers between devices, on_device(): lax.all_to_all(send_tiles, 'rows', split_axis=0, concat_axis=0, tiled=True)  43.3 us
    pallas_call x2, Pallas kernels, apply_tiles(): pl.pallas_call(functools.partial(product_kernel, first), out_shape=out_sh...  16.4 us
    all_to_all x1, starting transfers between devices, on_device(): lax.all_to_all(index_send, 'rows', split_axis=0, concat_axis=0, tiled=True)  15.9 us
    pallas_call x1, Pallas kernels, presum_tiles(): pl.pallas_call(presum_kernel, out_shape=jax.ShapeDtypeStruct((n_rows, blo...  14.4 us
    all_to_all x1, starting transfers between devices, on_device(): lax.all_to_all(send_tiles, 'rows', split_axis=0, concat_axis=0, tiled=True)  12.8 us
    all_to_all x1, starting transfers between devices, exchange_ghosts(): lax.all_to_all(outgoing, 'rows', split_axis=0, concat_axis=0, tiled=True)  11.6 us
  transfers between devices with their start and end apart: 4, of which 2 were waited for; matrix products, arithmetic and copies ran while one was open for 4% of the time, Pallas kernels for 6%

profile of v11, /device:TPU:56, one launch (start us, length us, event | category | flops | bytes accessed | tf_op | source)
XLA Modules:
  0.0 248.5 jit_solution(7657353066199012152)
XLA Ops:
  7.2 0.8 slice_bitcast_fusion.2
  7.9 0.7 compare_select_fusion.1
  8.7 0.7 copy.30
  9.5 15.9 %all-to-all-start = ((s32[64,1,3]{2,1,0:T(1,128)}), s32[64,1,3]{2,1,0:T(1,128)S(1)}, u32[]{:S(2)}, u32[]{:S(2)}) async-start(s32[64,1,3]{2,1,0:T(1,128)} %copy.30), calls=%async_computation | async-start | bytes 65536 | tf_op jit(solution)/shard_map/all_to_all | solution.py:150
  25.4 0.8 copy.32
  26.2 0.7 reshape.46.index_ref
  26.9 1.5 copy.33.potential_ref
  28.4 14.4 %shard_map.95 = bf16[64,128,128]{2,1,0:T(8,128)(2,1)} custom-call(s32[512]{0:T(512)} %reshape.46.index_ref, f32[512,1]{1,0:T(8,128)} %copy.33.potential_ref, bf16[16,512,128]{2,1,0:T(8,128)(2,1)} %basis_ref.1), custom_call_target="tpu_custom_call" | custom-call | flops 4294967296 | bytes 6291456 | tf_op jit(solution)/shard_map/pallas_call | solution.py:35
  42.8 12.8 %all-to-all-start.1 = ((bf16[64,128,128]{2,1,0:T(8,128)(2,1)}), bf16[64,128,128]{2,1,0:T(8,128)(2,1)S(1)}, u32[]{:S(2)}, u32[]{:S(2)}) async-start(bf16[64,128,128]{2,1,0:T(8,128)(2,1)} %shard_map.95), calls=%async_computation.1 | async-start | bytes 4194304 | tf_op jit(solution)/shard_map/all_to_all | solution.py:179
  55.7 0.2 all-gather.2.cloned.1.call-start
  56.4 2.1 gather_fusion
  58.5 3.1 %broadcast_select_fusion = bf16[64,2,64,128]{3,2,1,0:T(8,128)(2,1)} fusion(bf16[64,2,64,128]{3,2,1,0:T(8,128)(2,1)} %bitcast.37, pred[64,2]{1,0:T(8,128)(4,1)S(1)} %copy.34), kind=kLoop, calls=%fused_computation.4 | loop fusion | flops 1048576 | bytes 4194432 | tf_op jit(solution)/shard_map/jit(_where)/select_n | solution.py:165
  61.7 43.3 %all-to-all-done.1 = bf16[64,128,128]{2,1,0:T(8,128)(2,1)S(1)} async-done(((bf16[64,128,128]{2,1,0:T(8,128)(2,1)}), bf16[64,128,128]{2,1,0:T(8,128)(2,1)S(1)}, u32[]{:S(2)}, u32[]{:S(2)}) %all-to-all-start.1) | async-done | bytes 2097184 | tf_op jit(solution)/shard_map/all_to_all | solution.py:179
  105.0 1.2 fusion.2
  106.3 0.9 copy.40
  107.2 11.6 %all-to-all-start.2 = ((bf16[64,2,64,128]{3,2,1,0:T(8,128)(2,1)}), bf16[64,2,64,128]{3,2,1,0:T(8,128)(2,1)S(1)}, u32[]{:S(2)}, u32[]{:S(2)}) async-start(bf16[64,2,64,128]{3,2,1,0:T(8,128)(2,1)} %broadcast_select_fusion), calls=%async_computation.2 | async-start | bytes 4194304 | tf_op jit(solution)/shard_map/all_to_all | solution.py:172
  120.2 0.7 reshape.45.pattern_ref
  121.0 0.6 pad_maximum_fusion.scalar_ref
  121.6 0.7 reshape.51.refs_1_
  122.3 45.3 %all-to-all-done.2 = bf16[64,2,64,128]{3,2,1,0:T(8,128)(2,1)S(1)} async-done(((bf16[64,2,64,128]{3,2,1,0:T(8,128)(2,1)}), bf16[64,2,64,128]{3,2,1,0:T(8,128)(2,1)S(1)}, u32[]{:S(2)}, u32[]{:S(2)}) %all-to-all-start.2) | async-done | bytes 2097184 | tf_op jit(solution)/shard_map/all_to_all | solution.py:172
  167.6 1.3 copy-done.1
  168.9 9.3 %shard_map.96 = (f32[64,1024]{1,0:T(8,128)}, bf16[8,64,128]{2,1,0:T(8,128)(2,1)}, bf16[64,2,64,128]{3,2,1,0:T(8,128)(2,1)}) custom-call(s32[256]{0:T(256)} %reshape.45.pattern_ref, f32[2]{0:T(128)} %pad_maximum_fusion.scalar_ref, bf16[128,128,128]{2,1,0:T(8,128)(2,1)} %all-gather.2.cloned.1.call-done.tiles_ref, bf16[8,64,128]{2,1,0:T(8,128)(2,1)} %copy-done, ...), custom_call_target="tpu_custom_call" | custom-call | flops 268435456 | bytes 7077888 | tf_op jit(solution)/shard_map/pallas_call | solution.py:117
  178.2 56.3 %all_to_all.27 = bf16[64,2,64,128]{3,2,1,0:T(8,128)(2,1)} all-to-all(bf16[64,2,64,128]{3,2,1,0:T(8,128)(2,1)} %get-tuple-element.11), channel_id=1, replica_groups=mesh['rows'=64,'cols'=8] {'rows'}, dimensions={0} | all-to-all | bytes 4194304 | tf_op jit(solution)/shard_map/all_to_all | solution.py:172
  234.5 7.1 %shard_map.97 = f32[64,1024]{1,0:T(8,128)} custom-call(s32[256]{0:T(256)} %reshape.45.pattern_ref, f32[2]{0:T(128)} %pad_maximum_fusion.scalar_ref, bf16[128,128,128]{2,1,0:T(8,128)(2,1)} %all-gather.2.cloned.1.call-done.tiles_ref, bf16[8,64,128]{2,1,0:T(8,128)(2,1)} %get-tuple-element.10.local_ref, bf16[128,64,128]{2,1,0:T(8,128)(2,1)} %bitcast.38, ...), custom_call_target="tpu_custom_call" | custom-call | flops 268435456 | bytes 7077888 | tf_op jit(solution)/shard_map/pallas_call | solution.py:117
  (24 shorter events, 0.8 us)
Async XLA Ops:
  9.5 33.4 %all-to-all-start = ((s32[64,1,3]{2,1,0:T(1,128)}), s32[64,1,3]{2,1,0:T(1,128)S(1)}, u32[]{:S(2)}, u32[]{:S(2)}) async-start(s32[64,1,3]{2,1,0:T(1,128)} %copy.30), calls=%async_computation | async-start | bytes 65536 | tf_op jit(solution)/shard_map/all_to_all | solution.py:150
  42.8 13.1 %copy-start.2 = (f32[64,1024]{1,0:T(8,128)S(1)}, f32[64,1024]{1,0:T(8,128)}, u32[]{:S(2)}) copy-start(f32[64,1024]{1,0:T(8,128)} %refs_1_.1) | copy-start | bytes 786436
  42.8 62.2 %all-to-all-start.1 = ((bf16[64,128,128]{2,1,0:T(8,128)(2,1)}), bf16[64,128,128]{2,1,0:T(8,128)(2,1)S(1)}, u32[]{:S(2)}, u32[]{:S(2)}) async-start(bf16[64,128,128]{2,1,0:T(8,128)(2,1)} %shard_map.95), calls=%async_computation.1 | async-start | bytes 4194304 | tf_op jit(solution)/shard_map/all_to_all | solution.py:179
  55.7 111.9 %all-gather.2.cloned.1.call-start = ((), (), s32[]{:S(2)}) async-start(), calls=%async_computation.4 | async-start | bytes 4718592 | tf_op jit(solution)/shard_map/all_gather | solution.py:190
  55.9 2.6 %copy-start = (bf16[8,64,128]{2,1,0:T(8,128)(2,1)}, bf16[8,64,128]{2,1,0:T(8,128)(2,1)S(1)}, u32[]{:S(2)}) copy-start(bf16[8,64,128]{2,1,0:T(8,128)(2,1)S(1)} %bitcast_bitcast_fusion.local_ref) | copy-start | bytes 393220
  107.2 12.9 %copy-start.3 = (s32[1,128,2]{1,2,0:T(2,128)S(1)}, s32[1,128,2]{1,2,0:T(2,128)}, u32[]{:S(2)}) copy-start(s32[1,128,2]{1,2,0:T(2,128)} %param.11) | copy-start | bytes 3076
  107.2 60.4 %all-to-all-start.2 = ((bf16[64,2,64,128]{3,2,1,0:T(8,128)(2,1)}), bf16[64,2,64,128]{3,2,1,0:T(8,128)(2,1)S(1)}, u32[]{:S(2)}, u32[]{:S(2)}) async-start(bf16[64,2,64,128]{3,2,1,0:T(8,128)(2,1)} %broadcast_select_fusion), calls=%async_computation.2 | async-start | bytes 4194304 | tf_op jit(solution)/shard_map/all_to_all | solution.py:172
  167.6 1.3 copy-start.1
Sparse Core Ops, SparseCore 0:
  107.3 37.1 all-gather.1

commit v12 on v11

--- a/solution.py
+++ b/solution.py
@@ -11,8 +11,8 @@
 def presum_kernel(index_ref, potential_ref, basis_ref, out_ref, stacked_ref, tiles_ref, acc_ref):
     blocks, block_size = basis_ref.shape[0], basis_ref.shape[2]
     for right in range(blocks):
-        weighted = basis_ref[right].astype(jnp.float32) * potential_ref[...]
-        stacked_ref[right * block_size : (right + 1) * block_size] = weighted.T.astype(jnp.bfloat16)
+        weighted = basis_ref[right].astype(jnp.float32).T * potential_ref[...]
+        stacked_ref[right * block_size : (right + 1) * block_size] = weighted.astype(jnp.bfloat16)
     for left in range(blocks):
         product = jnp.dot(stacked_ref[...], basis_ref[left], preferred_element_type=jnp.float32)
         for right in range(blocks):
@@ -51,7 +51,7 @@
             transcendentals=0,
             bytes_accessed=2 * basis.size * 2 + n_rows * block_size * block_size * 2,
         ),
-    )(index_flat, potential[:, None], basis)
+    )(index_flat, potential[None, :], basis)
 
 
 def product_kernel(first, pattern_ref, scalar_ref, tiles_ref, local_ref, ghost_ref, *refs):

time: 251 us -> 249 us (level)
  transfers between devices with their start and end apart: 4 -> 4, of which waited for: 2 -> 2; matrix products, arithmetic and copies ran while one was open for 4% -> 4% of each run, Pallas kernels for 6% -> 5%
where the time goes in v12:
time: 249 us; the launch traced here: 246 us
  waiting for transfers between devices  88.8 us (36%)
  blocking collectives  56.2 us (23%)
  starting transfers between devices  40.6 us (16%)
  Pallas kernels  29.8 us (12%)
  between operations  15.4 us (6%)
  local copies, waits for them, and re-layouts  9.37 us (4%)
  other arithmetic  4.57 us (2%)
    all_to_all x1, blocking collectives, exchange_ghosts(): lax.all_to_all(outgoing, 'rows', split_axis=0, concat_axis=0, tiled=True)  56.2 us
    all_to_all x1, waiting for transfers between devices, exchange_ghosts(): lax.all_to_all(outgoing, 'rows', split_axis=0, concat_axis=0, tiled=True)  45.2 us
    all_to_all x1, waiting for transfers between devices, on_device(): lax.all_to_all(send_tiles, 'rows', split_axis=0, concat_axis=0, tiled=True)  43.5 us
    pallas_call x2, Pallas kernels, apply_tiles(): pl.pallas_call(functools.partial(product_kernel, first), out_shape=out_sh...  16.4 us
    all_to_all x1, starting transfers between devices, on_device(): lax.all_to_all(index_send, 'rows', split_axis=0, concat_axis=0, tiled=True)  15.9 us
    pallas_call x1, Pallas kernels, presum_tiles(): pl.pallas_call(presum_kernel, out_shape=jax.ShapeDtypeStruct((n_rows, blo...  13.3 us
    all_to_all x1, starting transfers between devices, on_device(): lax.all_to_all(send_tiles, 'rows', split_axis=0, concat_axis=0, tiled=True)  12.8 us
    all_to_all x1, starting transfers between devices, exchange_ghosts(): lax.all_to_all(outgoing, 'rows', split_axis=0, concat_axis=0, tiled=True)  11.8 us
  transfers between devices with their start and end apart: 4, of which 2 were waited for; matrix products, arithmetic and copies ran while one was open for 4% of the time, Pallas kernels for 5%

profile of v12, /device:TPU:56, one launch (start us, length us, event | category | flops | bytes accessed | tf_op | source)
XLA Modules:
  0.0 245.9 jit_solution(3781810871457196052)
XLA Ops:
  7.2 0.8 slice_bitcast_fusion.2
  7.9 0.7 compare_select_fusion.1
  8.7 0.7 copy.28
  9.5 15.9 %all-to-all-start = ((s32[64,1,3]{2,1,0:T(1,128)}), s32[64,1,3]{2,1,0:T(1,128)S(1)}, u32[]{:S(2)}, u32[]{:S(2)}) async-start(s32[64,1,3]{2,1,0:T(1,128)} %copy.28), calls=%async_computation | async-start | bytes 65536 | tf_op jit(solution)/shard_map/all_to_all | solution.py:150
  25.4 0.8 copy.30
  26.2 0.7 reshape.46.index_ref
  26.8 13.3 %shard_map.95 = bf16[64,128,128]{2,1,0:T(8,128)(2,1)} custom-call(s32[512]{0:T(512)} %reshape.46.index_ref, f32[1,512]{1,0:T(1,128)} %bitcast.44, bf16[16,512,128]{2,1,0:T(8,128)(2,1)} %basis_ref.1), custom_call_target="tpu_custom_call" | custom-call | flops 4294967296 | bytes 6291456 | tf_op jit(solution)/shard_map/pallas_call | solution.py:35
  40.2 12.8 %all-to-all-start.1 = ((bf16[64,128,128]{2,1,0:T(8,128)(2,1)}), bf16[64,128,128]{2,1,0:T(8,128)(2,1)S(1)}, u32[]{:S(2)}, u32[]{:S(2)}) async-start(bf16[64,128,128]{2,1,0:T(8,128)(2,1)} %shard_map.95), calls=%async_computation.1 | async-start | bytes 4194304 | tf_op jit(solution)/shard_map/all_to_all | solution.py:179
  53.2 0.1 copy.31
  53.5 0.1 reshape.55
  53.6 2.1 gather_fusion
  55.7 3.1 %broadcast_select_fusion = bf16[64,2,64,128]{3,2,1,0:T(8,128)(2,1)} fusion(bf16[64,2,64,128]{3,2,1,0:T(8,128)(2,1)} %bitcast.37, pred[64,2]{1,0:T(8,128)(4,1)S(1)} %copy.31), kind=kLoop, calls=%fused_computation.4 | loop fusion | flops 1048576 | bytes 4194432 | tf_op jit(solution)/shard_map/jit(_where)/select_n | solution.py:165
  58.9 43.5 %all-to-all-done.1 = bf16[64,128,128]{2,1,0:T(8,128)(2,1)S(1)} async-done(((bf16[64,128,128]{2,1,0:T(8,128)(2,1)}), bf16[64,128,128]{2,1,0:T(8,128)(2,1)S(1)}, u32[]{:S(2)}, u32[]{:S(2)}) %all-to-all-start.1) | async-done | bytes 2097184 | tf_op jit(solution)/shard_map/all_to_all | solution.py:179
  102.4 1.2 fusion.2
  103.7 0.9 copy.37
  104.6 11.8 %all-to-all-start.2 = ((bf16[64,2,64,128]{3,2,1,0:T(8,128)(2,1)}), bf16[64,2,64,128]{3,2,1,0:T(8,128)(2,1)S(1)}, u32[]{:S(2)}, u32[]{:S(2)}) async-start(bf16[64,2,64,128]{3,2,1,0:T(8,128)(2,1)} %broadcast_select_fusion), calls=%async_computation.2 | async-start | bytes 4194304 | tf_op jit(solution)/shard_map/all_to_all | solution.py:172
  117.8 0.7 reshape.45.pattern_ref
  118.5 0.6 pad_maximum_fusion.scalar_ref
  119.2 0.7 reshape.51.refs_1_
  119.9 45.2 %all-to-all-done.2 = bf16[64,2,64,128]{3,2,1,0:T(8,128)(2,1)S(1)} async-done(((bf16[64,2,64,128]{3,2,1,0:T(8,128)(2,1)}), bf16[64,2,64,128]{3,2,1,0:T(8,128)(2,1)S(1)}, u32[]{:S(2)}, u32[]{:S(2)}) %all-to-all-start.2) | async-done | bytes 2097184 | tf_op jit(solution)/shard_map/all_to_all | solution.py:172
  165.1 1.3 copy-done.1
  166.5 9.3 %shard_map.96 = (f32[64,1024]{1,0:T(8,128)}, bf16[8,64,128]{2,1,0:T(8,128)(2,1)}, bf16[64,2,64,128]{3,2,1,0:T(8,128)(2,1)}) custom-call(s32[256]{0:T(256)} %reshape.45.pattern_ref, f32[2]{0:T(128)} %pad_maximum_fusion.scalar_ref, bf16[128,128,128]{2,1,0:T(8,128)(2,1)} %all-gather.2.cloned.1.call-done.tiles_ref, bf16[8,64,128]{2,1,0:T(8,128)(2,1)} %copy-done, ...), custom_call_target="tpu_custom_call" | custom-call | flops 268435456 | bytes 7077888 | tf_op jit(solution)/shard_map/pallas_call | solution.py:117
  175.7 56.2 %all_to_all.27 = bf16[64,2,64,128]{3,2,1,0:T(8,128)(2,1)} all-to-all(bf16[64,2,64,128]{3,2,1,0:T(8,128)(2,1)} %get-tuple-element.11), channel_id=1, replica_groups=mesh['rows'=64,'cols'=8] {'rows'}, dimensions={0} | all-to-all | bytes 4194304 | tf_op jit(solution)/shard_map/all_to_all | solution.py:172
  231.9 7.2 %shard_map.97 = f32[64,1024]{1,0:T(8,128)} custom-call(s32[256]{0:T(256)} %reshape.45.pattern_ref, f32[2]{0:T(128)} %pad_maximum_fusion.scalar_ref, bf16[128,128,128]{2,1,0:T(8,128)(2,1)} %all-gather.2.cloned.1.call-done.tiles_ref, bf16[8,64,128]{2,1,0:T(8,128)(2,1)} %get-tuple-element.10.local_ref, bf16[128,64,128]{2,1,0:T(8,128)(2,1)} %bitcast.38, ...), custom_call_target="tpu_custom_call" | custom-call | flops 268435456 | bytes 7077888 | tf_op jit(solution)/shard_map/pallas_call | solution.py:117
  (23 shorter events, 0.6 us)
Async XLA Ops:
  9.5 30.7 %all-to-all-start = ((s32[64,1,3]{2,1,0:T(1,128)}), s32[64,1,3]{2,1,0:T(1,128)S(1)}, u32[]{:S(2)}, u32[]{:S(2)}) async-start(s32[64,1,3]{2,1,0:T(1,128)} %copy.28), calls=%async_computation | async-start | bytes 65536 | tf_op jit(solution)/shard_map/all_to_all | solution.py:150
  40.2 12.9 %copy-start.2 = (f32[64,1024]{1,0:T(8,128)S(1)}, f32[64,1024]{1,0:T(8,128)}, u32[]{:S(2)}) copy-start(f32[64,1024]{1,0:T(8,128)} %refs_1_.1) | copy-start | bytes 786436
  40.2 62.2 %all-to-all-start.1 = ((bf16[64,128,128]{2,1,0:T(8,128)(2,1)}), bf16[64,128,128]{2,1,0:T(8,128)(2,1)S(1)}, u32[]{:S(2)}, u32[]{:S(2)}) async-start(bf16[64,128,128]{2,1,0:T(8,128)(2,1)} %shard_map.95), calls=%async_computation.1 | async-start | bytes 4194304 | tf_op jit(solution)/shard_map/all_to_all | solution.py:179
  53.0 112.1 %all-gather.2.cloned.1.call-start = ((), (), s32[]{:S(2)}) async-start(), calls=%async_computation.4 | async-start | bytes 4718592 | tf_op jit(solution)/shard_map/all_gather | solution.py:190
  53.1 2.6 %copy-start = (bf16[8,64,128]{2,1,0:T(8,128)(2,1)}, bf16[8,64,128]{2,1,0:T(8,128)(2,1)S(1)}, u32[]{:S(2)}) copy-start(bf16[8,64,128]{2,1,0:T(8,128)(2,1)S(1)} %bitcast_bitcast_fusion.local_ref) | copy-start | bytes 393220
  104.6 13.1 %copy-start.3 = (s32[1,128,2]{1,2,0:T(2,128)S(1)}, s32[1,128,2]{1,2,0:T(2,128)}, u32[]{:S(2)}) copy-start(s32[1,128,2]{1,2,0:T(2,128)} %param.11) | copy-start | bytes 3076
  104.6 60.5 %all-to-all-start.2 = ((bf16[64,2,64,128]{3,2,1,0:T(8,128)(2,1)}), bf16[64,2,64,128]{3,2,1,0:T(8,128)(2,1)S(1)}, u32[]{:S(2)}, u32[]{:S(2)}) async-start(bf16[64,2,64,128]{3,2,1,0:T(8,128)(2,1)} %broadcast_select_fusion), calls=%async_computation.2 | async-start | bytes 4194304 | tf_op jit(solution)/shard_map/all_to_all | solution.py:172
  165.1 1.3 copy-start.1
Sparse Core Ops, SparseCore 0:
  104.7 37.0 all-gather.1

commit v13 on v12

--- a/solution.py
+++ b/solution.py
@@ -22,15 +22,15 @@
     acc_ref[...] = jnp.zeros_like(acc_ref)
 
     def body(s, carry):
-        target = index_ref[4 * s]
-        acc_ref[target] += tiles_ref[index_ref[4 * s + 2], index_ref[4 * s + 3]].astype(jnp.float32)
+        target = index_ref[s, 0]
+        acc_ref[target] += tiles_ref[index_ref[s, 2], index_ref[s, 3]].astype(jnp.float32)
         return carry
 
-    lax.fori_loop(0, index_ref.shape[0] // 4, body, 0, unroll=8)
+    lax.fori_loop(0, index_ref.shape[0], body, 0, unroll=8)
     out_ref[...] = acc_ref[...].astype(out_ref.dtype)
 
 
-def presum_tiles(index_flat, basis, potential, n_rows):
+def presum_tiles(index, basis, potential, n_rows):
     blocks, points, block_size = basis.shape
     return pl.pallas_call(
         presum_kernel,
@@ -51,7 +51,7 @@
             transcendentals=0,
             bytes_accessed=2 * basis.size * 2 + n_rows * block_size * block_size * 2,
         ),
-    )(index_flat, potential[None, :], basis)
+    )(index, potential[None, :], basis)
 
 
 def product_kernel(first, pattern_ref, scalar_ref, tiles_ref, local_ref, ghost_ref, *refs):
@@ -175,7 +175,7 @@
     state_blocks = own_blocks(state)
     state_outgoing = ghost_payload(state_blocks)
 
-    send_tiles = presum_tiles(contrib_index.reshape(-1), basis_values, potential, n_rows)
+    send_tiles = presum_tiles(contrib_index, basis_values, potential, n_rows)
     arrived_tiles = lax.all_to_all(send_tiles, "rows", split_axis=0, concat_axis=0, tiled=True)
     arrived_tiles, state_outgoing = lax.optimization_barrier((arrived_tiles, state_outgoing))
     state_ghosts = exchange_ghosts(state_outgoing)

time: 249 us -> 249 us (level)
  no operation moved by 1% of the time
where the time goes in v13:
time: 249 us; the launch traced here: 246 us
  waiting for transfers between devices  88.8 us (36%)
  blocking collectives  56.3 us (23%)
  starting transfers between devices  40.5 us (16%)
  Pallas kernels  29.9 us (12%)
  between operations  15.4 us (6%)
  local copies, waits for them, and re-layouts  9.31 us (4%)
  other arithmetic  4.57 us (2%)
    all_to_all x1, blocking collectives, exchange_ghosts(): lax.all_to_all(outgoing, 'rows', split_axis=0, concat_axis=0, tiled=True)  56.3 us
    all_to_all x1, waiting for transfers between devices, exchange_ghosts(): lax.all_to_all(outgoing, 'rows', split_axis=0, concat_axis=0, tiled=True)  45.3 us
    all_to_all x1, waiting for transfers between devices, on_device(): lax.all_to_all(send_tiles, 'rows', split_axis=0, concat_axis=0, tiled=True)  43.5 us
    pallas_call x2, Pallas kernels, apply_tiles(): pl.pallas_call(functools.partial(product_kernel, first), out_shape=out_sh...  16.4 us
    all_to_all x1, starting transfers between devices, on_device(): lax.all_to_all(index_send, 'rows', split_axis=0, concat_axis=0, tiled=True)  15.9 us
    pallas_call x1, Pallas kernels, presum_tiles(): pl.pallas_call(presum_kernel, out_shape=jax.ShapeDtypeStruct((n_rows, blo...  13.5 us
    all_to_all x1, starting transfers between devices, on_device(): lax.all_to_all(send_tiles, 'rows', split_axis=0, concat_axis=0, tiled=True)  12.8 us
    all_to_all x1, starting transfers between devices, exchange_ghosts(): lax.all_to_all(outgoing, 'rows', split_axis=0, concat_axis=0, tiled=True)  11.7 us
  transfers between devices with their start and end apart: 4, of which 2 were waited for; matrix products, arithmetic and copies ran while one was open for 4% of the time, Pallas kernels for 5%

profile of v13, /device:TPU:56, one launch (start us, length us, event | category | flops | bytes accessed | tf_op | source)
XLA Modules:
  0.0 246.0 jit_solution(7588064497896301805)
XLA Ops:
  7.2 0.8 slice_bitcast_fusion.2
  7.9 0.7 compare_select_fusion.1
  8.7 0.7 copy.29
  9.5 15.9 %all-to-all-start = ((s32[64,1,3]{2,1,0:T(1,128)}), s32[64,1,3]{2,1,0:T(1,128)S(1)}, u32[]{:S(2)}, u32[]{:S(2)}) async-start(s32[64,1,3]{2,1,0:T(1,128)} %copy.29), calls=%async_computation | async-start | bytes 65536 | tf_op jit(solution)/shard_map/all_to_all | solution.py:150
  25.4 1.4 copy.31.index_ref
  26.8 13.5 %shard_map.95 = bf16[64,128,128]{2,1,0:T(8,128)(2,1)} custom-call(s32[128,4]{1,0:T(8,128)} %copy.31.index_ref, f32[1,512]{1,0:T(1,128)} %bitcast.44, bf16[16,512,128]{2,1,0:T(8,128)(2,1)} %basis_ref.1), custom_call_target="tpu_custom_call" | custom-call | flops 4294967296 | bytes 6291456 | tf_op jit(solution)/shard_map/pallas_call | solution.py:35
  40.3 12.8 %all-to-all-start.1 = ((bf16[64,128,128]{2,1,0:T(8,128)(2,1)}), bf16[64,128,128]{2,1,0:T(8,128)(2,1)S(1)}, u32[]{:S(2)}, u32[]{:S(2)}) async-start(bf16[64,128,128]{2,1,0:T(8,128)(2,1)} %shard_map.95), calls=%async_computation.1 | async-start | bytes 4194304 | tf_op jit(solution)/shard_map/all_to_all | solution.py:179
  53.3 0.1 copy.32
  53.5 0.1 reshape.51
  53.7 2.1 gather_fusion
  55.8 3.1 %broadcast_select_fusion = bf16[64,2,64,128]{3,2,1,0:T(8,128)(2,1)} fusion(bf16[64,2,64,128]{3,2,1,0:T(8,128)(2,1)} %bitcast.37, pred[64,2]{1,0:T(8,128)(4,1)S(1)} %copy.32), kind=kLoop, calls=%fused_computation.4 | loop fusion | flops 1048576 | bytes 4194432 | tf_op jit(solution)/shard_map/jit(_where)/select_n | solution.py:165
  59.0 43.5 %all-to-all-done.1 = bf16[64,128,128]{2,1,0:T(8,128)(2,1)S(1)} async-done(((bf16[64,128,128]{2,1,0:T(8,128)(2,1)}), bf16[64,128,128]{2,1,0:T(8,128)(2,1)S(1)}, u32[]{:S(2)}, u32[]{:S(2)}) %all-to-all-start.1) | async-done | bytes 2097184 | tf_op jit(solution)/shard_map/all_to_all | solution.py:179
  102.5 1.2 fusion.2
  103.7 0.9 copy.38
  104.6 11.7 %all-to-all-start.2 = ((bf16[64,2,64,128]{3,2,1,0:T(8,128)(2,1)}), bf16[64,2,64,128]{3,2,1,0:T(8,128)(2,1)S(1)}, u32[]{:S(2)}, u32[]{:S(2)}) async-start(bf16[64,2,64,128]{3,2,1,0:T(8,128)(2,1)} %broadcast_select_fusion), calls=%async_computation.2 | async-start | bytes 4194304 | tf_op jit(solution)/shard_map/all_to_all | solution.py:172
  117.7 0.1 copy.28
  117.8 0.7 reshape.42.pattern_ref
  118.6 0.6 pad_maximum_fusion.scalar_ref
  119.2 0.7 reshape.47.refs_1_
  119.9 45.3 %all-to-all-done.2 = bf16[64,2,64,128]{3,2,1,0:T(8,128)(2,1)S(1)} async-done(((bf16[64,2,64,128]{3,2,1,0:T(8,128)(2,1)}), bf16[64,2,64,128]{3,2,1,0:T(8,128)(2,1)S(1)}, u32[]{:S(2)}, u32[]{:S(2)}) %all-to-all-start.2) | async-done | bytes 2097184 | tf_op jit(solution)/shard_map/all_to_all | solution.py:172
  165.2 1.3 copy-done.1
  166.5 9.3 %shard_map.96 = (f32[64,1024]{1,0:T(8,128)}, bf16[8,64,128]{2,1,0:T(8,128)(2,1)}, bf16[64,2,64,128]{3,2,1,0:T(8,128)(2,1)}) custom-call(s32[256]{0:T(256)} %reshape.42.pattern_ref, f32[2]{0:T(128)} %pad_maximum_fusion.scalar_ref, bf16[128,128,128]{2,1,0:T(8,128)(2,1)} %all-gather.2.cloned.1.call-done.tiles_ref, bf16[8,64,128]{2,1,0:T(8,128)(2,1)} %copy-done, ...), custom_call_target="tpu_custom_call" | custom-call | flops 268435456 | bytes 7077888 | tf_op jit(solution)/shard_map/pallas_call | solution.py:117
  175.8 56.3 %all_to_all.27 = bf16[64,2,64,128]{3,2,1,0:T(8,128)(2,1)} all-to-all(bf16[64,2,64,128]{3,2,1,0:T(8,128)(2,1)} %get-tuple-element.11), channel_id=1, replica_groups=mesh['rows'=64,'cols'=8] {'rows'}, dimensions={0} | all-to-all | bytes 4194304 | tf_op jit(solution)/shard_map/all_to_all | solution.py:172
  232.1 7.1 %shard_map.97 = f32[64,1024]{1,0:T(8,128)} custom-call(s32[256]{0:T(256)} %reshape.42.pattern_ref, f32[2]{0:T(128)} %pad_maximum_fusion.scalar_ref, bf16[128,128,128]{2,1,0:T(8,128)(2,1)} %all-gather.2.cloned.1.call-done.tiles_ref, bf16[8,64,128]{2,1,0:T(8,128)(2,1)} %get-tuple-element.10.local_ref, bf16[128,64,128]{2,1,0:T(8,128)(2,1)} %bitcast.38, ...), custom_call_target="tpu_custom_call" | custom-call | flops 268435456 | bytes 7077888 | tf_op jit(solution)/shard_map/pallas_call | solution.py:117
  (22 shorter events, 0.5 us)
Async XLA Ops:
  9.5 30.8 %all-to-all-start = ((s32[64,1,3]{2,1,0:T(1,128)}), s32[64,1,3]{2,1,0:T(1,128)S(1)}, u32[]{:S(2)}, u32[]{:S(2)}) async-start(s32[64,1,3]{2,1,0:T(1,128)} %copy.29), calls=%async_computation | async-start | bytes 65536 | tf_op jit(solution)/shard_map/all_to_all | solution.py:150
  40.3 12.9 %copy-start.2 = (f32[64,1024]{1,0:T(8,128)S(1)}, f32[64,1024]{1,0:T(8,128)}, u32[]{:S(2)}) copy-start(f32[64,1024]{1,0:T(8,128)} %refs_1_.1) | copy-start | bytes 786436
  40.3 62.2 %all-to-all-start.1 = ((bf16[64,128,128]{2,1,0:T(8,128)(2,1)}), bf16[64,128,128]{2,1,0:T(8,128)(2,1)S(1)}, u32[]{:S(2)}, u32[]{:S(2)}) async-start(bf16[64,128,128]{2,1,0:T(8,128)(2,1)} %shard_map.95), calls=%async_computation.1 | async-start | bytes 4194304 | tf_op jit(solution)/shard_map/all_to_all | solution.py:179
  53.1 112.1 %all-gather.2.cloned.1.call-start = ((), (), s32[]{:S(2)}) async-start(), calls=%async_computation.4 | async-start | bytes 4718592 | tf_op jit(solution)/shard_map/all_gather | solution.py:190
  53.2 2.6 %copy-start = (bf16[8,64,128]{2,1,0:T(8,128)(2,1)}, bf16[8,64,128]{2,1,0:T(8,128)(2,1)S(1)}, u32[]{:S(2)}) copy-start(bf16[8,64,128]{2,1,0:T(8,128)(2,1)S(1)} %bitcast_bitcast_fusion.local_ref) | copy-start | bytes 393220
  104.6 13.1 %copy-start.3 = (s32[1,128,2]{1,2,0:T(2,128)S(1)}, s32[1,128,2]{1,2,0:T(2,128)}, u32[]{:S(2)}) copy-start(s32[1,128,2]{1,2,0:T(2,128)} %param.11) | copy-start | bytes 3076
  104.6 60.5 %all-to-all-start.2 = ((bf16[64,2,64,128]{3,2,1,0:T(8,128)(2,1)}), bf16[64,2,64,128]{3,2,1,0:T(8,128)(2,1)S(1)}, u32[]{:S(2)}, u32[]{:S(2)}) async-start(bf16[64,2,64,128]{3,2,1,0:T(8,128)(2,1)} %broadcast_select_fusion), calls=%async_computation.2 | async-start | bytes 4194304 | tf_op jit(solution)/shard_map/all_to_all | solution.py:172
  165.2 1.3 copy-start.1
Sparse Core Ops, SparseCore 0:
  104.8 37.1 all-gather.1

commit v14 on v12

--- a/solution.py
+++ b/solution.py
@@ -46,6 +46,7 @@
             pltpu.VMEM((blocks, blocks, block_size, block_size), jnp.bfloat16),
             pltpu.VMEM((n_rows, block_size, block_size), jnp.float32),
         ],
+        compiler_params=pltpu.CompilerParams(vmem_limit_bytes=24 * 1024 * 1024),
         cost_estimate=pl.CostEstimate(
             flops=2 * blocks * blocks * points * block_size * block_size,
             transcendentals=0,
@@ -120,6 +121,7 @@
         in_specs=[smem, smem, vmem, vmem, vmem] + field_specs,
         out_specs=(vmem, vmem, vmem) if first else vmem,
         scratch_shapes=[pltpu.VMEM((row_blocks, vec_count, block_size), jnp.float32)],
+        compiler_params=pltpu.CompilerParams(vmem_limit_bytes=16 * 1024 * 1024),
         cost_estimate=pl.CostEstimate(
             flops=2 * slots * vec_count * block_size * block_size,
             transcendentals=0,

time: 249 us -> 244 us (0.980)
  Pallas kernels: 29.8 us -> 23.1 us
    pallas_call x2, Pallas kernels: 16.4 us -> 10.7 us  [apply_tiles(): pl.pallas_call(functools.partial(product_kernel, first), out_shape=out_sh...]
    unnamed x11 -> x15, local copies, waits for them, and re-layouts: 3.15 us -> 6.28 us
  transfers between devices with their start and end apart: 4 -> 4, of which waited for: 2 -> 2; matrix products, arithmetic and copies ran while one was open for 4% -> 3% of each run, Pallas kernels for 5% -> 5%
where the time goes in v14:
time: 244 us; the launch traced here: 242 us
  waiting for transfers between devices  90.5 us (37%)
  blocking collectives  56.1 us (23%)
  starting transfers between devices  40.5 us (17%)
  Pallas kernels  23.1 us (9%)
  between operations  15.4 us (6%)
  local copies, waits for them, and re-layouts  10.8 us (4%)
  other arithmetic  4.08 us (2%)
    all_to_all x1, blocking collectives, exchange_ghosts(): lax.all_to_all(outgoing, 'rows', split_axis=0, concat_axis=0, tiled=True)  56.1 us
    all_to_all x1, waiting for transfers between devices, exchange_ghosts(): lax.all_to_all(outgoing, 'rows', split_axis=0, concat_axis=0, tiled=True)  46.9 us
    all_to_all x1, waiting for transfers between devices, on_device(): lax.all_to_all(send_tiles, 'rows', split_axis=0, concat_axis=0, tiled=True)  43.5 us
    all_to_all x1, starting transfers between devices, on_device(): lax.all_to_all(index_send, 'rows', split_axis=0, concat_axis=0, tiled=True)  15.9 us
    all_to_all x1, starting transfers between devices, on_device(): lax.all_to_all(send_tiles, 'rows', split_axis=0, concat_axis=0, tiled=True)  12.8 us
    pallas_call x1, Pallas kernels, presum_tiles(): pl.pallas_call(presum_kernel, out_shape=jax.ShapeDtypeStruct((n_rows, blo...  12.4 us
    all_to_all x1, starting transfers between devices, exchange_ghosts(): lax.all_to_all(outgoing, 'rows', split_axis=0, concat_axis=0, tiled=True)  11.8 us
    pallas_call x2, Pallas kernels, apply_tiles(): pl.pallas_call(functools.partial(product_kernel, first), out_shape=out_sh...  10.7 us
  transfers between devices with their start and end apart: 4, of which 2 were waited for; matrix products, arithmetic and copies ran while one was open for 3% of the time, Pallas kernels for 5%

profile of v14, /device:TPU:56, one launch (start us, length us, event | category | flops | bytes accessed | tf_op | source)
XLA Modules:
  0.0 241.8 jit_solution(823943725232593546)
XLA Ops:
  7.2 0.8 slice_bitcast_fusion.2
  7.9 0.7 compare_select_fusion.1
  8.7 0.7 copy.28
  9.5 15.9 %all-to-all-start = ((s32[64,1,3]{2,1,0:T(1,128)}), s32[64,1,3]{2,1,0:T(1,128)S(1)}, u32[]{:S(2)}, u32[]{:S(2)}) async-start(s32[64,1,3]{2,1,0:T(1,128)} %copy.28), calls=%async_computation | async-start | bytes 65536 | tf_op jit(solution)/shard_map/all_to_all | solution.py:152
  25.4 0.8 copy.30
  26.3 1.6 copy-done.3
  27.9 0.7 copy-done.4
  28.5 12.4 %shard_map.95 = bf16[64,128,128]{2,1,0:T(8,128)(2,1)} custom-call(s32[512]{0:T(512)S(1)} %reshape.46.index_ref, f32[1,512]{1,0:T(1,128)S(1)} %bitcast.37, bf16[16,512,128]{2,1,0:T(8,128)(2,1)S(1)} %copy-done.3), custom_call_target="tpu_custom_call" | custom-call | flops 4294967296 | bytes 6291456 | tf_op jit(solution)/shard_map/pallas_call | solution.py:35
  40.9 12.8 %all-to-all-start.1 = ((bf16[64,128,128]{2,1,0:T(8,128)(2,1)}), bf16[64,128,128]{2,1,0:T(8,128)(2,1)S(1)}, u32[]{:S(2)}, u32[]{:S(2)}) async-start(bf16[64,128,128]{2,1,0:T(8,128)(2,1)} %shard_map.95), calls=%async_computation.1 | async-start | bytes 4194304 | tf_op jit(solution)/shard_map/all_to_all | solution.py:181
  53.9 0.1 copy.31
  54.2 0.1 reshape.55
  54.3 2.1 gather_fusion
  56.5 3.2 %broadcast_select_fusion = bf16[64,2,64,128]{3,2,1,0:T(8,128)(2,1)} fusion(bf16[64,2,64,128]{3,2,1,0:T(8,128)(2,1)} %bitcast.39, pred[64,2]{1,0:T(8,128)(4,1)S(1)} %copy.31), kind=kLoop, calls=%fused_computation.4 | loop fusion | flops 1048576 | bytes 4194432 | tf_op jit(solution)/shard_map/jit(_where)/select_n | solution.py:167
  59.6 43.5 %all-to-all-done.1 = bf16[64,128,128]{2,1,0:T(8,128)(2,1)S(1)} async-done(((bf16[64,128,128]{2,1,0:T(8,128)(2,1)}), bf16[64,128,128]{2,1,0:T(8,128)(2,1)S(1)}, u32[]{:S(2)}, u32[]{:S(2)}) %all-to-all-start.1) | async-done | bytes 2097184 | tf_op jit(solution)/shard_map/all_to_all | solution.py:181
  103.2 1.2 fusion.2
  104.4 0.9 copy.37
  105.3 11.8 %all-to-all-start.2 = ((bf16[64,2,64,128]{3,2,1,0:T(8,128)(2,1)}), bf16[64,2,64,128]{3,2,1,0:T(8,128)(2,1)S(1)}, u32[]{:S(2)}, u32[]{:S(2)}) async-start(bf16[64,2,64,128]{3,2,1,0:T(8,128)(2,1)} %broadcast_select_fusion), calls=%async_computation.2 | async-start | bytes 4194304 | tf_op jit(solution)/shard_map/all_to_all | solution.py:174
  118.5 0.1 reshape.45.pattern_ref
  118.8 0.1 reshape.51.refs_1_
  119.0 46.9 %all-to-all-done.2 = bf16[64,2,64,128]{3,2,1,0:T(8,128)(2,1)S(1)} async-done(((bf16[64,2,64,128]{3,2,1,0:T(8,128)(2,1)}), bf16[64,2,64,128]{3,2,1,0:T(8,128)(2,1)S(1)}, u32[]{:S(2)}, u32[]{:S(2)}) %all-to-all-start.2) | async-done | bytes 2097184 | tf_op jit(solution)/shard_map/all_to_all | solution.py:174
  165.9 2.2 copy-done
  168.1 6.1 %shard_map.96 = (f32[64,1024]{1,0:T(8,128)}, bf16[8,64,128]{2,1,0:T(8,128)(2,1)S(1)}, bf16[64,2,64,128]{3,2,1,0:T(8,128)(2,1)S(1)}) custom-call(s32[256]{0:T(256)S(1)} %reshape.45.pattern_ref, f32[2]{0:T(128)S(1)} %pad_maximum_fusion.scalar_ref, bf16[128,128,128]{2,1,0:T(8,128)(2,1)S(1)} %copy-done, bf16[8,64,128]{2,1,0:T(8,128)(2,1)S(1)} %bitcast_bitcast_fusion.local_ref, ...), custom_call_target="tpu_custom_call" | custom-call | flops 268435456 | bytes 7077888 | tf_op jit(solution)/shard_map/pallas_call | solution.py:118
  174.2 56.1 %all_to_all.27 = bf16[64,2,64,128]{3,2,1,0:T(8,128)(2,1)S(1)} all-to-all(bf16[64,2,64,128]{3,2,1,0:T(8,128)(2,1)S(1)} %get-tuple-element.11), channel_id=1, replica_groups=mesh['rows'=64,'cols'=8] {'rows'}, dimensions={0} | all-to-all | bytes 4194304 | tf_op jit(solution)/shard_map/all_to_all | solution.py:174
  230.3 4.7 %shard_map.97 = f32[64,1024]{1,0:T(8,128)} custom-call(s32[256]{0:T(256)S(1)} %reshape.45.pattern_ref, f32[2]{0:T(128)S(1)} %pad_maximum_fusion.scalar_ref, bf16[128,128,128]{2,1,0:T(8,128)(2,1)S(1)} %copy-done, bf16[8,64,128]{2,1,0:T(8,128)(2,1)S(1)} %get-tuple-element.10.local_ref, bf16[128,64,128]{2,1,0:T(8,128)(2,1)S(1)} %bitcast.36, ...), custom_call_target="tpu_custom_call" | custom-call | flops 268435456 | bytes 7077888 | tf_op jit(solution)/shard_map/pallas_call | solution.py:118
  (27 shorter events, 0.8 us)
Async XLA Ops:
  9.5 31.5 %all-to-all-start = ((s32[64,1,3]{2,1,0:T(1,128)}), s32[64,1,3]{2,1,0:T(1,128)S(1)}, u32[]{:S(2)}, u32[]{:S(2)}) async-start(s32[64,1,3]{2,1,0:T(1,128)} %copy.28), calls=%async_computation | async-start | bytes 65536 | tf_op jit(solution)/shard_map/all_to_all | solution.py:152
  26.3 1.6 copy-start.3
  27.9 0.7 copy-start.4
  40.9 12.9 %copy-start.1 = (f32[64,1024]{1,0:T(8,128)S(1)}, f32[64,1024]{1,0:T(8,128)}, u32[]{:S(2)}) copy-start(f32[64,1024]{1,0:T(8,128)} %refs_1_.1) | copy-start | bytes 786436
  40.9 62.2 %all-to-all-start.1 = ((bf16[64,128,128]{2,1,0:T(8,128)(2,1)}), bf16[64,128,128]{2,1,0:T(8,128)(2,1)S(1)}, u32[]{:S(2)}, u32[]{:S(2)}) async-start(bf16[64,128,128]{2,1,0:T(8,128)(2,1)} %shard_map.95), calls=%async_computation.1 | async-start | bytes 4194304 | tf_op jit(solution)/shard_map/all_to_all | solution.py:181
  53.8 112.1 %all-gather.2.cloned.1.call-start = ((), (), s32[]{:S(2)}) async-start(), calls=%async_computation.4 | async-start | bytes 4718592 | tf_op jit(solution)/shard_map/all_gather | solution.py:192
  105.3 13.1 %copy-start.5 = (s32[1,128,2]{1,2,0:T(2,128)S(1)}, s32[1,128,2]{1,2,0:T(2,128)}, u32[]{:S(2)}) copy-start(s32[1,128,2]{1,2,0:T(2,128)} %param.11) | copy-start | bytes 3076
  105.3 60.6 %all-to-all-start.2 = ((bf16[64,2,64,128]{3,2,1,0:T(8,128)(2,1)}), bf16[64,2,64,128]{3,2,1,0:T(8,128)(2,1)S(1)}, u32[]{:S(2)}, u32[]{:S(2)}) async-start(bf16[64,2,64,128]{3,2,1,0:T(8,128)(2,1)} %broadcast_select_fusion), calls=%async_computation.2 | async-start | bytes 4194304 | tf_op jit(solution)/shard_map/all_to_all | solution.py:174
  165.9 2.2 copy-start
  174.2 56.1 %copy-start.2 = (f32[64,1024]{1,0:T(8,128)S(1)}, f32[64,1024]{1,0:T(8,128)}, u32[]{:S(2)}) copy-start(f32[64,1024]{1,0:T(8,128)} %get-tuple-element.5.refs_0_) | copy-start | bytes 786436
Sparse Core Ops, SparseCore 0:
  105.4 37.0 all-gather.1

commit v15 on v14

--- a/solution.py
+++ b/solution.py
@@ -130,6 +130,37 @@
     )(pattern_flat, scalars, tiles, local_blocks, ghost_blocks, *fields)
 
 
+def assemble_kernel(slot_ref, arrived_ref, out_ref, acc_ref):
+    acc_ref[...] = jnp.zeros_like(acc_ref)
+
+    def body(p, carry):
+        slot = slot_ref[p]
+
+        @pl.when(slot >= 0)
+        def _():
+            acc_ref[slot] += arrived_ref[p].astype(jnp.float32)
+
+        return carry
+
+    lax.fori_loop(0, arrived_ref.shape[0], body, 0, unroll=8)
+    out_ref[...] = acc_ref[...].astype(out_ref.dtype)
+
+
+def assemble_tiles(slots, arrived, slot_count):
+    peers, block_size = arrived.shape[0], arrived.shape[1]
+    return pl.pallas_call(
+        assemble_kernel,
+        out_shape=jax.ShapeDtypeStruct((slot_count, block_size, block_size), jnp.bfloat16),
+        in_specs=[pl.BlockSpec(memory_space=pltpu.SMEM), pl.BlockSpec(memory_space=pltpu.VMEM)],
+        out_specs=pl.BlockSpec(memory_space=pltpu.VMEM),
+        scratch_shapes=[pltpu.VMEM((slot_count, block_size, block_size), jnp.float32)],
+        compiler_params=pltpu.CompilerParams(vmem_limit_bytes=8 * 1024 * 1024),
+        cost_estimate=pl.CostEstimate(
+            flops=arrived.size, transcendentals=0, bytes_accessed=arrived.size * 2
+        ),
+    )(slots, arrived)
+
+
 def on_device(
     basis_values, potential, contrib_index, pattern, ghost_list, state, damp_lower, damp_upper
 ):
@@ -181,14 +212,7 @@
     arrived_tiles = lax.all_to_all(send_tiles, "rows", split_axis=0, concat_axis=0, tiled=True)
     arrived_tiles, state_outgoing = lax.optimization_barrier((arrived_tiles, state_outgoing))
     state_ghosts = exchange_ghosts(state_outgoing)
-    slot_wanted = jnp.arange(slot_count, dtype=jnp.int32)
-    selector = (arrived_slots[None, :] == slot_wanted[:, None]).astype(jnp.bfloat16)
-    assembled = jnp.dot(
-        selector,
-        arrived_tiles.reshape(n_rows, block_size * block_size),
-        preferred_element_type=jnp.float32,
-    )
-    assembled = assembled.astype(jnp.bfloat16).reshape(slot_count, block_size, block_size)
+    assembled = assemble_tiles(arrived_slots, arrived_tiles, slot_count)
     group_tiles = lax.all_gather(assembled, "cols", axis=0, tiled=True)
 
     pattern_flat = pattern.reshape(-1)

time: 244 us -> 244 us (level)
    unnamed x15 -> x16, local copies, waits for them, and re-layouts: 6.28 us -> 6.7 us
where the time goes in v15:
time: 244 us; the launch traced here: 242 us
  waiting for transfers between devices  90.5 us (37%)
  blocking collectives  56.3 us (23%)
  starting transfers between devices  40.3 us (17%)
  Pallas kernels  24.2 us (10%)
  between operations  15.5 us (6%)
  local copies, waits for them, and re-layouts  11.2 us (5%)
  other arithmetic  4.09 us (2%)
    all_to_all x1, blocking collectives, exchange_ghosts(): lax.all_to_all(outgoing, 'rows', split_axis=0, concat_axis=0, tiled=True)  56.3 us
    all_to_all x1, waiting for transfers between devices, exchange_ghosts(): lax.all_to_all(outgoing, 'rows', split_axis=0, concat_axis=0, tiled=True)  47 us
    all_to_all x1, waiting for transfers between devices, on_device(): lax.all_to_all(send_tiles, 'rows', split_axis=0, concat_axis=0, tiled=True)  43.5 us
    all_to_all x1, starting transfers between devices, on_device(): lax.all_to_all(index_send, 'rows', split_axis=0, concat_axis=0, tiled=True)  15.9 us
    all_to_all x1, starting transfers between devices, on_device(): lax.all_to_all(send_tiles, 'rows', split_axis=0, concat_axis=0, tiled=True)  12.8 us
    all_to_all x1, starting transfers between devices, exchange_ghosts(): lax.all_to_all(outgoing, 'rows', split_axis=0, concat_axis=0, tiled=True)  11.6 us
    pallas_call x1, Pallas kernels, presum_tiles(): pl.pallas_call(presum_kernel, out_shape=jax.ShapeDtypeStruct((n_rows, blo...  11 us
    pallas_call x2, Pallas kernels, apply_tiles(): pl.pallas_call(functools.partial(product_kernel, first), out_shape=out_sh...  10.8 us
  transfers between devices with their start and end apart: 4, of which 2 were waited for; matrix products, arithmetic and copies ran while one was open for 3% of the time, Pallas kernels for 5%

profile of v15, /device:TPU:56, one launch (start us, length us, event | category | flops | bytes accessed | tf_op | source)
XLA Modules:
  0.0 242.1 jit_solution(16364469152157299599)
XLA Ops:
  7.2 0.8 slice_bitcast_fusion.2
  7.9 0.7 compare_select_fusion.1
  8.7 0.7 copy.28
  9.5 15.9 %all-to-all-start = ((s32[64,1,3]{2,1,0:T(1,128)}), s32[64,1,3]{2,1,0:T(1,128)S(1)}, u32[]{:S(2)}, u32[]{:S(2)}) async-start(s32[64,1,3]{2,1,0:T(1,128)} %copy.28), calls=%async_computation | async-start | bytes 65536 | tf_op jit(solution)/shard_map/all_to_all | solution.py:183
  25.4 0.8 copy.30
  26.3 1.6 copy-done.4
  27.9 0.7 copy-done.5
  28.5 11.0 %shard_map.95 = bf16[64,128,128]{2,1,0:T(8,128)(2,1)S(1)} custom-call(s32[512]{0:T(512)S(1)} %reshape.39.index_ref, f32[1,512]{1,0:T(1,128)S(1)} %bitcast.28, bf16[16,512,128]{2,1,0:T(8,128)(2,1)S(1)} %copy-done.4), custom_call_target="tpu_custom_call" | custom-call | flops 4294967296 | bytes 6291456 | tf_op jit(solution)/shard_map/pallas_call | solution.py:35
  39.6 1.3 copy-done.2
  40.9 12.8 %all-to-all-start.1 = ((bf16[64,128,128]{2,1,0:T(8,128)(2,1)}), bf16[64,128,128]{2,1,0:T(8,128)(2,1)S(1)}, u32[]{:S(2)}, u32[]{:S(2)}) async-start(bf16[64,128,128]{2,1,0:T(8,128)(2,1)} %copy-done.2), calls=%async_computation.1 | async-start | bytes 4194304 | tf_op jit(solution)/shard_map/all_to_all | solution.py:212
  53.9 0.1 copy.31
  54.2 0.1 reshape.46
  54.3 2.1 gather_fusion
  56.5 3.2 %broadcast_select_fusion = bf16[64,2,64,128]{3,2,1,0:T(8,128)(2,1)} fusion(bf16[64,2,64,128]{3,2,1,0:T(8,128)(2,1)} %bitcast.29, pred[64,2]{1,0:T(8,128)(4,1)S(1)} %copy.31), kind=kLoop, calls=%fused_computation.1 | loop fusion | flops 1048576 | bytes 4194432 | tf_op jit(solution)/shard_map/jit(_where)/select_n | solution.py:198
  59.6 43.5 %all-to-all-done.1.arrived_ref = bf16[64,128,128]{2,1,0:T(8,128)(2,1)S(1)} async-done(((bf16[64,128,128]{2,1,0:T(8,128)(2,1)}), bf16[64,128,128]{2,1,0:T(8,128)(2,1)S(1)}, u32[]{:S(2)}, u32[]{:S(2)}) %all-to-all-start.1) | async-done | bytes 2097184 | tf_op jit(solution)/shard_map/all_to_all | solution.py:212
  103.2 2.3 shard_map.96
  105.5 11.6 %all-to-all-start.2 = ((bf16[64,2,64,128]{3,2,1,0:T(8,128)(2,1)}), bf16[64,2,64,128]{3,2,1,0:T(8,128)(2,1)S(1)}, u32[]{:S(2)}, u32[]{:S(2)}) async-start(bf16[64,2,64,128]{3,2,1,0:T(8,128)(2,1)} %broadcast_select_fusion), calls=%async_computation.2 | async-start | bytes 4194304 | tf_op jit(solution)/shard_map/all_to_all | solution.py:205
  118.5 0.1 reshape.38.pattern_ref
  118.8 0.1 reshape.42.refs_1_
  119.0 47.0 %all-to-all-done.2 = bf16[64,2,64,128]{3,2,1,0:T(8,128)(2,1)S(1)} async-done(((bf16[64,2,64,128]{3,2,1,0:T(8,128)(2,1)}), bf16[64,2,64,128]{3,2,1,0:T(8,128)(2,1)S(1)}, u32[]{:S(2)}, u32[]{:S(2)}) %all-to-all-start.2) | async-done | bytes 2097184 | tf_op jit(solution)/shard_map/all_to_all | solution.py:205
  166.0 2.2 copy-done
  168.2 6.1 %shard_map.97 = (f32[64,1024]{1,0:T(8,128)}, bf16[8,64,128]{2,1,0:T(8,128)(2,1)S(1)}, bf16[64,2,64,128]{3,2,1,0:T(8,128)(2,1)S(1)}) custom-call(s32[256]{0:T(256)S(1)} %reshape.38.pattern_ref, f32[2]{0:T(128)S(1)} %pad_maximum_fusion.scalar_ref, bf16[128,128,128]{2,1,0:T(8,128)(2,1)S(1)} %copy-done, bf16[8,64,128]{2,1,0:T(8,128)(2,1)S(1)} %bitcast_bitcast_fusion.local_ref, ...), custom_call_target="tpu_custom_call" | custom-call | flops 268435456 | bytes 7077888 | tf_op jit(solution)/shard_map/pallas_call | solution.py:118
  174.2 56.3 %all_to_all.27 = bf16[64,2,64,128]{3,2,1,0:T(8,128)(2,1)S(1)} all-to-all(bf16[64,2,64,128]{3,2,1,0:T(8,128)(2,1)S(1)} %get-tuple-element.11), channel_id=1, replica_groups=mesh['rows'=64,'cols'=8] {'rows'}, dimensions={0} | all-to-all | bytes 4194304 | tf_op jit(solution)/shard_map/all_to_all | solution.py:205
  230.6 4.7 %shard_map.98 = f32[64,1024]{1,0:T(8,128)} custom-call(s32[256]{0:T(256)S(1)} %reshape.38.pattern_ref, f32[2]{0:T(128)S(1)} %pad_maximum_fusion.scalar_ref, bf16[128,128,128]{2,1,0:T(8,128)(2,1)S(1)} %copy-done, bf16[8,64,128]{2,1,0:T(8,128)(2,1)S(1)} %get-tuple-element.10.local_ref, bf16[128,64,128]{2,1,0:T(8,128)(2,1)S(1)} %bitcast.27, ...), custom_call_target="tpu_custom_call" | custom-call | flops 268435456 | bytes 7077888 | tf_op jit(solution)/shard_map/pallas_call | solution.py:118
  (28 shorter events, 0.8 us)
Async XLA Ops:
  9.5 31.5 %all-to-all-start = ((s32[64,1,3]{2,1,0:T(1,128)}), s32[64,1,3]{2,1,0:T(1,128)S(1)}, u32[]{:S(2)}, u32[]{:S(2)}) async-start(s32[64,1,3]{2,1,0:T(1,128)} %copy.28), calls=%async_computation | async-start | bytes 65536 | tf_op jit(solution)/shard_map/all_to_all | solution.py:183
  26.3 1.6 copy-start.4
  27.9 0.7 copy-start.5
  39.6 1.3 copy-start.2
  40.9 12.9 %copy-start.1 = (f32[64,1024]{1,0:T(8,128)S(1)}, f32[64,1024]{1,0:T(8,128)}, u32[]{:S(2)}) copy-start(f32[64,1024]{1,0:T(8,128)} %refs_1_.1) | copy-start | bytes 786436
  40.9 62.2 %all-to-all-start.1 = ((bf16[64,128,128]{2,1,0:T(8,128)(2,1)}), bf16[64,128,128]{2,1,0:T(8,128)(2,1)S(1)}, u32[]{:S(2)}, u32[]{:S(2)}) async-start(bf16[64,128,128]{2,1,0:T(8,128)(2,1)} %copy-done.2), calls=%async_computation.1 | async-start | bytes 4194304 | tf_op jit(solution)/shard_map/all_to_all | solution.py:212
  53.8 112.2 %all-gather.2.cloned.1.call-start = ((), (), s32[]{:S(2)}) async-start(), calls=%async_computation.4 | async-start | bytes 4718592 | tf_op jit(solution)/shard_map/all_gather | solution.py:216
  105.5 12.9 %copy-start.6 = (s32[1,128,2]{1,2,0:T(2,128)S(1)}, s32[1,128,2]{1,2,0:T(2,128)}, u32[]{:S(2)}) copy-start(s32[1,128,2]{1,2,0:T(2,128)} %param.11) | copy-start | bytes 3076
  105.5 60.4 %all-to-all-start.2 = ((bf16[64,2,64,128]{3,2,1,0:T(8,128)(2,1)}), bf16[64,2,64,128]{3,2,1,0:T(8,128)(2,1)S(1)}, u32[]{:S(2)}, u32[]{:S(2)}) async-start(bf16[64,2,64,128]{3,2,1,0:T(8,128)(2,1)} %broadcast_select_fusion), calls=%async_computation.2 | async-start | bytes 4194304 | tf_op jit(solution)/shard_map/all_to_all | solution.py:205
  166.0 2.2 copy-start
  174.2 56.3 %copy-start.3 = (f32[64,1024]{1,0:T(8,128)S(1)}, f32[64,1024]{1,0:T(8,128)}, u32[]{:S(2)}) copy-start(f32[64,1024]{1,0:T(8,128)} %get-tuple-element.5.refs_0_) | copy-start | bytes 786436
Sparse Core Ops, SparseCore 0:
  105.7 37.1 all-gather.1

commit v16 on v14

--- a/solution.py
+++ b/solution.py
@@ -6,6 +6,9 @@
 from jax.experimental import pallas as pl
 from jax.experimental.pallas import tpu as pltpu
 from jax.sharding import PartitionSpec as P
+
+SLOTS_PER_SHARE = 16
+LOCAL_SLOTS = 4
 
 
 def presum_kernel(index_ref, potential_ref, basis_ref, out_ref, stacked_ref, tiles_ref, acc_ref):
@@ -60,16 +63,21 @@
     acc_ref = refs[-1]
     acc_ref[...] = jnp.zeros_like(acc_ref)
 
-    def body(g, carry):
-        row = pattern_ref[2 * g]
-        source = pattern_ref[2 * g + 1]
-        local = local_ref[jnp.minimum(source, row_blocks - 1)]
-        ghost = ghost_ref[jnp.maximum(source - row_blocks, 0)]
-        operand = jnp.where(source < row_blocks, local, ghost)
-        acc_ref[row] += jnp.dot(operand, tiles_ref[g], preferred_element_type=jnp.float32)
+    ghost_count = ghost_ref.shape[0]
+
+    def body(share, carry):
+        for j in range(SLOTS_PER_SHARE):
+            g = share * SLOTS_PER_SHARE + j
+            row = pattern_ref[2 * g]
+            source = pattern_ref[2 * g + 1]
+            if j < LOCAL_SLOTS:
+                operand = local_ref[jnp.clip(source, 0, row_blocks - 1)]
+            else:
+                operand = ghost_ref[jnp.clip(source - row_blocks, 0, ghost_count - 1)]
+            acc_ref[row] += jnp.dot(operand, tiles_ref[g], preferred_element_type=jnp.float32)
         return carry
 
-    lax.fori_loop(0, tiles_ref.shape[0], body, 0, unroll=8)
+    lax.fori_loop(0, tiles_ref.shape[0] // SLOTS_PER_SHARE, body, 0)
     center = scalar_ref[0]
     half_width = scalar_ref[1]
     if first:

time: 244 us -> 242 us (level)
  no operation moved by 1% of the time
where the time goes in v16:
time: 242 us; the launch traced here: 240 us
  waiting for transfers between devices  90.5 us (37%)
  blocking collectives  56.1 us (23%)
  starting transfers between devices  40.5 us (17%)
  Pallas kernels  20.9 us (9%)
  between operations  15.4 us (6%)
  local copies, waits for them, and re-layouts  10.8 us (4%)
  other arithmetic  4.08 us (2%)
    all_to_all x1, blocking collectives, exchange_ghosts(): lax.all_to_all(outgoing, 'rows', split_axis=0, concat_axis=0, tiled=True)  56.1 us
    all_to_all x1, waiting for transfers between devices, exchange_ghosts(): lax.all_to_all(outgoing, 'rows', split_axis=0, concat_axis=0, tiled=True)  46.9 us
    all_to_all x1, waiting for transfers between devices, on_device(): lax.all_to_all(send_tiles, 'rows', split_axis=0, concat_axis=0, tiled=True)  43.5 us
    all_to_all x1, starting transfers between devices, on_device(): lax.all_to_all(index_send, 'rows', split_axis=0, concat_axis=0, tiled=True)  15.9 us
    all_to_all x1, starting transfers between devices, on_device(): lax.all_to_all(send_tiles, 'rows', split_axis=0, concat_axis=0, tiled=True)  12.8 us
    pallas_call x1, Pallas kernels, presum_tiles(): pl.pallas_call(presum_kernel, out_shape=jax.ShapeDtypeStruct((n_rows, blo...  12.4 us
    all_to_all x1, starting transfers between devices, exchange_ghosts(): lax.all_to_all(outgoing, 'rows', split_axis=0, concat_axis=0, tiled=True)  11.8 us
    pallas_call x2, Pallas kernels, apply_tiles(): pl.pallas_call(functools.partial(product_kernel, first), out_shape=out_sh...  8.48 us
  transfers between devices with their start and end apart: 4, of which 2 were waited for; matrix products, arithmetic and copies ran while one was open for 3% of the time, Pallas kernels for 5%

profile of v16, /device:TPU:56, one launch (start us, length us, event | category | flops | bytes accessed | tf_op | source)
XLA Modules:
  0.0 239.5 jit_solution(16298556237515858059)
XLA Ops:
  7.2 0.8 slice_bitcast_fusion.2
  7.9 0.7 compare_select_fusion.1
  8.7 0.7 copy.28
  9.5 15.9 %all-to-all-start = ((s32[64,1,3]{2,1,0:T(1,128)}), s32[64,1,3]{2,1,0:T(1,128)S(1)}, u32[]{:S(2)}, u32[]{:S(2)}) async-start(s32[64,1,3]{2,1,0:T(1,128)} %copy.28), calls=%async_computation | async-start | bytes 65536 | tf_op jit(solution)/shard_map/all_to_all | solution.py:160
  25.4 0.8 copy.30
  26.3 1.6 copy-done.3
  27.9 0.7 copy-done.4
  28.5 12.4 %shard_map.95 = bf16[64,128,128]{2,1,0:T(8,128)(2,1)} custom-call(s32[512]{0:T(512)S(1)} %reshape.46.index_ref, f32[1,512]{1,0:T(1,128)S(1)} %bitcast.37, bf16[16,512,128]{2,1,0:T(8,128)(2,1)S(1)} %copy-done.3), custom_call_target="tpu_custom_call" | custom-call | flops 4294967296 | bytes 6291456 | tf_op jit(solution)/shard_map/pallas_call | solution.py:38
  40.9 12.8 %all-to-all-start.1 = ((bf16[64,128,128]{2,1,0:T(8,128)(2,1)}), bf16[64,128,128]{2,1,0:T(8,128)(2,1)S(1)}, u32[]{:S(2)}, u32[]{:S(2)}) async-start(bf16[64,128,128]{2,1,0:T(8,128)(2,1)} %shard_map.95), calls=%async_computation.1 | async-start | bytes 4194304 | tf_op jit(solution)/shard_map/all_to_all | solution.py:189
  53.9 0.1 copy.31
  54.2 0.1 reshape.55
  54.3 2.1 gather_fusion
  56.5 3.2 %broadcast_select_fusion = bf16[64,2,64,128]{3,2,1,0:T(8,128)(2,1)} fusion(bf16[64,2,64,128]{3,2,1,0:T(8,128)(2,1)} %bitcast.39, pred[64,2]{1,0:T(8,128)(4,1)S(1)} %copy.31), kind=kLoop, calls=%fused_computation.4 | loop fusion | flops 1048576 | bytes 4194432 | tf_op jit(solution)/shard_map/jit(_where)/select_n | solution.py:175
  59.6 43.5 %all-to-all-done.1 = bf16[64,128,128]{2,1,0:T(8,128)(2,1)S(1)} async-done(((bf16[64,128,128]{2,1,0:T(8,128)(2,1)}), bf16[64,128,128]{2,1,0:T(8,128)(2,1)S(1)}, u32[]{:S(2)}, u32[]{:S(2)}) %all-to-all-start.1) | async-done | bytes 2097184 | tf_op jit(solution)/shard_map/all_to_all | solution.py:189
  103.2 1.2 fusion.2
  104.4 0.9 copy.37
  105.3 11.8 %all-to-all-start.2 = ((bf16[64,2,64,128]{3,2,1,0:T(8,128)(2,1)}), bf16[64,2,64,128]{3,2,1,0:T(8,128)(2,1)S(1)}, u32[]{:S(2)}, u32[]{:S(2)}) async-start(bf16[64,2,64,128]{3,2,1,0:T(8,128)(2,1)} %broadcast_select_fusion), calls=%async_computation.2 | async-start | bytes 4194304 | tf_op jit(solution)/shard_map/all_to_all | solution.py:182
  118.5 0.1 reshape.45.pattern_ref
  118.8 0.1 reshape.51.refs_1_
  119.0 46.9 %all-to-all-done.2 = bf16[64,2,64,128]{3,2,1,0:T(8,128)(2,1)S(1)} async-done(((bf16[64,2,64,128]{3,2,1,0:T(8,128)(2,1)}), bf16[64,2,64,128]{3,2,1,0:T(8,128)(2,1)S(1)}, u32[]{:S(2)}, u32[]{:S(2)}) %all-to-all-start.2) | async-done | bytes 2097184 | tf_op jit(solution)/shard_map/all_to_all | solution.py:182
  165.9 2.2 copy-done
  168.1 4.9 %shard_map.96 = (f32[64,1024]{1,0:T(8,128)}, bf16[8,64,128]{2,1,0:T(8,128)(2,1)S(1)}, bf16[64,2,64,128]{3,2,1,0:T(8,128)(2,1)S(1)}) custom-call(s32[256]{0:T(256)S(1)} %reshape.45.pattern_ref, f32[2]{0:T(128)S(1)} %pad_maximum_fusion.scalar_ref, bf16[128,128,128]{2,1,0:T(8,128)(2,1)S(1)} %copy-done, bf16[8,64,128]{2,1,0:T(8,128)(2,1)S(1)} %bitcast_bitcast_fusion.local_ref, ...), custom_call_target="tpu_custom_call" | custom-call | flops 268435456 | bytes 7077888 | tf_op jit(solution)/shard_map/pallas_call | solution.py:126
  173.0 56.1 %all_to_all.27 = bf16[64,2,64,128]{3,2,1,0:T(8,128)(2,1)S(1)} all-to-all(bf16[64,2,64,128]{3,2,1,0:T(8,128)(2,1)S(1)} %get-tuple-element.11), channel_id=1, replica_groups=mesh['rows'=64,'cols'=8] {'rows'}, dimensions={0} | all-to-all | bytes 4194304 | tf_op jit(solution)/shard_map/all_to_all | solution.py:182
  229.1 3.5 %shard_map.97 = f32[64,1024]{1,0:T(8,128)} custom-call(s32[256]{0:T(256)S(1)} %reshape.45.pattern_ref, f32[2]{0:T(128)S(1)} %pad_maximum_fusion.scalar_ref, bf16[128,128,128]{2,1,0:T(8,128)(2,1)S(1)} %copy-done, bf16[8,64,128]{2,1,0:T(8,128)(2,1)S(1)} %get-tuple-element.10.local_ref, bf16[128,64,128]{2,1,0:T(8,128)(2,1)S(1)} %bitcast.36, ...), custom_call_target="tpu_custom_call" | custom-call | flops 268435456 | bytes 7077888 | tf_op jit(solution)/shard_map/pallas_call | solution.py:126
  (27 shorter events, 0.8 us)
Async XLA Ops:
  9.5 31.5 %all-to-all-start = ((s32[64,1,3]{2,1,0:T(1,128)}), s32[64,1,3]{2,1,0:T(1,128)S(1)}, u32[]{:S(2)}, u32[]{:S(2)}) async-start(s32[64,1,3]{2,1,0:T(1,128)} %copy.28), calls=%async_computation | async-start | bytes 65536 | tf_op jit(solution)/shard_map/all_to_all | solution.py:160
  26.3 1.6 copy-start.3
  27.9 0.7 copy-start.4
  40.9 12.9 %copy-start.1 = (f32[64,1024]{1,0:T(8,128)S(1)}, f32[64,1024]{1,0:T(8,128)}, u32[]{:S(2)}) copy-start(f32[64,1024]{1,0:T(8,128)} %refs_1_.1) | copy-start | bytes 786436
  40.9 62.2 %all-to-all-start.1 = ((bf16[64,128,128]{2,1,0:T(8,128)(2,1)}), bf16[64,128,128]{2,1,0:T(8,128)(2,1)S(1)}, u32[]{:S(2)}, u32[]{:S(2)}) async-start(bf16[64,128,128]{2,1,0:T(8,128)(2,1)} %shard_map.95), calls=%async_computation.1 | async-start | bytes 4194304 | tf_op jit(solution)/shard_map/all_to_all | solution.py:189
  53.8 112.1 %all-gather.2.cloned.1.call-start = ((), (), s32[]{:S(2)}) async-start(), calls=%async_computation.4 | async-start | bytes 4718592 | tf_op jit(solution)/shard_map/all_gather | solution.py:200
  105.3 13.1 %copy-start.5 = (s32[1,128,2]{1,2,0:T(2,128)S(1)}, s32[1,128,2]{1,2,0:T(2,128)}, u32[]{:S(2)}) copy-start(s32[1,128,2]{1,2,0:T(2,128)} %param.11) | copy-start | bytes 3076
  105.3 60.6 %all-to-all-start.2 = ((bf16[64,2,64,128]{3,2,1,0:T(8,128)(2,1)}), bf16[64,2,64,128]{3,2,1,0:T(8,128)(2,1)S(1)}, u32[]{:S(2)}, u32[]{:S(2)}) async-start(bf16[64,2,64,128]{3,2,1,0:T(8,128)(2,1)} %broadcast_select_fusion), calls=%async_computation.2 | async-start | bytes 4194304 | tf_op jit(solution)/shard_map/all_to_all | solution.py:182
  165.9 2.2 copy-start
  173.0 56.1 %copy-start.2 = (f32[64,1024]{1,0:T(8,128)S(1)}, f32[64,1024]{1,0:T(8,128)}, u32[]{:S(2)}) copy-start(f32[64,1024]{1,0:T(8,128)} %get-tuple-element.5.refs_0_) | copy-start | bytes 786436
Sparse Core Ops, SparseCore 0:
  105.4 37.0 all-gather.1

commit v17 on v16

--- a/solution.py
+++ b/solution.py
@@ -90,9 +90,7 @@
         width = outgoing_ref.shape[1]
 
         def send(e, carry):
-            wanted = wanted_ref[e]
-            block = blocks_ref[jnp.clip(wanted, 0, row_blocks - 1)]
-            outgoing_ref[e // width, e % width] = jnp.where(wanted >= 0, block, jnp.zeros_like(block))
+            outgoing_ref[e // width, e % width] = blocks_ref[jnp.clip(wanted_ref[e], 0, row_blocks - 1)]
             return carry
 
         lax.fori_loop(0, wanted_ref.shape[0], send, 0, unroll=8)

time: 242 us -> 242 us (level)
  no operation moved by 1% of the time
where the time goes in v17:
time: 242 us; the launch traced here: 239 us
  waiting for transfers between devices  90.5 us (37%)
  blocking collectives  56.1 us (23%)
  starting transfers between devices  40.5 us (17%)
  Pallas kernels  20.6 us (9%)
  between operations  15.4 us (6%)
  local copies, waits for them, and re-layouts  10.8 us (4%)
  other arithmetic  4.08 us (2%)
    all_to_all x1, blocking collectives, exchange_ghosts(): lax.all_to_all(outgoing, 'rows', split_axis=0, concat_axis=0, tiled=True)  56.1 us
    all_to_all x1, waiting for transfers between devices, exchange_ghosts(): lax.all_to_all(outgoing, 'rows', split_axis=0, concat_axis=0, tiled=True)  46.9 us
    all_to_all x1, waiting for transfers between devices, on_device(): lax.all_to_all(send_tiles, 'rows', split_axis=0, concat_axis=0, tiled=True)  43.5 us
    all_to_all x1, starting transfers between devices, on_device(): lax.all_to_all(index_send, 'rows', split_axis=0, concat_axis=0, tiled=True)  15.9 us
    all_to_all x1, starting transfers between devices, on_device(): lax.all_to_all(send_tiles, 'rows', split_axis=0, concat_axis=0, tiled=True)  12.8 us
    pallas_call x1, Pallas kernels, presum_tiles(): pl.pallas_call(presum_kernel, out_shape=jax.ShapeDtypeStruct((n_rows, blo...  12.4 us
    all_to_all x1, starting transfers between devices, exchange_ghosts(): lax.all_to_all(outgoing, 'rows', split_axis=0, concat_axis=0, tiled=True)  11.8 us
    pallas_call x2, Pallas kernels, apply_tiles(): pl.pallas_call(functools.partial(product_kernel, first), out_shape=out_sh...  8.21 us
  transfers between devices with their start and end apart: 4, of which 2 were waited for; matrix products, arithmetic and copies ran while one was open for 3% of the time, Pallas kernels for 5%

profile of v17, /device:TPU:56, one launch (start us, length us, event | category | flops | bytes accessed | tf_op | source)
XLA Modules:
  0.0 239.3 jit_solution(4004813589285598855)
XLA Ops:
  7.2 0.8 slice_bitcast_fusion.2
  7.9 0.7 compare_select_fusion.1
  8.7 0.7 copy.28
  9.5 15.9 %all-to-all-start = ((s32[64,1,3]{2,1,0:T(1,128)}), s32[64,1,3]{2,1,0:T(1,128)S(1)}, u32[]{:S(2)}, u32[]{:S(2)}) async-start(s32[64,1,3]{2,1,0:T(1,128)} %copy.28), calls=%async_computation | async-start | bytes 65536 | tf_op jit(solution)/shard_map/all_to_all | solution.py:158
  25.4 0.8 copy.30
  26.3 1.6 copy-done.3
  27.9 0.7 copy-done.4
  28.5 12.4 %shard_map.95 = bf16[64,128,128]{2,1,0:T(8,128)(2,1)} custom-call(s32[512]{0:T(512)S(1)} %reshape.46.index_ref, f32[1,512]{1,0:T(1,128)S(1)} %bitcast.37, bf16[16,512,128]{2,1,0:T(8,128)(2,1)S(1)} %copy-done.3), custom_call_target="tpu_custom_call" | custom-call | flops 4294967296 | bytes 6291456 | tf_op jit(solution)/shard_map/pallas_call | solution.py:38
  40.9 12.8 %all-to-all-start.1 = ((bf16[64,128,128]{2,1,0:T(8,128)(2,1)}), bf16[64,128,128]{2,1,0:T(8,128)(2,1)S(1)}, u32[]{:S(2)}, u32[]{:S(2)}) async-start(bf16[64,128,128]{2,1,0:T(8,128)(2,1)} %shard_map.95), calls=%async_computation.1 | async-start | bytes 4194304 | tf_op jit(solution)/shard_map/all_to_all | solution.py:187
  53.9 0.1 copy.31
  54.2 0.1 reshape.55
  54.3 2.1 gather_fusion
  56.5 3.2 %broadcast_select_fusion = bf16[64,2,64,128]{3,2,1,0:T(8,128)(2,1)} fusion(bf16[64,2,64,128]{3,2,1,0:T(8,128)(2,1)} %bitcast.39, pred[64,2]{1,0:T(8,128)(4,1)S(1)} %copy.31), kind=kLoop, calls=%fused_computation.4 | loop fusion | flops 1048576 | bytes 4194432 | tf_op jit(solution)/shard_map/jit(_where)/select_n | solution.py:173
  59.6 43.5 %all-to-all-done.1 = bf16[64,128,128]{2,1,0:T(8,128)(2,1)S(1)} async-done(((bf16[64,128,128]{2,1,0:T(8,128)(2,1)}), bf16[64,128,128]{2,1,0:T(8,128)(2,1)S(1)}, u32[]{:S(2)}, u32[]{:S(2)}) %all-to-all-start.1) | async-done | bytes 2097184 | tf_op jit(solution)/shard_map/all_to_all | solution.py:187
  103.2 1.2 fusion.2
  104.4 0.9 copy.37
  105.3 11.8 %all-to-all-start.2 = ((bf16[64,2,64,128]{3,2,1,0:T(8,128)(2,1)}), bf16[64,2,64,128]{3,2,1,0:T(8,128)(2,1)S(1)}, u32[]{:S(2)}, u32[]{:S(2)}) async-start(bf16[64,2,64,128]{3,2,1,0:T(8,128)(2,1)} %broadcast_select_fusion), calls=%async_computation.2 | async-start | bytes 4194304 | tf_op jit(solution)/shard_map/all_to_all | solution.py:180
  118.5 0.1 reshape.45.pattern_ref
  118.8 0.1 reshape.51.refs_1_
  119.0 46.9 %all-to-all-done.2 = bf16[64,2,64,128]{3,2,1,0:T(8,128)(2,1)S(1)} async-done(((bf16[64,2,64,128]{3,2,1,0:T(8,128)(2,1)}), bf16[64,2,64,128]{3,2,1,0:T(8,128)(2,1)S(1)}, u32[]{:S(2)}, u32[]{:S(2)}) %all-to-all-start.2) | async-done | bytes 2097184 | tf_op jit(solution)/shard_map/all_to_all | solution.py:180
  165.9 2.2 copy-done
  168.1 4.7 %shard_map.96 = (f32[64,1024]{1,0:T(8,128)}, bf16[8,64,128]{2,1,0:T(8,128)(2,1)S(1)}, bf16[64,2,64,128]{3,2,1,0:T(8,128)(2,1)S(1)}) custom-call(s32[256]{0:T(256)S(1)} %reshape.45.pattern_ref, f32[2]{0:T(128)S(1)} %pad_maximum_fusion.scalar_ref, bf16[128,128,128]{2,1,0:T(8,128)(2,1)S(1)} %copy-done, bf16[8,64,128]{2,1,0:T(8,128)(2,1)S(1)} %bitcast_bitcast_fusion.local_ref, ...), custom_call_target="tpu_custom_call" | custom-call | flops 268435456 | bytes 7077888 | tf_op jit(solution)/shard_map/pallas_call | solution.py:124
  172.8 56.1 %all_to_all.27 = bf16[64,2,64,128]{3,2,1,0:T(8,128)(2,1)S(1)} all-to-all(bf16[64,2,64,128]{3,2,1,0:T(8,128)(2,1)S(1)} %get-tuple-element.11), channel_id=1, replica_groups=mesh['rows'=64,'cols'=8] {'rows'}, dimensions={0} | all-to-all | bytes 4194304 | tf_op jit(solution)/shard_map/all_to_all | solution.py:180
  228.9 3.5 %shard_map.97 = f32[64,1024]{1,0:T(8,128)} custom-call(s32[256]{0:T(256)S(1)} %reshape.45.pattern_ref, f32[2]{0:T(128)S(1)} %pad_maximum_fusion.scalar_ref, bf16[128,128,128]{2,1,0:T(8,128)(2,1)S(1)} %copy-done, bf16[8,64,128]{2,1,0:T(8,128)(2,1)S(1)} %get-tuple-element.10.local_ref, bf16[128,64,128]{2,1,0:T(8,128)(2,1)S(1)} %bitcast.36, ...), custom_call_target="tpu_custom_call" | custom-call | flops 268435456 | bytes 7077888 | tf_op jit(solution)/shard_map/pallas_call | solution.py:124
  (27 shorter events, 0.8 us)
Async XLA Ops:
  9.5 31.5 %all-to-all-start = ((s32[64,1,3]{2,1,0:T(1,128)}), s32[64,1,3]{2,1,0:T(1,128)S(1)}, u32[]{:S(2)}, u32[]{:S(2)}) async-start(s32[64,1,3]{2,1,0:T(1,128)} %copy.28), calls=%async_computation | async-start | bytes 65536 | tf_op jit(solution)/shard_map/all_to_all | solution.py:158
  26.3 1.6 copy-start.3
  27.9 0.7 copy-start.4
  40.9 12.9 %copy-start.1 = (f32[64,1024]{1,0:T(8,128)S(1)}, f32[64,1024]{1,0:T(8,128)}, u32[]{:S(2)}) copy-start(f32[64,1024]{1,0:T(8,128)} %refs_1_.1) | copy-start | bytes 786436
  40.9 62.2 %all-to-all-start.1 = ((bf16[64,128,128]{2,1,0:T(8,128)(2,1)}), bf16[64,128,128]{2,1,0:T(8,128)(2,1)S(1)}, u32[]{:S(2)}, u32[]{:S(2)}) async-start(bf16[64,128,128]{2,1,0:T(8,128)(2,1)} %shard_map.95), calls=%async_computation.1 | async-start | bytes 4194304 | tf_op jit(solution)/shard_map/all_to_all | solution.py:187
  53.8 112.1 %all-gather.2.cloned.1.call-start = ((), (), s32[]{:S(2)}) async-start(), calls=%async_computation.4 | async-start | bytes 4718592 | tf_op jit(solution)/shard_map/all_gather | solution.py:198
  105.3 13.1 %copy-start.5 = (s32[1,128,2]{1,2,0:T(2,128)S(1)}, s32[1,128,2]{1,2,0:T(2,128)}, u32[]{:S(2)}) copy-start(s32[1,128,2]{1,2,0:T(2,128)} %param.11) | copy-start | bytes 3076
  105.3 60.6 %all-to-all-start.2 = ((bf16[64,2,64,128]{3,2,1,0:T(8,128)(2,1)}), bf16[64,2,64,128]{3,2,1,0:T(8,128)(2,1)S(1)}, u32[]{:S(2)}, u32[]{:S(2)}) async-start(bf16[64,2,64,128]{3,2,1,0:T(8,128)(2,1)} %broadcast_select_fusion), calls=%async_computation.2 | async-start | bytes 4194304 | tf_op jit(solution)/shard_map/all_to_all | solution.py:180
  165.9 2.2 copy-start
  172.8 56.1 %copy-start.2 = (f32[64,1024]{1,0:T(8,128)S(1)}, f32[64,1024]{1,0:T(8,128)}, u32[]{:S(2)}) copy-start(f32[64,1024]{1,0:T(8,128)} %get-tuple-element.5.refs_0_) | copy-start | bytes 786436
Sparse Core Ops, SparseCore 0:
  105.4 37.0 all-gather.1

commit v18 on v16

--- a/solution.py
+++ b/solution.py
@@ -29,7 +29,7 @@
         acc_ref[target] += tiles_ref[index_ref[4 * s + 2], index_ref[4 * s + 3]].astype(jnp.float32)
         return carry
 
-    lax.fori_loop(0, index_ref.shape[0] // 4, body, 0, unroll=8)
+    lax.fori_loop(0, index_ref.shape[0] // 4, body, 0, unroll=16)
     out_ref[...] = acc_ref[...].astype(out_ref.dtype)
 
 

time: 242 us -> 242 us (level)
  no operation moved by 1% of the time
where the time goes in v18:
time: 242 us; the launch traced here: 240 us
  waiting for transfers between devices  90.5 us (37%)
  blocking collectives  56.1 us (23%)
  starting transfers between devices  40.5 us (17%)
  Pallas kernels  20.9 us (9%)
  between operations  15.4 us (6%)
  local copies, waits for them, and re-layouts  10.8 us (4%)
  other arithmetic  4.08 us (2%)
    all_to_all x1, blocking collectives, exchange_ghosts(): lax.all_to_all(outgoing, 'rows', split_axis=0, concat_axis=0, tiled=True)  56.1 us
    all_to_all x1, waiting for transfers between devices, exchange_ghosts(): lax.all_to_all(outgoing, 'rows', split_axis=0, concat_axis=0, tiled=True)  46.9 us
    all_to_all x1, waiting for transfers between devices, on_device(): lax.all_to_all(send_tiles, 'rows', split_axis=0, concat_axis=0, tiled=True)  43.5 us
    all_to_all x1, starting transfers between devices, on_device(): lax.all_to_all(index_send, 'rows', split_axis=0, concat_axis=0, tiled=True)  15.9 us
    all_to_all x1, starting transfers between devices, on_device(): lax.all_to_all(send_tiles, 'rows', split_axis=0, concat_axis=0, tiled=True)  12.8 us
    pallas_call x1, Pallas kernels, presum_tiles(): pl.pallas_call(presum_kernel, out_shape=jax.ShapeDtypeStruct((n_rows, blo...  12.4 us
    all_to_all x1, starting transfers between devices, exchange_ghosts(): lax.all_to_all(outgoing, 'rows', split_axis=0, concat_axis=0, tiled=True)  11.8 us
    pallas_call x2, Pallas kernels, apply_tiles(): pl.pallas_call(functools.partial(product_kernel, first), out_shape=out_sh...  8.48 us
  transfers between devices with their start and end apart: 4, of which 2 were waited for; matrix products, arithmetic and copies ran while one was open for 3% of the time, Pallas kernels for 5%

profile of v18, /device:TPU:56, one launch (start us, length us, event | category | flops | bytes accessed | tf_op | source)
XLA Modules:
  0.0 239.6 jit_solution(2585806471677461487)
XLA Ops:
  7.2 0.8 slice_bitcast_fusion.2
  7.9 0.7 compare_select_fusion.1
  8.7 0.7 copy.28
  9.5 15.9 %all-to-all-start = ((s32[64,1,3]{2,1,0:T(1,128)}), s32[64,1,3]{2,1,0:T(1,128)S(1)}, u32[]{:S(2)}, u32[]{:S(2)}) async-start(s32[64,1,3]{2,1,0:T(1,128)} %copy.28), calls=%async_computation | async-start | bytes 65536 | tf_op jit(solution)/shard_map/all_to_all | solution.py:160
  25.4 0.8 copy.30
  26.3 1.6 copy-done.3
  27.9 0.7 copy-done.4
  28.5 12.4 %shard_map.95 = bf16[64,128,128]{2,1,0:T(8,128)(2,1)} custom-call(s32[512]{0:T(512)S(1)} %reshape.46.index_ref, f32[1,512]{1,0:T(1,128)S(1)} %bitcast.37, bf16[16,512,128]{2,1,0:T(8,128)(2,1)S(1)} %copy-done.3), custom_call_target="tpu_custom_call" | custom-call | flops 4294967296 | bytes 6291456 | tf_op jit(solution)/shard_map/pallas_call | solution.py:38
  41.0 12.8 %all-to-all-start.1 = ((bf16[64,128,128]{2,1,0:T(8,128)(2,1)}), bf16[64,128,128]{2,1,0:T(8,128)(2,1)S(1)}, u32[]{:S(2)}, u32[]{:S(2)}) async-start(bf16[64,128,128]{2,1,0:T(8,128)(2,1)} %shard_map.95), calls=%async_computation.1 | async-start | bytes 4194304 | tf_op jit(solution)/shard_map/all_to_all | solution.py:189
  54.0 0.1 copy.31
  54.2 0.1 reshape.55
  54.4 2.1 gather_fusion
  56.5 3.2 %broadcast_select_fusion = bf16[64,2,64,128]{3,2,1,0:T(8,128)(2,1)} fusion(bf16[64,2,64,128]{3,2,1,0:T(8,128)(2,1)} %bitcast.39, pred[64,2]{1,0:T(8,128)(4,1)S(1)} %copy.31), kind=kLoop, calls=%fused_computation.4 | loop fusion | flops 1048576 | bytes 4194432 | tf_op jit(solution)/shard_map/jit(_where)/select_n | solution.py:175
  59.7 43.5 %all-to-all-done.1 = bf16[64,128,128]{2,1,0:T(8,128)(2,1)S(1)} async-done(((bf16[64,128,128]{2,1,0:T(8,128)(2,1)}), bf16[64,128,128]{2,1,0:T(8,128)(2,1)S(1)}, u32[]{:S(2)}, u32[]{:S(2)}) %all-to-all-start.1) | async-done | bytes 2097184 | tf_op jit(solution)/shard_map/all_to_all | solution.py:189
  103.2 1.2 fusion.2
  104.4 0.9 copy.37
  105.4 11.8 %all-to-all-start.2 = ((bf16[64,2,64,128]{3,2,1,0:T(8,128)(2,1)}), bf16[64,2,64,128]{3,2,1,0:T(8,128)(2,1)S(1)}, u32[]{:S(2)}, u32[]{:S(2)}) async-start(bf16[64,2,64,128]{3,2,1,0:T(8,128)(2,1)} %broadcast_select_fusion), calls=%async_computation.2 | async-start | bytes 4194304 | tf_op jit(solution)/shard_map/all_to_all | solution.py:182
  118.5 0.1 reshape.45.pattern_ref
  118.9 0.1 reshape.51.refs_1_
  119.0 46.9 %all-to-all-done.2 = bf16[64,2,64,128]{3,2,1,0:T(8,128)(2,1)S(1)} async-done(((bf16[64,2,64,128]{3,2,1,0:T(8,128)(2,1)}), bf16[64,2,64,128]{3,2,1,0:T(8,128)(2,1)S(1)}, u32[]{:S(2)}, u32[]{:S(2)}) %all-to-all-start.2) | async-done | bytes 2097184 | tf_op jit(solution)/shard_map/all_to_all | solution.py:182
  165.9 2.2 copy-done
  168.1 5.0 %shard_map.96 = (f32[64,1024]{1,0:T(8,128)}, bf16[8,64,128]{2,1,0:T(8,128)(2,1)S(1)}, bf16[64,2,64,128]{3,2,1,0:T(8,128)(2,1)S(1)}) custom-call(s32[256]{0:T(256)S(1)} %reshape.45.pattern_ref, f32[2]{0:T(128)S(1)} %pad_maximum_fusion.scalar_ref, bf16[128,128,128]{2,1,0:T(8,128)(2,1)S(1)} %copy-done, bf16[8,64,128]{2,1,0:T(8,128)(2,1)S(1)} %bitcast_bitcast_fusion.local_ref, ...), custom_call_target="tpu_custom_call" | custom-call | flops 268435456 | bytes 7077888 | tf_op jit(solution)/shard_map/pallas_call | solution.py:126
  173.1 56.1 %all_to_all.27 = bf16[64,2,64,128]{3,2,1,0:T(8,128)(2,1)S(1)} all-to-all(bf16[64,2,64,128]{3,2,1,0:T(8,128)(2,1)S(1)} %get-tuple-element.11), channel_id=1, replica_groups=mesh['rows'=64,'cols'=8] {'rows'}, dimensions={0} | all-to-all | bytes 4194304 | tf_op jit(solution)/shard_map/all_to_all | solution.py:182
  229.2 3.5 %shard_map.97 = f32[64,1024]{1,0:T(8,128)} custom-call(s32[256]{0:T(256)S(1)} %reshape.45.pattern_ref, f32[2]{0:T(128)S(1)} %pad_maximum_fusion.scalar_ref, bf16[128,128,128]{2,1,0:T(8,128)(2,1)S(1)} %copy-done, bf16[8,64,128]{2,1,0:T(8,128)(2,1)S(1)} %get-tuple-element.10.local_ref, bf16[128,64,128]{2,1,0:T(8,128)(2,1)S(1)} %bitcast.36, ...), custom_call_target="tpu_custom_call" | custom-call | flops 268435456 | bytes 7077888 | tf_op jit(solution)/shard_map/pallas_call | solution.py:126
  (27 shorter events, 0.8 us)
Async XLA Ops:
  9.5 31.5 %all-to-all-start = ((s32[64,1,3]{2,1,0:T(1,128)}), s32[64,1,3]{2,1,0:T(1,128)S(1)}, u32[]{:S(2)}, u32[]{:S(2)}) async-start(s32[64,1,3]{2,1,0:T(1,128)} %copy.28), calls=%async_computation | async-start | bytes 65536 | tf_op jit(solution)/shard_map/all_to_all | solution.py:160
  26.3 1.6 copy-start.3
  27.9 0.7 copy-start.4
  41.0 12.9 %copy-start.1 = (f32[64,1024]{1,0:T(8,128)S(1)}, f32[64,1024]{1,0:T(8,128)}, u32[]{:S(2)}) copy-start(f32[64,1024]{1,0:T(8,128)} %refs_1_.1) | copy-start | bytes 786436
  41.0 62.2 %all-to-all-start.1 = ((bf16[64,128,128]{2,1,0:T(8,128)(2,1)}), bf16[64,128,128]{2,1,0:T(8,128)(2,1)S(1)}, u32[]{:S(2)}, u32[]{:S(2)}) async-start(bf16[64,128,128]{2,1,0:T(8,128)(2,1)} %shard_map.95), calls=%async_computation.1 | async-start | bytes 4194304 | tf_op jit(solution)/shard_map/all_to_all | solution.py:189
  53.8 112.1 %all-gather.2.cloned.1.call-start = ((), (), s32[]{:S(2)}) async-start(), calls=%async_computation.4 | async-start | bytes 4718592 | tf_op jit(solution)/shard_map/all_gather | solution.py:200
  105.4 13.1 %copy-start.5 = (s32[1,128,2]{1,2,0:T(2,128)S(1)}, s32[1,128,2]{1,2,0:T(2,128)}, u32[]{:S(2)}) copy-start(s32[1,128,2]{1,2,0:T(2,128)} %param.11) | copy-start | bytes 3076
  105.4 60.6 %all-to-all-start.2 = ((bf16[64,2,64,128]{3,2,1,0:T(8,128)(2,1)}), bf16[64,2,64,128]{3,2,1,0:T(8,128)(2,1)S(1)}, u32[]{:S(2)}, u32[]{:S(2)}) async-start(bf16[64,2,64,128]{3,2,1,0:T(8,128)(2,1)} %broadcast_select_fusion), calls=%async_computation.2 | async-start | bytes 4194304 | tf_op jit(solution)/shard_map/all_to_all | solution.py:182
  165.9 2.2 copy-start
  173.1 56.1 %copy-start.2 = (f32[64,1024]{1,0:T(8,128)S(1)}, f32[64,1024]{1,0:T(8,128)}, u32[]{:S(2)}) copy-start(f32[64,1024]{1,0:T(8,128)} %get-tuple-element.5.refs_0_) | copy-start | bytes 786436
Sparse Core Ops, SparseCore 0:
  105.5 37.0 all-gather.1
